TPU v7x, 32 devices: a whole 2x2x4 slice. The times are simulated.
32 devices in a mesh: rep: 8 (over y, x, core), shard: 4 (over z).
Axes of the slice: x: 2, y: 2, z: 4, core: 2. Of those that a mesh axis runs over, the one named last changes fastest.
Arguments:
- inputs: bfloat16 [2, 1024, 4, 1024], P(None, 'rep', 'shard'), may hold values from -6 to 6
- early_gain: bfloat16 [1024], P('shard'), may hold values from 0.5 to 1.5
- early_shift: bfloat16 [1024], P('shard'), may hold values from -2 to 2
- early_widen: bfloat16 [1024, 4096], P('shard'), may hold values from -0.1875 to 0.1875
- early_offset: bfloat16 [4096], P('shard'), may hold values from -2 to 2
- early_narrow: bfloat16 [4096, 1024], P('shard'), may hold values from -0.1875 to 0.1875
- early_bias: bfloat16 [1024], P('shard'), may hold values from -2 to 2
- attend_gain: bfloat16 [1024], P('shard'), may hold values from 0.5 to 1.5
- attend_shift: bfloat16 [1024], P('shard'), may hold values from -2 to 2
- query_weight: bfloat16 [1024, 1024], P('shard'), may hold values from -0.25 to 0.25
- query_bias: bfloat16 [1024], P('shard'), may hold values from -2 to 2
- key_weight: bfloat16 [1024, 1024], P('shard'), may hold values from -0.25 to 0.25
- value_weight: bfloat16 [1024, 1024], P('shard'), may hold values from -0.1875 to 0.1875
- value_bias: bfloat16 [1024], P('shard'), may hold values from -2 to 2
- mixer_weight: bfloat16 [1024, 1024], P('shard'), may hold values from -0.75 to 0.75
- mixer_bias: bfloat16 [1024], P('shard'), may hold values from -2 to 2
- distance_table: bfloat16 [73, 64], P(None, 'shard'), may hold values from -3 to 3
- conv_gain: bfloat16 [1024], P('shard'), may hold values from 0.5 to 1.5
- conv_shift: bfloat16 [1024], P('shard'), may hold values from -2 to 2
- gated_weight: bfloat16 [1024, 2048], P('shard'), may hold values from -0.1875 to 0.1875
- depth_kernel: bfloat16 [31, 1024], P(None, 'shard'), may hold values from -1 to 1
- depth_gain: bfloat16 [1024], P('shard'), may hold values from 0.5 to 1.5
- depth_shift: bfloat16 [1024], P('shard'), may hold values from -2 to 2
- pointwise_weight: bfloat16 [1024, 1024], P('shard'), may hold values from -0.1875 to 0.1875
- later_gain: bfloat16 [1024], P('shard'), may hold values from 0.5 to 1.5
- later_shift: bfloat16 [1024], P('shard'), may hold values from -2 to 2
- later_widen: bfloat16 [1024, 4096], P('shard'), may hold values from -0.1875 to 0.1875
- later_offset: bfloat16 [4096], P('shard'), may hold values from -2 to 2
- later_narrow: bfloat16 [4096, 1024], P('shard'), may hold values from -0.1875 to 0.1875
- later_bias: bfloat16 [1024], P('shard'), may hold values from -2 to 2
- final_gain: bfloat16 [1024], P('shard'), may hold values from 0.5 to 1.5
- final_shift: bfloat16 [1024], P('shard'), may hold values from -2 to 2
- cotangent: bfloat16 [2, 1024, 4, 1024], P(None, 'rep', 'shard'), may hold values from -6 to 6
Outputs:
- output: bfloat16 [2, 1024, 4, 1024], P(None, 'rep', 'shard')
- input_grad: float32 [2, 1024, 4, 1024], P(None, 'rep', 'shard')
- grad_early_gain: float32 [1024], P('shard')
- grad_early_shift: float32 [1024], P('shard')
- grad_early_widen: float32 [1024, 4096], P('shard')
- grad_early_offset: float32 [4096], P('shard')
- grad_early_narrow: float32 [4096, 1024], P('shard')
- grad_early_bias: float32 [1024], P('shard')
- grad_attend_gain: float32 [1024], P('shard')
- grad_attend_shift: float32 [1024], P('shard')
- grad_query_weight: float32 [1024, 1024], P('shard')
- grad_query_bias: float32 [1024], P('shard')
- grad_key_weight: float32 [1024, 1024], P('shard')
- grad_value_weight: float32 [1024, 1024], P('shard')
- grad_value_bias: float32 [1024], P('shard')
- grad_mixer_weight: float32 [1024, 1024], P('shard')
- grad_mixer_bias: float32 [1024], P('shard')
- grad_distance_table: float32 [73, 64], P(None, 'shard')
- grad_conv_gain: float32 [1024], P('shard')
- grad_conv_shift: float32 [1024], P('shard')
- grad_gated_weight: float32 [1024, 2048], P('shard')
- grad_depth_kernel: float32 [31, 1024], P(None, 'shard')
- grad_depth_gain: float32 [1024], P('shard')
- grad_depth_shift: float32 [1024], P('shard')
- grad_pointwise_weight: float32 [1024, 1024], P('shard')
- grad_later_gain: float32 [1024], P('shard')
- grad_later_shift: float32 [1024], P('shard')
- grad_later_widen: float32 [1024, 4096], P('shard')
- grad_later_offset: float32 [4096], P('shard')
- grad_later_narrow: float32 [4096, 1024], P('shard')
- grad_later_bias: float32 [1024], P('shard')
- grad_final_gain: float32 [1024], P('shard')
- grad_final_shift: float32 [1024], P('shard')
All inputs are finite; a program needn't handle non-finite values.
Results may differ from a plain program's by a relative error of at most 0.025.
Values may be sent and summed in bfloat16 or wider, within the bound.
A program may use at most 320 MiB of HBM per device.

v0:
```python
import jax
import jax.numpy as jnp
from jax import lax
from jax.sharding import PartitionSpec as P

H = 16
HD = 64
LEFT = 64
RIGHT = 8
TABLE = 73


EPSILON = 1e-05


def shifted(value, axis, steps):
    count = lax.axis_size(axis)
    leading, last = (max(0, -steps), min(count, count - steps))
    return lax.ppermute(value, axis, [(source, source + steps) for source in range(leading, last)])


def as_sent(array):
    return jax.tree.map(lambda a: a.astype(jnp.bfloat16) if a.dtype == jnp.float32 else a, array)


def norm_rows(values, scale_row, offset_row):
    centre = jnp.mean(values, axis=-1, keepdims=True)
    centred = values - centre
    spread = jnp.mean(centred * centred, axis=-1, keepdims=True)
    return centred * lax.rsqrt(spread + EPSILON) * scale_row + offset_row


def swish_value(values):
    return values * jax.nn.sigmoid(values)


def gated_linear(doubled):
    halfway = doubled.shape[-1] // 2
    return doubled[:, :halfway] * jax.nn.sigmoid(doubled[:, halfway:])


def depth_tail(depth_rows, scale_row, offset_row):
    return swish_value(norm_rows(depth_rows, scale_row, offset_row))


def matmul_plain(left_side, right_side):
    return jnp.dot(left_side, right_side, preferred_element_type=jnp.float32)


def matmul_rows(left_side, right_side):
    return lax.dot_general(
        left_side, right_side, (((0,), (0,)), ((), ())), preferred_element_type=jnp.float32
    )


def matmul_back(left_side, right_side):
    return lax.dot_general(
        left_side, right_side, (((1,), (1,)), ((), ())), preferred_element_type=jnp.float32
    )


def fetch_weights(shards):
    return (
        lax.all_gather(shards[0], "shard", axis=0, tiled=True),
        lax.all_gather(shards[1], "shard", axis=0, tiled=True),
        lax.all_gather(shards[2], "shard", axis=0, tiled=True),
        lax.all_gather(shards[3], "shard", axis=0, tiled=True),
        lax.all_gather(shards[4], "shard", axis=0, tiled=True),
        lax.all_gather(shards[5], "shard", axis=0, tiled=True),
        lax.all_gather(shards[6], "shard", axis=0, tiled=True),
        lax.all_gather(shards[7], "shard", axis=0, tiled=True),
        lax.all_gather(shards[8], "shard", axis=0, tiled=True),
        lax.all_gather(shards[9], "shard", axis=0, tiled=True),
        lax.all_gather(shards[10], "shard", axis=0, tiled=True),
        lax.all_gather(shards[11], "shard", axis=0, tiled=True),
        lax.all_gather(shards[12], "shard", axis=0, tiled=True),
        lax.all_gather(shards[13], "shard", axis=0, tiled=True),
        lax.all_gather(shards[14], "shard", axis=0, tiled=True),
        lax.all_gather(shards[15], "shard", axis=1, tiled=True),
        lax.all_gather(shards[16], "shard", axis=0, tiled=True),
        lax.all_gather(shards[17], "shard", axis=0, tiled=True),
        lax.all_gather(shards[18], "shard", axis=0, tiled=True),
        lax.all_gather(shards[19], "shard", axis=1, tiled=True),
        lax.all_gather(shards[20], "shard", axis=0, tiled=True),
        lax.all_gather(shards[21], "shard", axis=0, tiled=True),
        lax.all_gather(shards[22], "shard", axis=0, tiled=True),
        lax.all_gather(shards[23], "shard", axis=0, tiled=True),
        lax.all_gather(shards[24], "shard", axis=0, tiled=True),
        lax.all_gather(shards[25], "shard", axis=0, tiled=True),
        lax.all_gather(shards[26], "shard", axis=0, tiled=True),
        lax.all_gather(shards[27], "shard", axis=0, tiled=True),
        lax.all_gather(shards[28], "shard", axis=0, tiled=True),
        lax.all_gather(shards[29], "shard", axis=0, tiled=True),
        lax.all_gather(shards[30], "shard", axis=0, tiled=True),
    )


def norm_pull(entering, scale_row, offset_row, normed_grad):
    return jax.vjp(
        norm_rows, entering, scale_row.astype(jnp.float32), offset_row.astype(jnp.float32)
    )[1](normed_grad)


def feed_forward(weights, entering):
    normed = norm_rows(
        entering, weights[0].astype(jnp.float32), weights[1].astype(jnp.float32)
    ).astype(jnp.bfloat16)
    inner_act = matmul_plain(normed, weights[2]) + weights[3].astype(jnp.float32)
    hidden = swish_value(inner_act).astype(jnp.bfloat16)
    result = matmul_plain(hidden, weights[4]) + weights[5].astype(jnp.float32)
    return (result, (entering, normed, inner_act, hidden))


def feed_backward(weights, saved, out_grad):
    entering, normed, inner_act, hidden = saved
    out_low = out_grad.astype(jnp.bfloat16)
    grad_narrow = matmul_rows(hidden, out_low)
    grad_bias = jnp.sum(out_low.astype(jnp.float32), axis=0)
    hidden_grad = matmul_back(out_low, weights[4])
    inner_grad = jax.vjp(swish_value, inner_act)[1](hidden_grad)[0].astype(jnp.bfloat16)
    grad_widen = matmul_rows(normed, inner_grad)
    grad_offset = jnp.sum(inner_grad.astype(jnp.float32), axis=0)
    normed_grad = matmul_back(inner_grad, weights[2])
    entering_grad, grad_scale, grad_shift = norm_pull(entering, weights[0], weights[1], normed_grad)
    return (
        entering_grad,
        [grad_scale, grad_shift, grad_widen, grad_offset, grad_narrow, grad_bias],
    )


def relation(query_part, offset_part, query_first, key_part, key_first):
    query_count, seq_count = (query_part.shape[0], query_part.shape[1])
    key_count = key_part.shape[0]
    query_heads = query_part.reshape(query_count, seq_count, H, HD)
    key_heads = key_part.reshape(key_count, seq_count, H, HD)
    raw_scores = jnp.einsum(
        "qshd,kshd->shqk", query_heads, key_heads, preferred_element_type=jnp.float32
    )
    distance = (key_first + jnp.arange(key_count, dtype=jnp.int32))[None, :] - (
        query_first + jnp.arange(query_count, dtype=jnp.int32)
    )[:, None]
    lookup = jnp.clip(distance, -LEFT, RIGHT) + LEFT
    onehot = (lookup[:, :, None] == jnp.arange(TABLE, dtype=jnp.int32)[None, None, :]).astype(
        jnp.bfloat16
    )
    placed = jnp.einsum("qshr,qkr->shqk", offset_part, onehot, preferred_element_type=jnp.float32)
    return ((raw_scores + placed) * 0.125, onehot)


def gradient_terms(
    query_part,
    offset_part,
    query_first,
    grad_part,
    logsum_part,
    balance_part,
    key_part,
    value_part,
    key_first,
):
    scores, onehot = relation(query_part, offset_part, query_first, key_part, key_first)
    probability = jnp.exp(scores - jnp.transpose(logsum_part, (1, 2, 0))[..., None])
    query_count, seq_count = (grad_part.shape[0], grad_part.shape[1])
    key_count = value_part.shape[0]
    value_heads = value_part.reshape(key_count, seq_count, H, HD)
    grad_heads = grad_part.reshape(query_count, seq_count, H, HD)
    prob_grad = jnp.einsum(
        "qshd,kshd->shqk", grad_heads, value_heads, preferred_element_type=jnp.float32
    )
    score_grad = (
        probability * (prob_grad - jnp.transpose(balance_part, (1, 2, 0))[..., None])
    ).astype(jnp.bfloat16)
    return (probability, score_grad, onehot)


def key_terms(
    query_part,
    offset_part,
    query_first,
    grad_part,
    logsum_part,
    balance_part,
    key_part,
    value_part,
    key_first,
):
    probability, score_grad, onehot = gradient_terms(
        query_part,
        offset_part,
        query_first,
        grad_part,
        logsum_part,
        balance_part,
        key_part,
        value_part,
        key_first,
    )
    query_count, seq_count = (query_part.shape[0], query_part.shape[1])
    query_heads = query_part.reshape(query_count, seq_count, H, HD)
    grad_heads = grad_part.reshape(query_count, seq_count, H, HD)
    key_grad = jnp.einsum(
        "shqk,qshd->kshd", score_grad, query_heads, preferred_element_type=jnp.float32
    )
    value_grad = jnp.einsum(
        "shqk,qshd->kshd",
        probability.astype(jnp.bfloat16),
        grad_heads,
        preferred_element_type=jnp.float32,
    )
    return (key_grad, value_grad)


def attention_forward(weights, entering):
    local_len, seq_count, features = entering.shape
    row_count = local_len * seq_count
    flat_rows = entering.reshape(row_count, features)
    normed = norm_rows(
        flat_rows, weights[0].astype(jnp.float32), weights[1].astype(jnp.float32)
    ).astype(jnp.bfloat16)
    query_rows = (
        (matmul_plain(normed, weights[2]) + weights[3].astype(jnp.float32))
        .astype(jnp.bfloat16)
        .reshape(local_len, seq_count, features)
    )
    key_rows = (
        matmul_plain(normed, weights[4])
        .astype(jnp.bfloat16)
        .reshape(local_len, seq_count, features)
    )
    values = (
        (matmul_plain(normed, weights[5]) + weights[6].astype(jnp.float32))
        .astype(jnp.bfloat16)
        .reshape(local_len, seq_count, features)
    )
    offsets = jnp.einsum(
        "cshd,rd->cshr",
        query_rows.reshape(local_len, seq_count, H, HD),
        weights[9],
        preferred_element_type=jnp.float32,
    ).astype(jnp.bfloat16)
    own_first = lax.axis_index("rep") * local_len
    highest = jnp.full((seq_count, H, local_len), -jnp.inf, jnp.float32)
    summed = jnp.zeros((seq_count, H, local_len), jnp.float32)
    scores = relation(
        query_rows,
        offsets,
        own_first,
        lax.all_gather(key_rows, "rep", axis=0, tiled=True),
        jnp.int32(0),
    )[0]
    newest = jnp.max(scores, axis=-1)
    summed = summed * jnp.exp(highest - newest) + jnp.sum(
        jnp.exp(scores - newest[..., None]), axis=-1
    )
    highest, summed = (newest, summed)
    logsum_heads = highest + jnp.log(summed)
    key_part = lax.all_gather(key_rows, "rep", axis=0, tiled=True)
    value_part = lax.all_gather(values, "rep", axis=0, tiled=True)
    scores = relation(query_rows, offsets, own_first, key_part, jnp.int32(0))[0]
    probability = jnp.exp(scores - logsum_heads[..., None]).astype(jnp.bfloat16)
    key_count = value_part.shape[0]
    value_heads = value_part.reshape(key_count, seq_count, H, HD)
    mixed_heads = jnp.einsum(
        "shqk,kshd->qshd", probability, value_heads, preferred_element_type=jnp.float32
    )
    mixed_low = mixed_heads.astype(jnp.bfloat16).reshape(row_count, features)
    result = matmul_plain(mixed_low, weights[7]) + weights[8].astype(jnp.float32)
    logsum = jnp.transpose(logsum_heads, (2, 0, 1))
    return (
        result,
        (flat_rows, normed, query_rows, key_rows, values, offsets, logsum, mixed_heads, mixed_low),
    )


def attention_backward(weights, saved, out_grad):
    flat_rows, normed, query_rows, key_rows, values, offsets, logsum, mixed_heads, mixed_low = saved
    local_len, seq_count, features = query_rows.shape
    row_count = local_len * seq_count
    out_low = out_grad.astype(jnp.bfloat16)
    grad_mixer = matmul_rows(mixed_low, out_low)
    grad_mixer_bias = jnp.sum(out_low.astype(jnp.float32), axis=0)
    mixed_grad = (
        matmul_back(out_low, weights[7])
        .astype(jnp.bfloat16)
        .reshape(local_len, seq_count, features)
    )
    balance = jnp.sum(
        mixed_grad.astype(jnp.float32).reshape(local_len, seq_count, H, HD) * mixed_heads, axis=-1
    )
    own_first = lax.axis_index("rep") * local_len
    zero_heads = jnp.zeros((local_len, seq_count, H, HD), jnp.float32)
    zero_table = jnp.zeros((local_len, seq_count, H, TABLE), jnp.float32)

    def query_step(running, key_parts, key_first):
        key_part, value_part = key_parts
        score_grad, onehot = gradient_terms(
            query_rows,
            offsets,
            own_first,
            mixed_grad,
            logsum,
            balance,
            key_part,
            value_part,
            key_first,
        )[1:]
        key_count = key_part.shape[0]
        key_heads = key_part.reshape(key_count, seq_count, H, HD)
        return (
            running[0]
            + jnp.einsum(
                "shqk,kshd->qshd", score_grad, key_heads, preferred_element_type=jnp.float32
            ),
            running[1]
            + jnp.einsum("shqk,qkr->qshr", score_grad, onehot, preferred_element_type=jnp.float32),
        )

    all_keys, all_values = (
        lax.all_gather(key_rows, "rep", axis=0, tiled=True),
        lax.all_gather(values, "rep", axis=0, tiled=True),
    )
    blocks = all_keys.shape[0] // local_len

    def scan_step(running, members):
        key_part, value_part, key_first = members
        return (query_step(running, (key_part, value_part), key_first), None)

    scan_parts = (
        all_keys.reshape(blocks, local_len, seq_count, features),
        all_values.reshape(blocks, local_len, seq_count, features),
        jnp.arange(blocks, dtype=jnp.int32) * local_len,
    )
    (query_total, offset_total), _ = lax.scan(scan_step, (zero_heads, zero_table), scan_parts)
    count = lax.axis_size("rep") * local_len
    key_part = all_keys
    value_part = all_values
    key_grad, value_grad = key_terms(
        query_rows,
        offsets,
        own_first,
        mixed_grad,
        logsum,
        balance,
        key_part,
        value_part,
        jnp.int32(0),
    )
    summed = lax.psum_scatter(
        jnp.stack(
            [
                key_grad.reshape(count, seq_count, features),
                value_grad.reshape(count, seq_count, features),
            ],
            axis=1,
        ).astype(jnp.bfloat16),
        "rep",
        scatter_dimension=0,
        tiled=True,
    ).astype(jnp.float32)
    key_total = summed[:, 0]
    value_total = summed[:, 1]
    offset_grad = (offset_total * 0.125).astype(jnp.bfloat16)
    query_grad = query_total * 0.125 + jnp.einsum(
        "cshr,rd->cshd", offset_grad, weights[9], preferred_element_type=jnp.float32
    )
    query_grad = query_grad.astype(jnp.bfloat16).reshape(row_count, features)
    grad_table = jnp.einsum(
        "cshr,cshd->rd",
        offset_grad,
        query_rows.reshape(local_len, seq_count, H, HD),
        preferred_element_type=jnp.float32,
    )
    key_grad = (key_total * 0.125).astype(jnp.bfloat16).reshape(row_count, features)
    value_grad = value_total.astype(jnp.bfloat16).reshape(row_count, features)
    grad_query = matmul_rows(normed, query_grad)
    grad_query_bias = jnp.sum(query_grad.astype(jnp.float32), axis=0)
    grad_key = matmul_rows(normed, key_grad)
    grad_value = matmul_rows(normed, value_grad)
    grad_value_bias = jnp.sum(value_grad.astype(jnp.float32), axis=0)
    normed_grad = (
        matmul_back(query_grad, weights[2])
        + matmul_back(key_grad, weights[4])
        + matmul_back(value_grad, weights[5])
    )
    entering_grad, grad_scale, grad_shift = norm_pull(
        flat_rows, weights[0], weights[1], normed_grad
    )
    return (
        entering_grad,
        [
            grad_scale,
            grad_shift,
            grad_query,
            grad_query_bias,
            grad_key,
            grad_value,
            grad_value_bias,
            grad_mixer,
            grad_mixer_bias,
            grad_table,
        ],
    )


def conv_forward(weights, entering):
    local_len, seq_count, features = entering.shape
    row_count = local_len * seq_count
    flat_rows = entering.reshape(row_count, features)
    normed = norm_rows(
        flat_rows, weights[0].astype(jnp.float32), weights[1].astype(jnp.float32)
    ).astype(jnp.bfloat16)
    doubled = matmul_plain(normed, weights[2])
    gated_rows = gated_linear(doubled).reshape(local_len, seq_count, features)
    kernel = weights[3].astype(jnp.float32)
    rim_rows = kernel.shape[0] - 1
    rim_rows_in = shifted(gated_rows[local_len - rim_rows :].astype(jnp.bfloat16), "rep", 1).astype(
        jnp.float32
    )
    padded = jnp.concatenate([rim_rows_in, gated_rows], axis=0)
    depth_rows = padded[0:local_len] * kernel[0]
    for tap_index in range(1, rim_rows + 1):
        depth_rows = depth_rows + padded[tap_index : tap_index + local_len] * kernel[tap_index]
    acted_rows = depth_tail(
        depth_rows, weights[4].astype(jnp.float32), weights[5].astype(jnp.float32)
    )
    acted_rows = acted_rows.astype(jnp.bfloat16).reshape(row_count, features)
    result = matmul_plain(acted_rows, weights[6])
    return (result, (flat_rows, normed, doubled, padded, depth_rows, acted_rows))


def conv_backward(weights, saved, out_grad):
    flat_rows, normed, doubled, padded, depth_rows, acted_rows = saved
    local_len, seq_count, features = depth_rows.shape
    row_count = local_len * seq_count
    out_low = out_grad.astype(jnp.bfloat16)
    grad_pointwise = matmul_rows(acted_rows, out_low)
    acted_grad = matmul_back(out_low, weights[6]).reshape(local_len, seq_count, features)
    depth_grad, grad_depth_scale, grad_depth_shift = jax.vjp(
        depth_tail, depth_rows, weights[4].astype(jnp.float32), weights[5].astype(jnp.float32)
    )[1](acted_grad)
    kernel = weights[3].astype(jnp.float32)
    rim_rows = kernel.shape[0] - 1
    kernel_rows = []
    padded_grad = jnp.zeros((local_len + rim_rows, seq_count, features), jnp.float32)
    for tap_index in range(rim_rows + 1):
        kernel_rows.append(
            jnp.sum(depth_grad * padded[tap_index : tap_index + local_len], axis=(0, 1))
        )
        padded_grad = padded_grad + jnp.pad(
            depth_grad * kernel[tap_index], ((tap_index, rim_rows - tap_index), (0, 0), (0, 0))
        )
    grad_kernel = jnp.stack(kernel_rows, axis=0)
    rim_grad = shifted(as_sent(padded_grad[:rim_rows]), "rep", -1)
    gated_grad = padded_grad[rim_rows:] + jnp.concatenate(
        [jnp.zeros((local_len - rim_rows, seq_count, features), jnp.float32), rim_grad], axis=0
    )
    doubled_grad = jax.vjp(gated_linear, doubled)[1](gated_grad.reshape(row_count, features))[
        0
    ].astype(jnp.bfloat16)
    grad_gated = matmul_rows(normed, doubled_grad)
    normed_grad = matmul_back(doubled_grad, weights[2])
    entering_grad, grad_scale, grad_shift = norm_pull(
        flat_rows, weights[0], weights[1], normed_grad
    )
    return (
        entering_grad,
        [
            grad_scale,
            grad_shift,
            grad_gated,
            grad_kernel,
            grad_depth_scale,
            grad_depth_shift,
            grad_pointwise,
        ],
    )


def on_device(
    inputs,
    early_gain,
    early_shift,
    early_widen,
    early_offset,
    early_narrow,
    early_bias,
    attend_gain,
    attend_shift,
    query_weight,
    query_bias,
    key_weight,
    value_weight,
    value_bias,
    mixer_weight,
    mixer_bias,
    distance_table,
    conv_gain,
    conv_shift,
    gated_weight,
    depth_kernel,
    depth_gain,
    depth_shift,
    pointwise_weight,
    later_gain,
    later_shift,
    later_widen,
    later_offset,
    later_narrow,
    later_bias,
    final_gain,
    final_shift,
    cotangent,
):
    shards = (
        early_gain,
        early_shift,
        early_widen,
        early_offset,
        early_narrow,
        early_bias,
        attend_gain,
        attend_shift,
        query_weight,
        query_bias,
        key_weight,
        value_weight,
        value_bias,
        mixer_weight,
        mixer_bias,
        distance_table,
        conv_gain,
        conv_shift,
        gated_weight,
        depth_kernel,
        depth_gain,
        depth_shift,
        pointwise_weight,
        later_gain,
        later_shift,
        later_widen,
        later_offset,
        later_narrow,
        later_bias,
        final_gain,
        final_shift,
    )
    totals = None
    outputs = []
    input_grads = []
    for micro_index in range(inputs.shape[0]):
        weights = fetch_weights(shards)
        entering = inputs[micro_index].astype(jnp.float32)
        local_len, seq_count, features = entering.shape
        row_count = local_len * seq_count
        level_zero = entering.reshape(row_count, features)
        early_result, early_saved = feed_forward(weights[0:6], level_zero)
        level_one = level_zero + 0.5 * early_result
        attend_result, attend_saved = attention_forward(
            weights[6:16], level_one.reshape(local_len, seq_count, features)
        )
        level_two = level_one + attend_result
        conv_result, conv_saved = conv_forward(
            weights[16:23], level_two.reshape(local_len, seq_count, features)
        )
        level_three = level_two + conv_result
        later_result, later_saved = feed_forward(weights[23:29], level_three)
        level_four = level_three + 0.5 * later_result
        final_rows = norm_rows(
            level_four, weights[29].astype(jnp.float32), weights[30].astype(jnp.float32)
        )
        outputs.append(final_rows.astype(jnp.bfloat16).reshape(local_len, seq_count, features))
        back_weights = fetch_weights(shards)
        incoming = cotangent[micro_index].astype(jnp.float32).reshape(row_count, features)
        back_four, grad_final_scale, grad_final_shift = norm_pull(
            level_four, back_weights[29], back_weights[30], incoming
        )
        back_part, later_grads = feed_backward(back_weights[23:29], later_saved, 0.5 * back_four)
        back_three = back_four + back_part
        back_part, conv_grads = conv_backward(back_weights[16:23], conv_saved, back_three)
        back_two = back_three + back_part
        back_part, attend_grads = attention_backward(back_weights[6:16], attend_saved, back_two)
        back_one = back_two + back_part
        back_part, early_grads = feed_backward(back_weights[0:6], early_saved, 0.5 * back_one)
        input_grads.append((back_one + back_part).reshape(local_len, seq_count, features))
        fresh_grads = (
            early_grads
            + attend_grads
            + conv_grads
            + later_grads
            + [grad_final_scale, grad_final_shift]
        )
        totals = fresh_grads if totals is None else jax.tree.map(jnp.add, totals, fresh_grads)
    sectioned = list(totals)
    shares = (
        lax.psum_scatter(
            sectioned[0].astype(jnp.bfloat16), "shard", scatter_dimension=0, tiled=True
        ).astype(jnp.float32),
        lax.psum_scatter(
            sectioned[1].astype(jnp.bfloat16), "shard", scatter_dimension=0, tiled=True
        ).astype(jnp.float32),
        lax.psum_scatter(
            sectioned[2].astype(jnp.bfloat16), "shard", scatter_dimension=0, tiled=True
        ).astype(jnp.float32),
        lax.psum_scatter(
            sectioned[3].astype(jnp.bfloat16), "shard", scatter_dimension=0, tiled=True
        ).astype(jnp.float32),
        lax.psum_scatter(
            sectioned[4].astype(jnp.bfloat16), "shard", scatter_dimension=0, tiled=True
        ).astype(jnp.float32),
        lax.psum_scatter(
            sectioned[5].astype(jnp.bfloat16), "shard", scatter_dimension=0, tiled=True
        ).astype(jnp.float32),
        lax.psum_scatter(
            sectioned[6].astype(jnp.bfloat16), "shard", scatter_dimension=0, tiled=True
        ).astype(jnp.float32),
        lax.psum_scatter(
            sectioned[7].astype(jnp.bfloat16), "shard", scatter_dimension=0, tiled=True
        ).astype(jnp.float32),
        lax.psum_scatter(
            sectioned[8].astype(jnp.bfloat16), "shard", scatter_dimension=0, tiled=True
        ).astype(jnp.float32),
        lax.psum_scatter(
            sectioned[9].astype(jnp.bfloat16), "shard", scatter_dimension=0, tiled=True
        ).astype(jnp.float32),
        lax.psum_scatter(
            sectioned[10].astype(jnp.bfloat16), "shard", scatter_dimension=0, tiled=True
        ).astype(jnp.float32),
        lax.psum_scatter(
            sectioned[11].astype(jnp.bfloat16), "shard", scatter_dimension=0, tiled=True
        ).astype(jnp.float32),
        lax.psum_scatter(
            sectioned[12].astype(jnp.bfloat16), "shard", scatter_dimension=0, tiled=True
        ).astype(jnp.float32),
        lax.psum_scatter(
            sectioned[13].astype(jnp.bfloat16), "shard", scatter_dimension=0, tiled=True
        ).astype(jnp.float32),
        lax.psum_scatter(
            sectioned[14].astype(jnp.bfloat16), "shard", scatter_dimension=0, tiled=True
        ).astype(jnp.float32),
        lax.psum_scatter(
            sectioned[15].astype(jnp.bfloat16), "shard", scatter_dimension=1, tiled=True
        ).astype(jnp.float32),
        lax.psum_scatter(
            sectioned[16].astype(jnp.bfloat16), "shard", scatter_dimension=0, tiled=True
        ).astype(jnp.float32),
        lax.psum_scatter(
            sectioned[17].astype(jnp.bfloat16), "shard", scatter_dimension=0, tiled=True
        ).astype(jnp.float32),
        lax.psum_scatter(
            sectioned[18].astype(jnp.bfloat16), "shard", scatter_dimension=0, tiled=True
        ).astype(jnp.float32),
        lax.psum_scatter(
            sectioned[19].astype(jnp.bfloat16), "shard", scatter_dimension=1, tiled=True
        ).astype(jnp.float32),
        lax.psum_scatter(
            sectioned[20].astype(jnp.bfloat16), "shard", scatter_dimension=0, tiled=True
        ).astype(jnp.float32),
        lax.psum_scatter(
            sectioned[21].astype(jnp.bfloat16), "shard", scatter_dimension=0, tiled=True
        ).astype(jnp.float32),
        lax.psum_scatter(
            sectioned[22].astype(jnp.bfloat16), "shard", scatter_dimension=0, tiled=True
        ).astype(jnp.float32),
        lax.psum_scatter(
            sectioned[23].astype(jnp.bfloat16), "shard", scatter_dimension=0, tiled=True
        ).astype(jnp.float32),
        lax.psum_scatter(
            sectioned[24].astype(jnp.bfloat16), "shard", scatter_dimension=0, tiled=True
        ).astype(jnp.float32),
        lax.psum_scatter(
            sectioned[25].astype(jnp.bfloat16), "shard", scatter_dimension=0, tiled=True
        ).astype(jnp.float32),
        lax.psum_scatter(
            sectioned[26].astype(jnp.bfloat16), "shard", scatter_dimension=0, tiled=True
        ).astype(jnp.float32),
        lax.psum_scatter(
            sectioned[27].astype(jnp.bfloat16), "shard", scatter_dimension=0, tiled=True
        ).astype(jnp.float32),
        lax.psum_scatter(
            sectioned[28].astype(jnp.bfloat16), "shard", scatter_dimension=0, tiled=True
        ).astype(jnp.float32),
        lax.psum_scatter(
            sectioned[29].astype(jnp.bfloat16), "shard", scatter_dimension=0, tiled=True
        ).astype(jnp.float32),
        lax.psum_scatter(
            sectioned[30].astype(jnp.bfloat16), "shard", scatter_dimension=0, tiled=True
        ).astype(jnp.float32),
    )
    summed = (
        lax.psum(shares[0].astype(jnp.bfloat16), "rep").astype(jnp.float32),
        lax.psum(shares[1].astype(jnp.bfloat16), "rep").astype(jnp.float32),
        lax.psum(shares[2].astype(jnp.bfloat16), "rep").astype(jnp.float32),
        lax.psum(shares[3].astype(jnp.bfloat16), "rep").astype(jnp.float32),
        lax.psum(shares[4].astype(jnp.bfloat16), "rep").astype(jnp.float32),
        lax.psum(shares[5].astype(jnp.bfloat16), "rep").astype(jnp.float32),
        lax.psum(shares[6].astype(jnp.bfloat16), "rep").astype(jnp.float32),
        lax.psum(shares[7].astype(jnp.bfloat16), "rep").astype(jnp.float32),
        lax.psum(shares[8].astype(jnp.bfloat16), "rep").astype(jnp.float32),
        lax.psum(shares[9].astype(jnp.bfloat16), "rep").astype(jnp.float32),
        lax.psum(shares[10].astype(jnp.bfloat16), "rep").astype(jnp.float32),
        lax.psum(shares[11].astype(jnp.bfloat16), "rep").astype(jnp.float32),
        lax.psum(shares[12].astype(jnp.bfloat16), "rep").astype(jnp.float32),
        lax.psum(shares[13].astype(jnp.bfloat16), "rep").astype(jnp.float32),
        lax.psum(shares[14].astype(jnp.bfloat16), "rep").astype(jnp.float32),
        lax.psum(shares[15].astype(jnp.bfloat16), "rep").astype(jnp.float32),
        lax.psum(shares[16].astype(jnp.bfloat16), "rep").astype(jnp.float32),
        lax.psum(shares[17].astype(jnp.bfloat16), "rep").astype(jnp.float32),
        lax.psum(shares[18].astype(jnp.bfloat16), "rep").astype(jnp.float32),
        lax.psum(shares[19].astype(jnp.bfloat16), "rep").astype(jnp.float32),
        lax.psum(shares[20].astype(jnp.bfloat16), "rep").astype(jnp.float32),
        lax.psum(shares[21].astype(jnp.bfloat16), "rep").astype(jnp.float32),
        lax.psum(shares[22].astype(jnp.bfloat16), "rep").astype(jnp.float32),
        lax.psum(shares[23].astype(jnp.bfloat16), "rep").astype(jnp.float32),
        lax.psum(shares[24].astype(jnp.bfloat16), "rep").astype(jnp.float32),
        lax.psum(shares[25].astype(jnp.bfloat16), "rep").astype(jnp.float32),
        lax.psum(shares[26].astype(jnp.bfloat16), "rep").astype(jnp.float32),
        lax.psum(shares[27].astype(jnp.bfloat16), "rep").astype(jnp.float32),
        lax.psum(shares[28].astype(jnp.bfloat16), "rep").astype(jnp.float32),
        lax.psum(shares[29].astype(jnp.bfloat16), "rep").astype(jnp.float32),
        lax.psum(shares[30].astype(jnp.bfloat16), "rep").astype(jnp.float32),
    )
    return (
        jnp.stack(outputs, axis=0),
        jnp.stack(input_grads, axis=0),
        summed[0],
        summed[1],
        summed[2],
        summed[3],
        summed[4],
        summed[5],
        summed[6],
        summed[7],
        summed[8],
        summed[9],
        summed[10],
        summed[11],
        summed[12],
        summed[13],
        summed[14],
        summed[15],
        summed[16],
        summed[17],
        summed[18],
        summed[19],
        summed[20],
        summed[21],
        summed[22],
        summed[23],
        summed[24],
        summed[25],
        summed[26],
        summed[27],
        summed[28],
        summed[29],
        summed[30],
    )


def solution(mesh):
    in_specs = (
        P(None, "rep", "shard", None),
        P("shard"),
        P("shard"),
        P("shard", None),
        P("shard"),
        P("shard", None),
        P("shard"),
        P("shard"),
        P("shard"),
        P("shard", None),
        P("shard"),
        P("shard", None),
        P("shard", None),
        P("shard"),
        P("shard", None),
        P("shard"),
        P(None, "shard"),
        P("shard"),
        P("shard"),
        P("shard", None),
        P(None, "shard"),
        P("shard"),
        P("shard"),
        P("shard", None),
        P("shard"),
        P("shard"),
        P("shard", None),
        P("shard"),
        P("shard", None),
        P("shard"),
        P("shard"),
        P("shard"),
        P(None, "rep", "shard", None),
    )
    out_specs = (
        P(None, "rep", "shard", None),
        P(None, "rep", "shard", None),
        P("shard"),
        P("shard"),
        P("shard", None),
        P("shard"),
        P("shard", None),
        P("shard"),
        P("shard"),
        P("shard"),
        P("shard", None),
        P("shard"),
        P("shard", None),
        P("shard", None),
        P("shard"),
        P("shard", None),
        P("shard"),
        P(None, "shard"),
        P("shard"),
        P("shard"),
        P("shard", None),
        P(None, "shard"),
        P("shard"),
        P("shard"),
        P("shard", None),
        P("shard"),
        P("shard"),
        P("shard", None),
        P("shard"),
        P("shard", None),
        P("shard"),
        P("shard"),
        P("shard"),
    )
    return jax.shard_map(
        on_device, mesh=mesh, in_specs=in_specs, out_specs=out_specs, check_vma=False
    )
```

profile of v0, /device:TPU:0, one launch (start us, length us, event | category | flops | bytes accessed | tf_op | source)
XLA Modules:
  0.0 2506.4 jit_solution(17123563090635617798)
XLA Ops:
  10.7 12.6 all-gather.6
  23.4 13.6 all_gather.73
  37.0 9.0 all-gather.5
  46.0 10.3 all-gather.4
  57.4 8.5 all-gather.8
  65.9 12.4 all-gather.7
  78.4 11.2 all-gather.9
  89.6 72.7 %all-gather.36.cloned.1.call-done = bf16[1024,4096]{1,0:T(8,128)(2,1)} async-done(((bf16[256,4096]{1,0:T(8,128)(2,1)}), bf16[1024,4096]{1,0:T(8,128)(2,1)}) %all-gather.36.cloned.1.call-update) | async-done | bytes 8388624 | tf_op jit(solution)/shard_map/all_gather | solution.py:66
  167.1 144.7 %all-gather.38.cloned.1.call-done = bf16[4096,1024]{1,0:T(8,128)(2,1)} async-done(((bf16[1024,1024]{1,0:T(8,128)(2,1)}), bf16[4096,1024]{1,0:T(8,128)(2,1)}) %all-gather.38.cloned.1.call-update) | async-done | bytes 8388624 | tf_op jit(solution)/shard_map/all_gather | solution.py:68
  323.5 34.1 %all-gather.40.cloned.1.call-done = bf16[1024,1024]{1,0:T(8,128)(2,1)} async-done(((bf16[256,1024]{1,0:T(8,128)(2,1)}), bf16[1024,1024]{1,0:T(8,128)(2,1)}) %all-gather.40.cloned.1.call-update) | async-done | bytes 2097168 | tf_op jit(solution)/shard_map/all_gather | solution.py:75
  360.4 43.3 %all-gather.44.cloned.1.call-done = bf16[1024,1024]{1,0:T(8,128)(2,1)} async-done(((bf16[256,1024]{1,0:T(8,128)(2,1)}), bf16[1024,1024]{1,0:T(8,128)(2,1)}) %all-gather.44.cloned.1.call-update) | async-done | bytes 2097168 | tf_op jit(solution)/shard_map/all_gather | solution.py:74
  414.2 13.8 all_gather.91
  429.4 8.6 all-gather.11
  438.6 9.9 all-gather.10
  448.5 13.1 all_gather.85
  462.6 7.9 all-gather.15
  471.1 9.2 all-gather.14
  480.9 7.9 all-gather.13
  488.9 9.2 all-gather.12
  498.1 7.9 all-gather.18
  506.7 11.9 all_gather.98
  518.5 8.4 all-gather.17
  527.0 8.9 all-gather.16
  535.9 8.6 all-gather.19
  545.2 8.8 all-gather.20
  560.6 9.9 fusion.33
  570.5 8.7 fusion.32
  586.7 9.9 fusion.304
  596.6 15.4 exponential_reduce_fusion.1
  617.3 22.0 all-gather.48.cloned.1.call-done
  645.5 22.6 all-gather.60.cloned.1.call-done
  672.0 26.5 %all-gather.62.cloned.1.call-done = bf16[1024,1024]{1,0:T(8,128)(2,1)} async-done(((bf16[128,1024]{1,0:T(8,128)(2,1)}), bf16[1024,1024]{1,0:T(8,128)(2,1)}) %all-gather.62.cloned.1.call-update) | async-done | bytes 2097168 | tf_op jit(solution)/shard_map/all_gather | solution.py:257
  702.4 9.8 fusion.309
  730.5 15.3 all-gather.50.cloned.1.call-done
  749.4 146.4 %all-gather.52.cloned.1.call-done = bf16[1024,4096]{1,0:T(8,128)(2,1)} async-done(((bf16[256,4096]{1,0:T(8,128)(2,1)}), bf16[1024,4096]{1,0:T(8,128)(2,1)}) %all-gather.52.cloned.1.call-update) | async-done | bytes 8388624 | tf_op jit(solution)/shard_map/all_gather | solution.py:89
  902.1 143.0 %all-gather.54.cloned.1.call-done = bf16[4096,1024]{1,0:T(8,128)(2,1)} async-done(((bf16[1024,1024]{1,0:T(8,128)(2,1)}), bf16[4096,1024]{1,0:T(8,128)(2,1)}) %all-gather.54.cloned.1.call-update) | async-done | bytes 8388624 | tf_op jit(solution)/shard_map/all_gather | solution.py:91
  1064.8 7.2 convert_reduce_fusion
  1074.9 7.1 convert_reduce_fusion.1
  1125.9 6.5 convolution_convert_fusion
  1132.5 6.6 fusion.70
  1158.7 7.3 convolution_convert_fusion.1
  1191.1 113.7 %while.27 = (s32[]{:T(128)}, f32[128,1,16,64]{0,3,2,1:T(8,128)}, f32[128,1,16,73]{3,2,0,1:T(8,128)}, bf16[8,128,1,1024]{3,1,0,2:T(8,128)(2,1)}, bf16[128,1024]{0...) while((s32[]{:T(128)}, f32[128,1,16,64]{0,3,2,1:T(8,128)}, ...), condition=%wide.region_54.55_spmd.clone, body=%wide.region_53.54_spmd.clone.sunk | while | flops 181784832 | bytes 19863784 | solution.py:333
  1304.8 98.1 %while.26 = (s32[]{:T(128)}, f32[128,1,16,64]{0,3,2,1:T(8,128)}, f32[128,1,16,73]{3,2,0,1:T(8,128)}, bf16[8,128,1,1024]{3,1,0,2:T(8,128)(2,1)}, bf16[128,1024]{0...) while((s32[]{:T(128)}, f32[128,1,16,64]{0,3,2,1:T(8,128)}, ...), condition=%wide.region_38.39_spmd.clone, body=%wide.region_37.38_spmd.clone.sunk | while | flops 181784832 | bytes 22108448 | solution.py:333
  1433.7 9.4 fusion.281
  1443.1 11.5 add_convert_fusion.1
  1456.2 8.1 fusion.283
  1464.3 11.8 add_convert_fusion
  1488.5 6.6 convert_reduce_fusion.3
  1495.2 8.2 fusion.273
  1503.4 6.5 convert_reduce_fusion.2
  1510.9 12.2 add_convert_fusion.3
  1523.2 9.3 fusion.270
  1532.5 9.2 add_convert_fusion.2
  1554.2 28.1 %reduce-scatter.33.cloned.1.call-done = bf16[256,2048]{1,0:T(8,128)(2,1)} async-done(((bf16[1024,2048]{1,0:T(8,128)(2,1)}), bf16[256,2048]{1,0:T(8,128)(2,1)}) %reduce-scatter.33.cloned.1.call-update) | async-done | bytes 1048592 | tf_op jit(solution)/shard_map/reduce_scatter | solution.py:649
  1582.3 47.3 %reduce-scatter.25.cloned.1.call-done = bf16[256,1024]{1,0:T(8,128)(2,1)} async-done(((bf16[1024,1024]{1,0:T(8,128)(2,1)}), bf16[256,1024]{1,0:T(8,128)(2,1)}) %reduce-scatter.25.cloned.1.call-update) | async-done | bytes 524304 | tf_op jit(solution)/shard_map/reduce_scatter | solution.py:625
  1629.6 46.2 %reduce-scatter.27.cloned.1.call-done = bf16[256,1024]{1,0:T(8,128)(2,1)} async-done(((bf16[1024,1024]{1,0:T(8,128)(2,1)}), bf16[256,1024]{1,0:T(8,128)(2,1)}) %reduce-scatter.27.cloned.1.call-update) | async-done | bytes 524304 | tf_op jit(solution)/shard_map/reduce_scatter | solution.py:628
  1675.7 146.2 %reduce-scatter.39.cloned.1.call-done = bf16[256,4096]{1,0:T(8,128)(2,1)} async-done(((bf16[1024,4096]{1,0:T(8,128)(2,1)}), bf16[256,4096]{1,0:T(8,128)(2,1)}) %reduce-scatter.39.cloned.1.call-update) | async-done | bytes 2097168 | tf_op jit(solution)/shard_map/reduce_scatter | solution.py:670
  1821.9 147.4 %reduce-scatter.41.cloned.1.call-done = bf16[1024,1024]{1,0:T(8,128)(2,1)} async-done(((bf16[4096,1024]{1,0:T(8,128)(2,1)}), bf16[1024,1024]{1,0:T(8,128)(2,1)}) %reduce-scatter.41.cloned.1.call-update) | async-done | bytes 2097168 | tf_op jit(solution)/shard_map/reduce_scatter | solution.py:676
  1969.4 147.6 %reduce-scatter.19.cloned.1.call-done = bf16[256,4096]{1,0:T(8,128)(2,1)} async-done(((bf16[1024,4096]{1,0:T(8,128)(2,1)}), bf16[256,4096]{1,0:T(8,128)(2,1)}) %reduce-scatter.19.cloned.1.call-update) | async-done | bytes 2097168 | tf_op jit(solution)/shard_map/reduce_scatter | solution.py:601
  2117.0 147.4 %reduce-scatter.21.cloned.1.call-done = bf16[1024,1024]{1,0:T(8,128)(2,1)} async-done(((bf16[4096,1024]{1,0:T(8,128)(2,1)}), bf16[1024,1024]{1,0:T(8,128)(2,1)}) %reduce-scatter.21.cloned.1.call-update) | async-done | bytes 2097168 | tf_op jit(solution)/shard_map/reduce_scatter | solution.py:607
  2272.9 6.5 fusion.131
  2283.0 19.2 all-reduce.89
  2306.3 23.6 all-reduce.87
  2341.9 138.7 %all-reduce.92.cloned.1.call-done = (bf16[256,4096]{1,0:T(8,128)(2,1)}, bf16[1024,1024]{1,0:T(8,128)(2,1)}, bf16[256,1024]{1,0:T(8,128)(2,1)}, bf16[256,1024]{1,...) async-done(((bf16[256,4096]{1,0:T(8,128)(2,1)}, ...) | async-done | bytes 12058640 | tf_op jit(solution)/shard_map/psum | solution.py:692
  (1356 shorter events, 522.3 us)
Async XLA Ops:
  7.2 155.1 %all-gather.36.cloned.1.call-start = ((), (), s32[]{:S(2)}) async-start(), calls=%async_computation.14 | async-start | bytes 10485760 | tf_op jit(solution)/shard_map/all_gather | solution.py:66
  8.0 57.9 %copy-start.318 = (bf16[256]{0:T(256)(128)(2,1)S(1)}, bf16[256]{0:T(256)(128)(2,1)}, u32[]{:S(2)}) copy-start(bf16[256]{0:T(256)(128)(2,1)} %param.44) | copy-start | bytes 1540
  8.0 70.3 %copy-start.319 = (bf16[256]{0:T(256)(128)(2,1)S(1)}, bf16[256]{0:T(256)(128)(2,1)}, u32[]{:S(2)}) copy-start(bf16[256]{0:T(256)(128)(2,1)} %param.50) | copy-start | bytes 1540
  8.0 303.8 %all-gather.38.cloned.1.call-start = ((), (), s32[]{:S(2)}) async-start(), calls=%async_computation.15 | async-start | bytes 10485760 | tf_op jit(solution)/shard_map/all_gather | solution.py:68
  8.8 348.8 %all-gather.40.cloned.1.call-start = ((), (), s32[]{:S(2)}) async-start(), calls=%async_computation.16 | async-start | bytes 2621440 | tf_op jit(solution)/shard_map/all_gather | solution.py:75
  9.5 394.2 %all-gather.44.cloned.1.call-start = ((), (), s32[]{:S(2)}) async-start(), calls=%async_computation.18 | async-start | bytes 2621440 | tf_op jit(solution)/shard_map/all_gather | solution.py:74
  10.1 544.5 %all-gather.42.cloned.1.call-start = ((), (), s32[]{:S(2)}) async-start(), calls=%async_computation.17 | async-start | bytes 2621440 | tf_op jit(solution)/shard_map/all_gather | solution.py:72
  10.7 568.5 %all-gather.56.cloned.1.call-start = ((), (), s32[]{:S(2)}) async-start(), calls=%async_computation.36 | async-start | bytes 2359296 | tf_op jit(solution)/shard_map/all_gather | solution.py:258
  46.0 271.0 %copy-start.134 = (f32[4,1,256]{2,1,0:T(1,128)}, f32[4,1,256]{2,1,0:T(1,128)S(1)}, u32[]{:S(2)}) copy-start(f32[4,1,256]{2,1,0:T(1,128)S(1)} %convert_element_type.934) | copy-start | bytes 12292
  56.3 260.7 %copy-start.125 = (f32[4,1,256]{2,1,0:T(1,128)}, f32[4,1,256]{2,1,0:T(1,128)S(1)}, u32[]{:S(2)}) copy-start(f32[4,1,256]{2,1,0:T(1,128)S(1)} %convert_element_type.933) | copy-start | bytes 12292
  56.5 110.6 %copy-start.191 = (f32[128]{0:T(128)}, f32[128]{0:T(128)S(1)}, u32[]{:S(2)}) copy-start(f32[128]{0:T(128)S(1)} %get-tuple-element.837) | copy-start | bytes 1540
  56.5 260.5 %copy-start.199 = (f32[128]{0:T(128)}, f32[128]{0:T(128)S(1)}, u32[]{:S(2)}) copy-start(f32[128]{0:T(128)S(1)} %get-tuple-element.836) | copy-start | bytes 1540
  57.3 109.7 %copy-start.205 = (f32[128]{0:T(128)}, f32[128]{0:T(128)S(1)}, u32[]{:S(2)}) copy-start(f32[128]{0:T(128)S(1)} %fusion.250) | copy-start | bytes 1540
  78.3 244.4 %copy-start.186 = (f32[4,1,256]{2,1,0:T(1,128)}, f32[4,1,256]{2,1,0:T(1,128)S(1)}, u32[]{:S(2)}) copy-start(f32[4,1,256]{2,1,0:T(1,128)S(1)} %convert_element_type.936) | copy-start | bytes 12292
  78.4 238.7 %copy-start.263 = (f32[128]{0:T(128)}, f32[128]{0:T(128)S(1)}, u32[]{:S(2)}) copy-start(f32[128]{0:T(128)S(1)} %fusion.256) | copy-start | bytes 1540
  167.1 149.7 %copy-start.50 = (f32[128,4096]{1,0:T(8,128)}, f32[128,4096]{1,0:T(8,128)S(1)}, u32[]{:S(2)}) copy-start(f32[128,4096]{1,0:T(8,128)S(1)} %convolution_add_fusion.3) | copy-start | bytes 6291460
  323.4 231.1 %copy-start.46 = (bf16[128,1024]{1,0:T(8,128)(2,1)}, bf16[128,1024]{1,0:T(8,128)(2,1)S(1)}, u32[]{:S(2)}) copy-start(bf16[128,1024]{1,0:T(8,128)(2,1)S(1)} %get-tuple-element.777) | copy-start | bytes 786436
  323.5 235.0 %copy-start.48 = (bf16[128,1024]{1,0:T(8,128)(2,1)}, bf16[128,1024]{1,0:T(8,128)(2,1)S(1)}, u32[]{:S(2)}) copy-start(bf16[128,1024]{1,0:T(8,128)(2,1)S(1)} %get-tuple-element.778) | copy-start | bytes 786436
  360.4 221.7 %all-gather.58.cloned.1.call-start = ((), (), s32[]{:S(2)}) async-start(), calls=%async_computation.37 | async-start | bytes 2359296 | tf_op jit(solution)/shard_map/all_gather | solution.py:257
  406.5 208.3 %all-gather.46.cloned.1.call-start = ((), (), s32[]{:S(2)}) async-start(), calls=%async_computation.19 | async-start | bytes 2621440 | tf_op jit(solution)/shard_map/all_gather | solution.py:77
  407.2 232.1 %all-gather.48.cloned.1.call-start = ((), (), s32[]{:S(2)}) async-start(), calls=%async_computation.20 | async-start | bytes 5242880 | tf_op jit(solution)/shard_map/all_gather | solution.py:82
  407.9 260.1 %all-gather.60.cloned.1.call-start = ((), (), s32[]{:S(2)}) async-start(), calls=%async_computation.38 | async-start | bytes 2359296 | tf_op jit(solution)/shard_map/all_gather | solution.py:258
  409.2 289.3 %all-gather.62.cloned.1.call-start = ((), (), s32[]{:S(2)}) async-start(), calls=%async_computation.39 | async-start | bytes 2359296 | tf_op jit(solution)/shard_map/all_gather | solution.py:257
  412.1 333.7 %all-gather.50.cloned.1.call-start = ((), (), s32[]{:S(2)}) async-start(), calls=%async_computation.21 | async-start | bytes 2621440 | tf_op jit(solution)/shard_map/all_gather | solution.py:86
  412.7 58.4 %copy-start.323 = (bf16[256]{0:T(256)(128)(2,1)S(1)}, bf16[256]{0:T(256)(128)(2,1)}, u32[]{:S(2)}) copy-start(bf16[256]{0:T(256)(128)(2,1)} %param.58) | copy-start | bytes 1540
  412.8 68.2 %copy-start.324 = (bf16[256]{0:T(256)(128)(2,1)S(1)}, bf16[256]{0:T(256)(128)(2,1)}, u32[]{:S(2)}) copy-start(bf16[256]{0:T(256)(128)(2,1)} %param.55) | copy-start | bytes 1540
  412.8 76.1 %copy-start.325 = (bf16[256]{0:T(256)(128)(2,1)S(1)}, bf16[256]{0:T(256)(128)(2,1)}, u32[]{:S(2)}) copy-start(bf16[256]{0:T(256)(128)(2,1)} %param.54) | copy-start | bytes 1540
  412.8 85.4 %copy-start.326 = (bf16[256]{0:T(256)(128)(2,1)S(1)}, bf16[256]{0:T(256)(128)(2,1)}, u32[]{:S(2)}) copy-start(bf16[256]{0:T(256)(128)(2,1)} %param.66) | copy-start | bytes 1540
  412.8 93.9 %copy-start.295 = (bf16[1024]{0:T(1024)(128)(2,1)S(1)}, bf16[1024]{0:T(1024)(128)(2,1)}, u32[]{:S(2)}) copy-start(bf16[1024]{0:T(1024)(128)(2,1)} %param.64) | copy-start | bytes 6148
  412.8 105.7 %copy-start.327 = (bf16[256]{0:T(256)(128)(2,1)S(1)}, bf16[256]{0:T(256)(128)(2,1)}, u32[]{:S(2)}) copy-start(bf16[256]{0:T(256)(128)(2,1)} %param.62) | copy-start | bytes 1540
  412.8 483.0 %all-gather.52.cloned.1.call-start = ((), (), s32[]{:S(2)}) async-start(), calls=%async_computation.22 | async-start | bytes 10485760 | tf_op jit(solution)/shard_map/all_gather | solution.py:89
  413.6 113.4 %copy-start.328 = (bf16[256]{0:T(256)(128)(2,1)S(1)}, bf16[256]{0:T(256)(128)(2,1)}, u32[]{:S(2)}) copy-start(bf16[256]{0:T(256)(128)(2,1)} %param.61) | copy-start | bytes 1540
  413.6 122.3 %copy-start.329 = (bf16[256]{0:T(256)(128)(2,1)S(1)}, bf16[256]{0:T(256)(128)(2,1)}, u32[]{:S(2)}) copy-start(bf16[256]{0:T(256)(128)(2,1)} %param.67) | copy-start | bytes 1540
  413.6 131.6 %copy-start.330 = (bf16[256]{0:T(256)(128)(2,1)S(1)}, bf16[256]{0:T(256)(128)(2,1)}, u32[]{:S(2)}) copy-start(bf16[256]{0:T(256)(128)(2,1)} %param.68) | copy-start | bytes 1540
  413.6 631.5 %all-gather.54.cloned.1.call-start = ((), (), s32[]{:S(2)}) async-start(), calls=%async_computation.23 | async-start | bytes 10485760 | tf_op jit(solution)/shard_map/all_gather | solution.py:91
  414.2 1009.9 %reduce-scatter.45.cloned.1.call-start = ((), (), s32[]{:S(2)}) async-start(), calls=%async_computation.41 | async-start | bytes 4718592
  448.5 106.1 %copy-start.195 = (f32[4,1,256]{2,1,0:T(1,128)}, f32[4,1,256]{2,1,0:T(1,128)S(1)}, u32[]{:S(2)}) copy-start(f32[4,1,256]{2,1,0:T(1,128)S(1)} %convert_element_type.939) | copy-start | bytes 12292
  461.6 98.2 %copy-start.145 = (bf16[73,64]{0,1:T(8,128)(2,1)}, bf16[73,64]{0,1:T(8,128)(2,1)S(1)}, u32[]{:S(2)}) copy-start(bf16[73,64]{0,1:T(8,128)(2,1)S(1)} %all_gather.85) | copy-start | bytes 28036
  488.9 230.5 %copy-start.147 = (f32[4,1,256]{2,1,0:T(1,128)}, f32[4,1,256]{2,1,0:T(1,128)S(1)}, u32[]{:S(2)}) copy-start(f32[4,1,256]{2,1,0:T(1,128)S(1)} %convert_element_type.942) | copy-start | bytes 12292
  527.0 529.3 %copy-start.136 = (f32[4,1,256]{2,1,0:T(1,128)}, f32[4,1,256]{2,1,0:T(1,128)S(1)}, u32[]{:S(2)}) copy-start(f32[4,1,256]{2,1,0:T(1,128)S(1)} %convert_element_type.946) | copy-start | bytes 12292
  617.0 128.8 %copy-start.20 = (f32[128,1024]{1,0:T(8,128)}, f32[128,1024]{1,0:T(8,128)S(1)}, u32[]{:S(2)}) copy-start(f32[128,1024]{1,0:T(8,128)S(1)} %get-tuple-element.808) | copy-start | bytes 1572868
  643.1 82.8 %collective-permute-start = (bf16[30,1,1024]{2,0,1:T(8,128)(2,1)}, bf16[30,1,1024]{2,0,1:T(8,128)(2,1)}, u32[]{:S(2)}, u32[]{:S(2)}) collective-permute-start(bf16[30,1,1024]{2,0,1:T(8,128)(2,1)} %fusion.236), channel_id=1, source_target_pairs={{0,4},{4,8},{8,12},{12,16},{16,20},{20,24},{24,28},{1,5},{5,9},{9,... | collective-permute-start | bytes 184328 | tf_op jit(solution)/shard_map/ppermute | solution.py:19
  723.1 328.0 %collective-permute-start.1 = (bf16[30,1,1024]{2,0,1:T(8,128)(2,1)S(1)}, bf16[30,1,1024]{2,0,1:T(8,128)(2,1)}, u32[]{:S(2)}, u32[]{:S(2)}) collective-permute-start(bf16[30,1,1024]{2,0,1:T(8,128)(2,1)S(1)} %fusion.237), channel_id=1, source_target_pairs={{0,4},{4,8},{8,12},{12,16},{16,20},{20,24},{24,28},{1,5},{5,9},{9,... | collective-permute-start | bytes 184328 | tf_op jit(solution)/shard_map/ppermute | solution.py:19
  748.3 153.7 %copy-start.201 = (f32[128]{0:T(128)}, f32[128]{0:T(128)S(1)}, u32[]{:S(2)}) copy-start(f32[128]{0:T(128)S(1)} %broadcast_multiply_fusion.69) | copy-start | bytes 1540
  749.3 146.5 %copy-start.310 = (f32[128]{0:T(128)}, f32[128]{0:T(128)S(1)}, u32[]{:S(2)}) copy-start(f32[128]{0:T(128)S(1)} %multiply_reduce_fusion.86) | copy-start | bytes 1540
  749.3 152.7 %copy-start.207 = (f32[128]{0:T(128)}, f32[128]{0:T(128)S(1)}, u32[]{:S(2)}) copy-start(f32[128]{0:T(128)S(1)} %fusion.254) | copy-start | bytes 1540
  895.8 149.3 %copy-start.37 = (f32[128,1024]{1,0:T(8,128)S(1)}, f32[128,1024]{1,0:T(8,128)}, u32[]{:S(2)}) copy-start(f32[128,1024]{1,0:T(8,128)} %copy-done.36) | copy-start | bytes 1572868
  895.8 149.3 %copy-start.287 = (f32[4,1,256]{2,1,0:T(1,128)S(1)}, f32[4,1,256]{2,1,0:T(1,128)}, u32[]{:S(2)}) copy-start(f32[4,1,256]{2,1,0:T(1,128)} %convert_element_type.947) | copy-start | bytes 12292
  1108.4 6.3 collective-permute-start.3
  1113.1 4.0 collective-permute-start.2
  1150.2 275.2 %reduce-scatter.43.cloned.1.call-start = ((), (), s32[]{:S(2)}) async-start(), calls=%async_computation.40 | async-start | bytes 4718592
  1184.0 370.1 %reduce-scatter.37.cloned.1.call-start = ((), (), s32[]{:S(2)}) async-start(), calls=%async_computation.33 | async-start | bytes 2621440 | tf_op jit(solution)/shard_map/reduce_scatter | solution.py:661
  1190.9 363.3 %reduce-scatter.23.cloned.1.call-start = ((), (), s32[]{:S(2)}) async-start(), calls=%async_computation.26 | async-start | bytes 2621440 | tf_op jit(solution)/shard_map/reduce_scatter | solution.py:619
  1413.2 141.0 %reduce-scatter.29.cloned.1.call-start = ((), (), s32[]{:S(2)}) async-start(), calls=%async_computation.29 | async-start | bytes 2621440 | tf_op jit(solution)/shard_map/reduce_scatter | solution.py:634
  1417.0 165.3 %reduce-scatter.33.cloned.1.call-start = ((), (), s32[]{:S(2)}) async-start(), calls=%async_computation.31 | async-start | bytes 5242880 | tf_op jit(solution)/shard_map/reduce_scatter | solution.py:649
  1424.0 205.6 %reduce-scatter.25.cloned.1.call-start = ((), (), s32[]{:S(2)}) async-start(), calls=%async_computation.27 | async-start | bytes 2621440 | tf_op jit(solution)/shard_map/reduce_scatter | solution.py:625
  1429.8 246.0 %reduce-scatter.27.cloned.1.call-start = ((), (), s32[]{:S(2)}) async-start(), calls=%async_computation.28 | async-start | bytes 2621440 | tf_op jit(solution)/shard_map/reduce_scatter | solution.py:628
  1432.7 389.2 %reduce-scatter.39.cloned.1.call-start = ((), (), s32[]{:S(2)}) async-start(), calls=%async_computation.34 | async-start | bytes 10485760 | tf_op jit(solution)/shard_map/reduce_scatter | solution.py:670
  1454.6 514.8 %reduce-scatter.41.cloned.1.call-start = ((), (), s32[]{:S(2)}) async-start(), calls=%async_computation.35 | async-start | bytes 10485760 | tf_op jit(solution)/shard_map/reduce_scatter | solution.py:676
  1476.1 640.8 %reduce-scatter.19.cloned.1.call-start = ((), (), s32[]{:S(2)}) async-start(), calls=%async_computation.24 | async-start | bytes 10485760 | tf_op jit(solution)/shard_map/reduce_scatter | solution.py:601
  1523.2 741.2 %reduce-scatter.21.cloned.1.call-start = ((), (), s32[]{:S(2)}) async-start(), calls=%async_computation.25 | async-start | bytes 10485760 | tf_op jit(solution)/shard_map/reduce_scatter | solution.py:607
  1542.1 761.3 %reduce-scatter.31.cloned.1.call-start = ((), (), s32[]{:S(2)}) async-start(), calls=%async_computation.30 | async-start | bytes 20480 | tf_op jit(solution)/shard_map/reduce_scatter | solution.py:640
  1553.0 753.3 %reduce-scatter.35.cloned.1.call-start = ((), (), s32[]{:S(2)}) async-start(), calls=%async_computation.32 | async-start | bytes 81920 | tf_op jit(solution)/shard_map/reduce_scatter | solution.py:652
  1553.8 926.9 %all-reduce.92.cloned.1.call-start = ((), (), s32[]{:S(2)}) async-start(), calls=%async_computation.42 | async-start | bytes 24117248 | tf_op jit(solution)/shard_map/psum | solution.py:692
  (346 other events, 2166.2 us)
Sparse Core Ops, SparseCore 0:
  9.6 152.6 all-gather.35
  163.9 147.8 all-gather.37
  313.4 44.1 all-gather.39
  359.0 44.6 all-gather.43
  405.1 45.7 all-gather.41
  453.3 26.7 all-gather.55
  482.6 27.8 all-gather.57
  512.0 46.2 all-gather.45
  559.9 79.3 all-gather.47
  641.6 26.4 all-gather.59
  670.5 27.8 all-gather.61
  699.9 45.9 all-gather.49
  747.4 148.3 all-gather.51
  897.2 147.8 all-gather.53
  1150.3 52.1 reduce-scatter.44
  1206.6 51.3 reduce-scatter.42
  1260.2 43.8 reduce-scatter.36
  1413.3 44.5 reduce-scatter.22
  1460.1 43.1 reduce-scatter.28
  1506.2 76.0 reduce-scatter.32
  1585.2 44.3 reduce-scatter.24
  1632.5 43.1 reduce-scatter.26
  1678.1 143.7 reduce-scatter.38
  1824.2 145.1 reduce-scatter.40
  1971.7 145.1 reduce-scatter.18
  2119.2 145.1 reduce-scatter.20
  2266.5 19.6 reduce-scatter.30
  2289.1 17.1 reduce-scatter.34
  2311.8 168.7 all-reduce.91
where the time goes:
time: 2520 us; the launch traced here: 2510 us
  waiting for transfers between devices  1530 us (61%)
  matrix products  401 us (16%)
  blocking collectives  255 us (10%)
  local copies, waits for them, and re-layouts  162 us (6%)
  other arithmetic  126 us (5%)
    reduce_scatter x1, waiting for transfers between devices, on_device(): lax.psum_scatter(sectioned[2].astype(jnp.bfloat16), 'shard', scatter_dime...  148 us
    reduce_scatter x1, waiting for transfers between devices, on_device(): lax.psum_scatter(sectioned[27].astype(jnp.bfloat16), 'shard', scatter_dim...  147 us
    reduce_scatter x1, waiting for transfers between devices, on_device(): lax.psum_scatter(sectioned[4].astype(jnp.bfloat16), 'shard', scatter_dime...  147 us
    all_gather x1, waiting for transfers between devices, fetch_weights(): lax.all_gather(shards[25], 'shard', axis=0, tiled=True)  146 us
    reduce_scatter x1, waiting for transfers between devices, on_device(): lax.psum_scatter(sectioned[25].astype(jnp.bfloat16), 'shard', scatter_dim...  146 us
    all_gather x1, waiting for transfers between devices, fetch_weights(): lax.all_gather(shards[4], 'shard', axis=0, tiled=True)  145 us
    all_gather x1, waiting for transfers between devices, fetch_weights(): lax.all_gather(shards[27], 'shard', axis=0, tiled=True)  143 us
    psum x1, waiting for transfers between devices, on_device(): lax.psum(shares[2].astype(jnp.bfloat16), 'rep').astype(jnp.float32)  139 us
  transfers between devices with their start and end apart: 33, of which 20 were waited for; matrix products, arithmetic and copies ran while one was open for 22% of the time, Pallas kernels for 0%

commit v1 on v0

v1 whole, which is shorter than its diff:
```python
import functools

import jax
import jax.numpy as jnp
from jax import lax
from jax.experimental import pallas as pl
from jax.experimental.pallas import tpu as pltpu
from jax.sharding import PartitionSpec as P

H = 16
HD = 64
LEFT = 64
RIGHT = 8
TABLE = 73
EPSILON = 1e-05
BAND = 512
MESH = pl.DeviceIdType.MESH
BF = jnp.bfloat16
F32 = jnp.float32
ANY = pl.BlockSpec(memory_space=pl.ANY)
VM = pl.BlockSpec(memory_space=pltpu.VMEM)


def here():
    rep = lax.axis_index("rep")
    z = lax.axis_index("shard")
    core = lax.rem(rep, 2)
    x = lax.rem(rep // 2, 2)
    y = rep // 4
    z0 = lax.rem(z, 2)
    z1 = z // 2
    peers = {
        "z1": (rep, lax.rem(z + 2, 4)),
        "z0": (rep, z + 1 - 2 * z0),
        "zz": (rep, 3 - z),
        "x": (rep + 2 - 4 * x, z),
        "y": (rep + 4 - 8 * y, z),
        "c": (rep + 1 - 2 * core, z),
    }
    return z, core, x, y, z0, z1, peers


def meet(peers):
    barrier = pltpu.get_barrier_semaphore()
    for name in peers:
        pl.semaphore_signal(barrier, inc=1, device_id=peers[name], device_id_type=MESH)
    pl.semaphore_wait(barrier, len(peers))


GATHER_LAG = (0, 2, 3, 4, 5)


def gather_kernel(chunks, n_arr, *refs):
    ins, small = (refs[:n_arr], refs[n_arr])
    outs, small_out = (refs[n_arr + 1 : 2 * n_arr + 1], refs[2 * n_arr + 1])
    ssem, rsem, lsem, lsem2, qsem, psem = refs[2 * n_arr + 2 : 2 * n_arr + 8]
    bufs = refs[2 * n_arr + 8 :]
    z, core, x, y, z0, z1, peers = here()
    far = ((slice(None), 1 - z0), (1 - z1, z0))
    meet(peers)
    sent = []

    def send(c, slot, src, dst, to):
        copy = pltpu.make_async_remote_copy(
            src_ref=src,
            dst_ref=dst,
            send_sem=ssem.at[c, slot],
            recv_sem=rsem.at[c, slot],
            device_id=peers[to],
            device_id_type=MESH,
        )
        copy.start()
        sent.append(copy)
        return copy

    smalls = []
    for k, to in enumerate(("z0", "z1", "zz")):
        copy = pltpu.make_async_remote_copy(
            src_ref=small,
            dst_ref=small_out.at[z],
            send_sem=qsem.at[k],
            recv_sem=psem.at[k],
            device_id=peers[to],
            device_id_type=MESH,
        )
        copy.start()
        smalls.append(copy)
    small_own = pltpu.make_async_copy(small, small_out.at[z], lsem.at[n_arr])
    small_own.start()
    state = {}

    def place(c):
        array, first, count = chunks[c]
        return (ins[array], outs[array], pl.ds(first, count))

    def wait(c, key):
        for copy in state[c, key]:
            copy.wait_recv()

    def stage_z(c):
        src, out, cols = place(c)
        src = src.at[y, x, core, :, :, cols]
        dst = out.at[z1, z0, y, x, core, :, :, cols]
        state[c, "z1"] = [send(c, 0, src, dst, "z1")]
        state[c, "z0"] = [send(c, 1, src, dst, "z0")]

    def stage_zz(c):
        _, out, cols = place(c)
        wait(c, "z1")
        view = out.at[1 - z1, z0, y, x, core, :, :, cols]
        state[c, "z0"].append(send(c, 2, view, view, "z0"))

    def stage_one(c):
        _, out, cols = place(c)
        wait(c, "z0")
        state[c, "one"] = []
        for i, (a, b) in enumerate(far):
            view = out.at[a, b, y, x, core, 0, :, cols]
            state[c, "one"].append(send(c, 3 + i, view, view, "x"))
            view = out.at[a, b, y, x, core, 1, :, cols]
            state[c, "one"].append(send(c, 5 + i, view, view, "y"))

    def stage_two(c):
        _, out, cols = place(c)
        wait(c, "one")
        state[c, "two"] = []
        for i, (a, b) in enumerate(far):
            view = out.at[a, b, y, :, core, 0, :, cols]
            state[c, "two"].append(send(c, 7 + i, view, view, "y"))
            view = out.at[a, b, :, x, core, 1, :, cols]
            state[c, "two"].append(send(c, 9 + i, view, view, "x"))

    def stage_core(c):
        _, out, cols = place(c)
        wait(c, "two")
        state[c, "core"] = []
        for i, (a, b) in enumerate(far):
            view = out.at[a, b, :, :, core, :, :, cols]
            state[c, "core"].append(send(c, 11 + i, view, view, "c"))

    stages = (stage_z, stage_zz, stage_one, stage_two, stage_core)
    local = []
    for step in range(len(chunks) + GATHER_LAG[-1]):
        for stage, lag in zip(stages, GATHER_LAG):
            if 0 <= step - lag < len(chunks):
                stage(step - lag)
        if step == 0:
            for a in range(n_arr):
                copy = pltpu.make_async_copy(ins[a], bufs[a], lsem.at[a])
                copy.start()
                local.append(copy)
        if step == 3:
            for a in range(n_arr):
                local[a].wait()
                copy = pltpu.make_async_copy(bufs[a], outs[a].at[z1, z0], lsem2.at[a])
                copy.start()
                local[a] = copy
    for c in range(len(chunks)):
        wait(c, "core")
    for copy in sent + smalls:
        copy.wait_send()
    for copy in smalls:
        copy.wait_recv()
    small_own.wait()
    for copy in local:
        copy.wait()


def gather_chunks(shapes):
    chunks = []
    for i, (rows, cols) in enumerate(shapes):
        for first in range(0, cols, 1024 * 256 // rows):
            chunks.append((i, first, 1024 * 256 // rows))
    return chunks


def gather_fast(shards, small):
    count = len(shards)
    ins = [w.reshape(2, 2, 2, 2, w.shape[0] // 16, w.shape[1]) for w in shards]
    chunks = gather_chunks([w.shape for w in shards])
    outs = [jax.ShapeDtypeStruct((2, 2) + w.shape, w.dtype) for w in ins]
    outs.append(jax.ShapeDtypeStruct((4,) + small.shape, small.dtype))
    dma = pltpu.SemaphoreType.DMA
    found = pl.pallas_call(
        functools.partial(gather_kernel, chunks, count),
        out_shape=outs,
        in_specs=[ANY] * (count + 1),
        out_specs=[ANY] * (count + 1),
        scratch_shapes=[
            dma((len(chunks), 13)),
            dma((len(chunks), 13)),
            dma((count + 1,)),
            dma((count,)),
            dma((3,)),
            dma((3,)),
        ]
        + [pltpu.VMEM(w.shape, w.dtype) for w in ins],
        compiler_params=pltpu.CompilerParams(
            collective_id=0, has_side_effects=True, vmem_limit_bytes=32 << 20
        ),
        name="gather_weights",
    )(*ins, small)
    return [w.reshape(-1, w.shape[-1]) for w in found[:count]], found[count]


REDUCE_LAG = (0, 1, 2, 3, 4, 5, 6, 7)


def reduce_kernel(groups, units, n_left, n_right, *refs):
    lefts, rights = (refs[:n_left], refs[n_left : n_left + n_right])
    out = refs[n_left + n_right]
    lbuf, rbuf, sbuf, b1, b2, b3, b4, b5, lsem, ssem, rsem, osem = refs[n_left + n_right + 1 :]
    z, core, x, y, z0, z1, peers = here()
    del peers["zz"]
    meet(peers)

    def remote(u, slot, src, dst, to):
        return pltpu.make_async_remote_copy(
            src_ref=src,
            dst_ref=dst,
            send_sem=ssem.at[u, slot],
            recv_sem=rsem.at[u, slot],
            device_id=peers[to],
            device_id_type=MESH,
        )

    def copy_core(u):
        return [remote(u, 0, sbuf.at[lax.rem(u, 2)], b1.at[u], "c")]

    def copy_first(u):
        return [
            remote(u, 1, b1.at[u, :, :, 0, 1 - x], b2.at[u, 0], "x"),
            remote(u, 2, b1.at[u, :, :, 1, 1 - y], b2.at[u, 1], "y"),
        ]

    def copy_z0(u):
        return [remote(u, 3, b2.at[u, :, :, 1 - z0], b3.at[u], "z0")]

    def copy_z1(u):
        return [remote(u, 4, b3.at[u, :, 1 - z1], b4.at[u], "z1")]

    def copy_second(u):
        return [
            remote(u, 5, b4.at[u, 0, 1 - y], b5.at[u, 0], "y"),
            remote(u, 6, b4.at[u, 1, 1 - x], b5.at[u, 1], "x"),
        ]

    def copy_own(u):
        return [
            pltpu.make_async_copy(b5.at[u, 0], out.at[u, core, 0, x, y], osem.at[u, 0]),
            pltpu.make_async_copy(b5.at[u, 1], out.at[u, core, 1, y, x], osem.at[u, 1]),
        ]

    def spread_second(u):
        return [
            remote(u, 7, b5.at[u, 0], out.at[u, core, 0, x, y], "y"),
            remote(u, 8, b5.at[u, 1], out.at[u, core, 1, y, x], "x"),
        ]

    def spread_first(u):
        return [
            remote(u, 9, out.at[u, core, 0, x], out.at[u, core, 0, x], "x"),
            remote(u, 10, out.at[u, core, 1, y], out.at[u, core, 1, y], "y"),
        ]

    def spread_core(u):
        return [remote(u, 11, out.at[u, core], out.at[u, core], "c")]

    def start(copies):
        for copy in copies:
            copy.start()

    def arrive(copies):
        for copy in copies:
            copy.wait_recv()

    def load(u):
        slot = lax.rem(u, 3)
        for li, ri, first, count, by_rows in groups:

            @pl.when(jnp.logical_and(u >= first, u < first + count))
            def _():
                k = u - first
                for part in range(4):
                    at = pl.multiple_of(part * 1024 + k * 256, 256) if by_rows else part * 256
                    pltpu.make_async_copy(
                        lefts[li].at[:, pl.ds(at, 256)], lbuf.at[slot, part], lsem.at[slot, part]
                    ).start()
                at = 0 if by_rows else pl.multiple_of(k * 1024, 1024)
                pltpu.make_async_copy(
                    rights[ri].at[:, pl.ds(at, 1024)], rbuf.at[slot], lsem.at[slot, 4]
                ).start()

    def product(u, part, half):
        slot = lax.rem(u, 3)
        left = lbuf[slot, part, :, pl.ds(pl.multiple_of(half * 128, 128), 128)]
        return lax.dot_general(
            left, rbuf[slot], (((0,), (0,)), ((), ())), preferred_element_type=F32
        ).reshape(2, 2, 2, 16, 1024)

    load(0)
    load(1)

    def stage_multiply(u):
        slot = lax.rem(u, 3)
        for part in range(4):
            pltpu.make_async_copy(
                lefts[0].at[:, pl.ds(0, 256)], lbuf.at[slot, part], lsem.at[slot, part]
            ).wait()
        pltpu.make_async_copy(
            rights[0].at[:, pl.ds(0, 1024)], rbuf.at[slot], lsem.at[slot, 4]
        ).wait()

        @pl.when(u >= 2)
        def _():
            for copy in copy_core(u - 2):
                copy.wait_send()

        def body(part, carry):
            sbuf[lax.rem(u, 2), part // 2, lax.rem(part, 2)] = product(u, part, 1 - core).astype(BF)
            return carry

        lax.fori_loop(0, 4, body, 0)
        start(copy_core(u))

    def stage_own(u):
        arrive(copy_core(u))

        def body(part, carry):
            a, b = (part // 2, lax.rem(part, 2))
            b1[u, a, b] = (product(u, part, core) + b1[u, a, b].astype(F32)).astype(BF)
            return carry

        lax.fori_loop(0, 4, body, 0)
        start(copy_first(u))

        @pl.when(u + 2 < units)
        def _():
            load(u + 2)

    def stage_first(u):
        arrive(copy_first(u))

        def body(part, carry):
            a, b = (part // 2, lax.rem(part, 2))
            for half, bit in ((0, x), (1, y)):
                b2[u, half, a, b] = (
                    b2[u, half, a, b].astype(F32) + b1[u, a, b, half, bit].astype(F32)
                ).astype(BF)
            return carry

        lax.fori_loop(0, 4, body, 0)
        start(copy_z0(u))

    def stage_z0(u):
        arrive(copy_z0(u))
        for half in range(2):
            for a in range(2):
                b3[u, half, a] = (
                    b3[u, half, a].astype(F32) + b2[u, half, a, z0].astype(F32)
                ).astype(BF)
        start(copy_z1(u))

    def stage_z1(u):
        arrive(copy_z1(u))
        for half in range(2):
            b4[u, half] = (b4[u, half].astype(F32) + b3[u, half, z1].astype(F32)).astype(BF)
        start(copy_second(u))

    def stage_second(u):
        arrive(copy_second(u))
        for half, bit in ((0, y), (1, x)):
            b5[u, half] = (b5[u, half].astype(F32) + b4[u, half, bit].astype(F32)).astype(BF)
        start(copy_own(u))
        start(spread_second(u))

    def stage_spread(u):
        arrive(spread_second(u))
        for copy in copy_own(u):
            copy.wait()
        start(spread_first(u))

    def stage_core(u):
        arrive(spread_first(u))
        start(spread_core(u))

    stages = (
        stage_multiply,
        stage_own,
        stage_first,
        stage_z0,
        stage_z1,
        stage_second,
        stage_spread,
        stage_core,
    )

    def step(i, carry):
        for stage, lag in zip(stages, REDUCE_LAG):
            u = i - lag

            @pl.when(jnp.logical_and(u >= 0, u < units))
            def _():
                stage(u)

        return carry

    lax.fori_loop(0, units + REDUCE_LAG[-1], step, 0)

    def finish(u, carry):
        arrive(spread_core(u))
        for copies in (
            copy_first,
            copy_z0,
            copy_z1,
            copy_second,
            spread_second,
            spread_first,
            spread_core,
        ):
            for copy in copies(u):
                copy.wait_send()

        @pl.when(u >= units - 2)
        def _():
            for copy in copy_core(u):
                copy.wait_send()

        return carry

    lax.fori_loop(0, units, finish, 0)


def reduce_fast(pairs):
    lefts, rights, groups, units = ([], [], [], 0)

    def index_of(arrays, array):
        for i, known in enumerate(arrays):
            if known is array:
                return i
        arrays.append(array)
        return len(arrays) - 1

    for left, right in pairs:
        by_rows = left.shape[1] > 1024
        count = left.shape[1] // 1024 if by_rows else right.shape[1] // 1024
        groups.append((index_of(lefts, left), index_of(rights, right), units, count, by_rows))
        units += count
    dma = pltpu.SemaphoreType.DMA
    found = pl.pallas_call(
        functools.partial(reduce_kernel, groups, units, len(lefts), len(rights)),
        out_shape=jax.ShapeDtypeStruct((units, 2, 2, 2, 2, 16, 1024), BF),
        in_specs=[ANY] * (len(lefts) + len(rights)),
        out_specs=ANY,
        scratch_shapes=[
            pltpu.VMEM((3, 4, 256, 256), BF),
            pltpu.VMEM((3, 256, 1024), BF),
            pltpu.VMEM((2, 2, 2, 2, 2, 2, 16, 1024), BF),
            pltpu.VMEM((units, 2, 2, 2, 2, 2, 16, 1024), BF),
            pltpu.VMEM((units, 2, 2, 2, 2, 16, 1024), BF),
            pltpu.VMEM((units, 2, 2, 2, 16, 1024), BF),
            pltpu.VMEM((units, 2, 2, 16, 1024), BF),
            pltpu.VMEM((units, 2, 16, 1024), BF),
            dma((3, 5)),
            dma((units, 12)),
            dma((units, 12)),
            dma((units, 2)),
        ],
        compiler_params=pltpu.CompilerParams(
            collective_id=1, has_side_effects=True, vmem_limit_bytes=60 << 20
        ),
        name="reduce_grads",
    )(*lefts, *rights)
    found = found.reshape(units, 256, 1024)
    grads = []
    for li, ri, first, count, by_rows in groups:
        part = found[first : first + count]
        if not by_rows:
            part = jnp.transpose(part, (1, 0, 2))
        grads.append(part.reshape((count * 256, 1024) if by_rows else (256, -1)).astype(F32))
    return grads


def reduce_plain(pairs):
    grads = []
    for left, right in pairs:
        full = lax.dot_general(left, right, (((0,), (0,)), ((), ())), preferred_element_type=F32)
        part = lax.psum_scatter(full.astype(BF), "shard", scatter_dimension=0, tiled=True)
        grads.append(lax.psum(part, "rep").astype(F32))
    return grads


def swap_kernel(n, x_ref, o_ref, ssem, rsem):
    rep = lax.axis_index("rep")
    barrier = pltpu.get_barrier_semaphore()
    for d in range(1, n):
        pl.semaphore_signal(
            barrier, inc=1, device_id={"rep": jnp.bitwise_xor(rep, d)}, device_id_type=MESH
        )
    pl.semaphore_wait(barrier, n - 1)
    copies = []
    for d in range(1, n):
        other = jnp.bitwise_xor(rep, d)
        copy = pltpu.make_async_remote_copy(
            src_ref=x_ref.at[other],
            dst_ref=o_ref.at[rep],
            send_sem=ssem.at[d],
            recv_sem=rsem.at[d],
            device_id={"rep": other},
            device_id_type=MESH,
        )
        copy.start()
        copies.append(copy)
    o_ref[rep] = x_ref[rep]
    for copy in copies:
        copy.wait()


def swap(array, which):
    n = array.shape[0]
    return pl.pallas_call(
        functools.partial(swap_kernel, n),
        out_shape=jax.ShapeDtypeStruct(array.shape, array.dtype),
        in_specs=[VM],
        out_specs=VM,
        scratch_shapes=[pltpu.SemaphoreType.DMA((n,)), pltpu.SemaphoreType.DMA((n,))],
        compiler_params=pltpu.CompilerParams(
            collective_id=2 + which, has_side_effects=True, vmem_limit_bytes=32 << 20
        ),
        name="swap_%d" % which,
    )(array)


def to_heads(arrays, n):
    batch, local, features = arrays[0].shape
    parts = [a.reshape(batch, local, n, features // n) for a in arrays]
    stacked = jnp.stack([jnp.transpose(p, (2, 0, 1, 3)) for p in parts], axis=1)
    return stacked


def from_positions(swapped):
    n, k, batch, local, width = swapped.shape
    return [
        jnp.transpose(swapped[:, i], (1, 0, 2, 3)).reshape(batch, n * local, width)
        for i in range(k)
    ]


def to_positions(arrays, n):
    batch, total, width = arrays[0].shape
    parts = [
        jnp.transpose(a.reshape(batch, n, total // n, width), (1, 0, 2, 3)) for a in arrays
    ]
    return jnp.stack(parts, axis=1)


def from_heads(swapped):
    n, k, batch, local, width = swapped.shape
    return [
        jnp.transpose(swapped[:, i], (1, 2, 0, 3)).reshape(batch * local, n * width)
        for i in range(k)
    ]


QROWS = 256


def head_mask(shape, head):
    lane = lax.broadcasted_iota(jnp.int32, shape, 1)
    return jnp.logical_and(lane >= head * HD, lane < (head + 1) * HD)


def spread_bias(bias, spread, block):
    wide = bias.shape[1]
    lane = lax.broadcasted_iota(jnp.int32, (128, wide), 1)
    bias[...] = jnp.where(lane < (block + 1) * 128, spread[:, 0:1], spread[:, 383:384])
    rolled = pltpu.roll(spread, 0, 1, stride=1, stride_axis=0)
    bias[:, pl.ds(pl.multiple_of(block * 128, 128), 384)] = rolled[:, 0:384]


def forward_kernel(q_ref, k_ref, v_ref, table_ref, mixed_ref, lse_ref, bias):
    step = pl.program_id(1)
    total, width = (k_ref.shape[1], k_ref.shape[2])
    heads = width // HD
    keys = k_ref[0]
    values = v_ref[0]
    ones = jnp.ones((total, 128), BF)
    wide_values = jnp.concatenate([values, ones], axis=1) if width == 128 else None
    for sub in range(QROWS // 128):
        rows = slice(sub * 128, (sub + 1) * 128)
        query = q_ref[0, rows, :] * jnp.asarray(0.125, BF)
        block = step * (QROWS // 128) + sub
        for head in range(heads):
            mask = head_mask((128, width), head)
            part = jnp.where(mask, query, jnp.zeros_like(query))
            spread = lax.dot_general(
                part, table_ref[...], (((1,), (1,)), ((), ())), preferred_element_type=F32
            )
            spread_bias(bias, spread.astype(BF).astype(F32), block)
            scores = lax.dot_general(
                part, keys, (((1,), (1,)), ((), ())), preferred_element_type=F32
            )
            scores = scores + bias[:, 128 : 128 + total]
            top = jnp.max(scores, axis=1, keepdims=True)
            weight = jnp.exp(scores - top)
            summed = jnp.sum(weight, axis=1, keepdims=True)
            mixed = jnp.dot(weight.astype(BF), values, preferred_element_type=F32) / summed
            logsum = jnp.broadcast_to(top + jnp.log(summed), (128, width))
            if head == 0:
                mixed_ref[0, rows, :] = mixed
                lse_ref[0, rows, :] = logsum
            else:
                mixed_ref[0, rows, :] = jnp.where(mask, mixed, mixed_ref[0, rows, :])
                lse_ref[0, rows, :] = jnp.where(mask, logsum, lse_ref[0, rows, :])


def attention_forward(query, keys, values, table):
    batch, total, width = query.shape
    part = pl.BlockSpec((1, QROWS, width), lambda b, i: (b, i, 0))
    whole = pl.BlockSpec((1, total, width), lambda b, i: (b, 0, 0))
    shape = jax.ShapeDtypeStruct((batch, total, width), F32)
    return pl.pallas_call(
        forward_kernel,
        out_shape=[shape, shape],
        grid=(batch, total // QROWS),
        in_specs=[part, whole, whole, pl.BlockSpec(table.shape, lambda b, i: (0, 0))],
        out_specs=[part, part],
        scratch_shapes=[pltpu.VMEM((128, total + 256), F32)],
        compiler_params=pltpu.CompilerParams(vmem_limit_bytes=32 << 20),
        name="attention_forward",
    )(query, keys, values, table)


def backward_kernel(
    q_ref,
    k_ref,
    v_ref,
    table_ref,
    mixed_ref,
    lse_ref,
    g_ref,
    dq_ref,
    dk_ref,
    dv_ref,
    dtable_ref,
    bias,
    keyx,
    dscore,
    prob,
    dkt,
    dvt,
):
    batch_at, step = (pl.program_id(0), pl.program_id(1))
    total, width = (k_ref.shape[1], k_ref.shape[2])
    heads = width // HD

    @pl.when(jnp.logical_and(batch_at == 0, step == 0))
    def _():
        dtable_ref[...] = jnp.zeros_like(dtable_ref)

    @pl.when(step == 0)
    def _():
        dkt[...] = jnp.zeros_like(dkt)
        dvt[...] = jnp.zeros_like(dvt)
        keyx[:, 0:width] = k_ref[0]
        row = lax.broadcasted_iota(jnp.int32, (total, 128), 0) // 128
        lane = lax.broadcasted_iota(jnp.int32, (total, 128), 1)
        keyx[:, width : width + 128] = (row == lane).astype(BF)
        dscore[:, 0:128] = jnp.zeros((128, 128), BF)
        dscore[:, 128 + total : 256 + total] = jnp.zeros((128, 128), BF)

    keys = k_ref[0]
    values = v_ref[0]
    flip = (
        lax.broadcasted_iota(jnp.int32, (128, 128), 0)
        + lax.broadcasted_iota(jnp.int32, (128, 128), 1)
        == 127
    ).astype(BF)
    lane_at = lax.broadcasted_iota(jnp.int32, (128, 128), 1)
    band_at = lax.broadcasted_iota(jnp.int32, (128, BAND), 1)
    for sub in range(QROWS // 128):
        rows = slice(sub * 128, (sub + 1) * 128)
        block = step * (QROWS // 128) + sub
        query = q_ref[0, rows, :] * jnp.asarray(0.125, BF)
        grad = g_ref[0, rows, :]
        weighed = grad.astype(F32) * mixed_ref[0, rows, :]
        query_t = jnp.transpose(query.astype(F32)).astype(BF)
        grad_t = jnp.transpose(grad.astype(F32)).astype(BF)
        for head in range(heads):
            mask = head_mask((128, width), head)
            lanes = slice(head * HD, (head + 1) * HD)
            part = jnp.where(mask, query, jnp.zeros_like(query))
            grad_part = jnp.where(mask, grad, jnp.zeros_like(grad))
            balance = jnp.sum(jnp.where(mask, weighed, 0.0), axis=1, keepdims=True)
            logsum = lse_ref[0, rows, head * HD : head * HD + 1]
            spread = lax.dot_general(
                part, table_ref[...], (((1,), (1,)), ((), ())), preferred_element_type=F32
            )
            spread_bias(bias, spread.astype(BF).astype(F32), block)
            scores = lax.dot_general(
                part, keys, (((1,), (1,)), ((), ())), preferred_element_type=F32
            )
            chance = jnp.exp(scores + bias[:, 128 : 128 + total] - logsum)
            back = lax.dot_general(
                grad_part, values, (((1,), (1,)), ((), ())), preferred_element_type=F32
            )
            prob[...] = chance.astype(BF)
            dscore[:, 128 : 128 + total] = (chance * (back - balance)).astype(BF)
            score_back = dscore[:, 128 : 128 + total]
            dkt[lanes, :] += jnp.dot(query_t[lanes, :], score_back, preferred_element_type=F32)
            dvt[lanes, :] += jnp.dot(grad_t[lanes, :], prob[...], preferred_element_type=F32)
            wide = jnp.dot(score_back, keyx[...], preferred_element_type=F32)
            sums = wide[:, width : width + 128]
            before = jnp.sum(jnp.where(lane_at < block - 1, sums, 0.0), axis=1, keepdims=True)
            after = jnp.sum(jnp.where(lane_at > block + 1, sums, 0.0), axis=1, keepdims=True)
            near = dscore[:, pl.ds(pl.multiple_of(block * 128, 128), 384)]
            near = jnp.dot(flip, near, preferred_element_type=F32)
            near = jnp.concatenate([near, jnp.zeros((128, BAND - 384), F32)], axis=1)
            near = pltpu.roll(near, BAND - 127, 1, stride=1, stride_axis=0)
            near = jnp.dot(flip, near.astype(BF), preferred_element_type=F32)
            near = near + jnp.where(band_at == 0, before, 0.0)
            near = (near + jnp.where(band_at == 383, after, 0.0)).astype(BF)
            query_back = wide[:, 0:width] + jnp.dot(
                near, table_ref[...], preferred_element_type=F32
            )
            dtable_ref[...] += lax.dot_general(
                near, part, (((0,), (0,)), ((), ())), preferred_element_type=F32
            )
            query_back = (query_back * 0.125).astype(BF)
            if head == 0:
                dq_ref[0, rows, :] = query_back
            else:
                dq_ref[0, rows, :] = jnp.where(mask, query_back, dq_ref[0, rows, :])

    @pl.when(step == pl.num_programs(1) - 1)
    def _():
        dk_ref[0] = jnp.transpose(dkt[...]).astype(BF)
        dv_ref[0] = jnp.transpose(dvt[...]).astype(BF)


def attention_backward(query, keys, values, table, mixed, logsum, grad):
    batch, total, width = query.shape
    part = pl.BlockSpec((1, QROWS, width), lambda b, i: (b, i, 0))
    whole = pl.BlockSpec((1, total, width), lambda b, i: (b, 0, 0))
    fixed = pl.BlockSpec(table.shape, lambda b, i: (0, 0))
    shape = jax.ShapeDtypeStruct((batch, total, width), BF)
    return pl.pallas_call(
        backward_kernel,
        out_shape=[shape, shape, shape, jax.ShapeDtypeStruct(table.shape, F32)],
        grid=(batch, total // QROWS),
        in_specs=[part, whole, whole, fixed, part, part, part],
        out_specs=[part, whole, whole, fixed],
        scratch_shapes=[
            pltpu.VMEM((128, total + 256), F32),
            pltpu.VMEM((total, width + 128), BF),
            pltpu.VMEM((128, total + 256), BF),
            pltpu.VMEM((128, total), BF),
            pltpu.VMEM((width, total), F32),
            pltpu.VMEM((width, total), F32),
        ],
        compiler_params=pltpu.CompilerParams(vmem_limit_bytes=40 << 20),
        name="attention_backward",
    )(query, keys, values, table, mixed, logsum, grad)


def shifted(value, axis, steps):
    count = lax.axis_size(axis)
    leading, last = (max(0, -steps), min(count, count - steps))
    return lax.ppermute(value, axis, [(source, source + steps) for source in range(leading, last)])


def statistics(values):
    centre = jnp.mean(values, axis=-1, keepdims=True)
    centred = values - centre
    spread = jnp.mean(centred * centred, axis=-1, keepdims=True)
    return centre, lax.rsqrt(spread + EPSILON)


def norm(values, gain, shift):
    centre, scale = statistics(values)
    return (values - centre) * scale * gain + shift


def norm_back(values, gain, grad):
    centre, scale = statistics(values)
    hat = (values - centre) * scale
    weighed = grad * gain
    back = (
        weighed
        - jnp.mean(weighed, axis=-1, keepdims=True)
        - hat * jnp.mean(weighed * hat, axis=-1, keepdims=True)
    ) * scale
    return back, jnp.sum(grad * hat, axis=0), jnp.sum(grad, axis=0)


def swish(values):
    return values * jax.nn.sigmoid(values)


def swish_slope(values):
    gate = jax.nn.sigmoid(values)
    return gate * (1.0 + values * (1.0 - gate))


def times(left, right):
    return jnp.dot(left, right, preferred_element_type=F32)


def times_back(left, right):
    return lax.dot_general(left, right, (((1,), (1,)), ((), ())), preferred_element_type=F32)


def column_sum(values):
    return jnp.sum(values.astype(F32), axis=0)


MATRICES = (2, 4, 8, 10, 11, 13, 18, 22, 25, 27)
VECTORS = (0, 1, 5, 6, 7, 9, 12, 14, 16, 17, 20, 21, 23, 24, 28, 29, 30)
OFFSETS = (3, 26)
TABLE_AT = 15
TAPS_AT = 19


def pack_small(shards):
    width = shards[0].shape[0]
    rows = [shards[i].reshape(1, width) for i in VECTORS]
    rows += [shards[i].reshape(-1, width) for i in OFFSETS]
    rows.append(shards[TAPS_AT])
    table = shards[TABLE_AT].reshape(-1)
    spare = -table.shape[0] % width
    rows.append(jnp.pad(table, (0, spare)).reshape(-1, width))
    count = sum(r.shape[0] for r in rows)
    rows.append(jnp.zeros((-count % 16, width), rows[0].dtype))
    return jnp.concatenate(rows, axis=0)


def unpack_small(gathered, shards):
    n, _, width = gathered.shape
    full = {}
    at = 0
    for i in VECTORS:
        full[i] = gathered[:, at].reshape(n * width).astype(F32)
        at += 1
    for i in OFFSETS:
        count = shards[i].shape[0] // width
        full[i] = gathered[:, at : at + count].reshape(n * width * count).astype(F32)
        at += count
    count = shards[TAPS_AT].shape[0]
    full[TAPS_AT] = jnp.transpose(gathered[:, at : at + count], (1, 0, 2)).reshape(count, -1)
    at += count
    rows, cols = shards[TABLE_AT].shape
    count = -(-rows * cols // width)
    table = gathered[:, at : at + count].reshape(n, -1)[:, : rows * cols].reshape(n, rows, cols)
    full[TABLE_AT] = jnp.transpose(table, (1, 0, 2)).reshape(rows, n * cols)
    return full


def sum_small(grads, shards):
    n = lax.axis_size("shard")
    order = VECTORS + OFFSETS + (TAPS_AT, TABLE_AT)
    flat = jnp.concatenate([grads[i].reshape(-1) for i in order])
    spare = -flat.shape[0] % 16384
    flat = jnp.pad(flat, (0, spare)).astype(BF).reshape(-1, 1024)
    flat = lax.psum(flat, ("rep", "shard")).astype(F32).reshape(-1)
    z = lax.axis_index("shard")
    found = {}
    at = 0
    for i in order:
        size = grads[i].size
        whole = flat[at : at + size].reshape(grads[i].shape)
        at += size
        axis = whole.ndim - 1
        part = whole.shape[axis] // n
        found[i] = lax.dynamic_slice_in_dim(whole, z * part, part, axis)
    return found


def feed_forward(entering, gain, shift, widen, offset, narrow, bias):
    normed = norm(entering, gain, shift).astype(BF)
    act = times(normed, widen) + offset
    hidden = swish(act).astype(BF)
    return entering + 0.5 * (times(hidden, narrow) + bias), (normed, act, hidden)


def feed_backward(entering, gain, widen, narrow, saved, out_grad):
    normed, act, hidden = saved
    out_low = (0.5 * out_grad).astype(BF)
    act_grad = (times_back(out_low, narrow) * swish_slope(act)).astype(BF)
    normed_grad = times_back(act_grad, widen)
    back, grad_gain, grad_shift = norm_back(entering, gain, normed_grad)
    return (
        out_grad + back,
        (grad_gain, grad_shift, column_sum(act_grad), column_sum(out_low)),
        [(hidden, out_low), (normed, act_grad)],
    )


def conv_taps(padded, taps, local):
    total = padded[:, 0:local] * taps[0]
    for j in range(1, taps.shape[0]):
        total = total + padded[:, j : j + local] * taps[j]
    return total


def on_device(*arguments):
    inputs, shards, cotangent = (arguments[0], arguments[1:32], arguments[32])
    n_rep, n_shard = (lax.axis_size("rep"), lax.axis_size("shard"))
    micro, local, seqs, features = inputs.shape
    batch = micro * seqs
    fast = (
        n_rep == 8
        and n_shard == 4
        and features == 1024
        and batch * local == 256
        and all(shards[i].shape[0] % 256 == 0 for i in MATRICES)
    )

    def rows_of(array):
        return jnp.transpose(array, (0, 2, 1, 3)).reshape(batch * local, features)

    def whole_of(rows):
        return jnp.transpose(rows.reshape(micro, seqs, local, features), (0, 2, 1, 3))

    small = pack_small(shards)
    if fast:
        full, gathered = gather_fast([shards[i] for i in MATRICES], small)
    else:
        full = [lax.all_gather(shards[i], "shard", axis=0, tiled=True) for i in MATRICES]
        gathered = lax.all_gather(small, "shard", axis=0, tiled=False)
    w = dict(zip(MATRICES, full))
    w.update(unpack_small(gathered, shards))

    level0 = rows_of(inputs).astype(F32)
    level1, early = feed_forward(level0, w[0], w[1], w[2], w[3], w[4], w[5])

    attend_in = norm(level1, w[6], w[7]).astype(BF)
    query = (times(attend_in, w[8]) + w[9]).astype(BF).reshape(batch, local, features)
    keys = times(attend_in, w[10]).astype(BF).reshape(batch, local, features)
    values = (times(attend_in, w[11]) + w[12]).astype(BF).reshape(batch, local, features)
    query_h, keys_h, values_h = from_positions(swap(to_heads([query, keys, values], n_rep), 0))
    place = jnp.clip(jnp.arange(BAND) - 64, 0, TABLE - 1)
    place = jnp.where(jnp.arange(BAND) >= 384, 0, place)
    table = w[TABLE_AT]
    spread_table = jnp.tile(jnp.take(table, place, axis=0), (1, query_h.shape[2] // HD))
    mixed_h, logsum = attention_forward(query_h, keys_h, values_h, spread_table)
    mixed = from_heads(swap(to_positions([mixed_h.astype(BF)], n_rep), 1))[0]
    level2 = level1 + times(mixed, w[13]) + w[14]

    conv_in = norm(level2, w[16], w[17]).astype(BF)
    doubled = times(conv_in, w[18])
    side_a, side_b = (doubled[:, :features], doubled[:, features:])
    gate = jax.nn.sigmoid(side_b)
    gated = (side_a * gate).reshape(batch, local, features)
    taps = w[TAPS_AT].astype(F32)
    rim = taps.shape[0] - 1
    rim_in = shifted(gated[:, local - rim :].astype(BF), "rep", 1).astype(F32)
    padded = jnp.concatenate([rim_in, gated], axis=1)
    depth = conv_taps(padded, taps, local).reshape(batch * local, features)
    depth_normed = norm(depth, w[20], w[21])
    acted = swish(depth_normed).astype(BF)
    level3 = level2 + times(acted, w[22])

    level4, later = feed_forward(level3, w[23], w[24], w[25], w[26], w[27], w[28])
    output = norm(level4, w[29], w[30]).astype(BF)

    grads = {}
    incoming = rows_of(cotangent).astype(F32)
    back4, grads[29], grads[30] = norm_back(level4, w[29], incoming)
    back3, found, later_pairs = feed_backward(level3, w[23], w[25], w[27], later, back4)
    grads[23], grads[24], grads[26], grads[28] = found

    conv_out = back3.astype(BF)
    depth_mid = times_back(conv_out, w[22]) * swish_slope(depth_normed)
    depth_back, grads[20], grads[21] = norm_back(depth, w[20], depth_mid)
    depth_back = depth_back.reshape(batch, local, features)
    rim_back = shifted(depth_back[:, :rim].astype(BF), "rep", -1).astype(F32)
    after = jnp.concatenate([depth_back, rim_back], axis=1)
    grads[TAPS_AT] = jnp.stack(
        [jnp.sum(depth_back * padded[:, j : j + local], axis=(0, 1)) for j in range(rim + 1)]
    )
    gated_back = conv_taps(after, taps[::-1], local).reshape(batch * local, features)
    doubled_back = jnp.concatenate(
        [gated_back * gate, gated_back * side_a * gate * (1.0 - gate)], axis=1
    ).astype(BF)
    conv_back = times_back(doubled_back, w[18])
    back, grads[16], grads[17] = norm_back(level2, w[16], conv_back)
    back2 = back3 + back

    mixer_out = back2.astype(BF)
    grads[14] = column_sum(mixer_out)
    mixed_back = times_back(mixer_out, w[13]).astype(BF).reshape(batch, local, features)
    grad_h = from_positions(swap(to_heads([mixed_back], n_rep), 2))[0]
    query_b, keys_b, values_b, table_b = attention_backward(
        query_h, keys_h, values_h, spread_table, mixed_h, logsum, grad_h
    )
    query_back, key_back, value_back = from_heads(
        swap(to_positions([query_b, keys_b, values_b], n_rep), 3)
    )
    folded = table_b.reshape(BAND, -1, HD).sum(axis=1)
    grads[TABLE_AT] = jnp.concatenate(
        [
            (folded[0:65].sum(axis=0) + folded[384:].sum(axis=0))[None],
            folded[65:136],
            folded[136:384].sum(axis=0)[None],
        ]
    )
    grads[9] = column_sum(query_back)
    grads[12] = column_sum(value_back)
    attend_back = (
        times_back(query_back, w[8]) + times_back(key_back, w[10]) + times_back(value_back, w[11])
    )
    back, grads[6], grads[7] = norm_back(level1, w[6], attend_back)
    back1 = back2 + back
    back0, found, early_pairs = feed_backward(level0, w[0], w[2], w[4], early, back1)
    grads[0], grads[1], grads[3], grads[5] = found

    pairs = (
        (27, later_pairs[0]),
        (25, later_pairs[1]),
        (22, (acted, conv_out)),
        (18, (conv_in, doubled_back)),
        (13, (mixed, mixer_out)),
        (8, (attend_in, query_back)),
        (10, (attend_in, key_back)),
        (11, (attend_in, value_back)),
        (4, early_pairs[0]),
        (2, early_pairs[1]),
    )
    reduce = reduce_fast if fast else reduce_plain
    summed = dict(zip([i for i, _ in pairs], reduce([pair for _, pair in pairs])))
    summed.update(sum_small(grads, shards))
    return (whole_of(output), whole_of(back0)) + tuple(summed[i] for i in range(31))


def solution(mesh):
    rows, vector, matrix = (P(None, "rep", "shard", None), P("shard"), P("shard", None))
    columns = P(None, "shard")
    weights = tuple(
        matrix if i in MATRICES else columns if i in (TABLE_AT, TAPS_AT) else vector
        for i in range(31)
    )
    return jax.shard_map(
        on_device,
        mesh=mesh,
        in_specs=(rows,) + weights + (rows,),
        out_specs=(rows, rows) + weights,
        check_vma=False,
    )
```

time: 2520 us -> 884 us (0.35)
  waiting for transfers between devices: 1530 us -> 99.2 us
  Pallas kernels: 0 us -> 525 us
  matrix products: 401 us -> 60.4 us
  blocking collectives: 255 us -> 0 us
  local copies, waits for them, and re-layouts: 162 us -> 81 us
  other arithmetic: 126 us -> 86 us
    reduce_scatter x12 -> x0, waiting for transfers between devices: 713 us -> none  [the longest x1 148 us: on_device(): lax.psum_scatter(sectioned[2].astype(jnp.bfloat16), 'shard', scatter_dime...]
    all_gather x14 -> x0, waiting for transfers between devices: 671 us -> none  [the longest x1 146 us: fetch_weights(): lax.all_gather(shards[25], 'shard', axis=0, tiled=True)]
    pallas_call x0 -> x8, Pallas kernels: none -> 525 us  [the longest x1 231 us: reduce_fast(): pl.pallas_call(functools.partial(reduce_kernel, groups, units, len(lefts)...]
    dot_general x156 -> x20, matrix products: 401 us -> 60.4 us  [the longest x10 35.6 us: times_back(): lax.dot_general(left, right, (((1,), (1,)), ((), ())), preferred_element_...]
    all_gather x21 -> x0, blocking collectives: 212 us -> none  [the longest x1 13.8 us: fetch_weights(): lax.all_gather(shards[19], 'shard', axis=1, tiled=True)]
    psum x1, waiting for transfers between devices: 139 us -> 98.4 us  [sum_small(): flat = lax.psum(flat, ('rep', 'shard')).astype(F32).reshape(-1)]
    dot_general x16 -> x0, local copies, waits for them, and re-layouts: 25.5 us -> none  [relation(): jnp.einsum('qshr,qkr->shqk', offset_part, onehot, preferred_element_type=...]
    unnamed x704 -> x380, local copies, waits for them, and re-layouts: 52.1 us -> 30.2 us
  transfers between devices with their start and end apart: 33 -> 3, of which waited for: 20 -> 2; matrix products, arithmetic and copies ran while one was open for 22% -> 3% of each run, Pallas kernels for 0% -> 0%
where the time goes in v1:
time: 884 us; the launch traced here: 873 us
  Pallas kernels  525 us (59%)
  waiting for transfers between devices  99.2 us (11%)
  other arithmetic  86 us (10%)
  local copies, waits for them, and re-layouts  81 us (9%)
  matrix products  60.4 us (7%)
  between operations  17.5 us (2%)
    pallas_call x1, Pallas kernels, reduce_fast(): pl.pallas_call(functools.partial(reduce_kernel, groups, units, len(lefts)...  231 us
    pallas_call x1, Pallas kernels, gather_fast(): pl.pallas_call(functools.partial(gather_kernel, chunks, count), out_shape...  176 us
    psum x1, waiting for transfers between devices, sum_small(): flat = lax.psum(flat, ('rep', 'shard')).astype(F32).reshape(-1)  98.4 us
    pallas_call x4, Pallas kernels, swap(): pl.pallas_call(functools.partial(swap_kernel, n), out_shape=jax.ShapeDtyp...  63.8 us
    pallas_call x1, Pallas kernels, attention_backward(): pl.pallas_call(backward_kernel, out_shape=[shape, shape, shape, jax.Shape...  35.9 us
    dot_general x10, matrix products, times_back(): lax.dot_general(left, right, (((1,), (1,)), ((), ())), preferred_element_...  35.6 us
    unnamed x380, local copies, waits for them, and re-layouts  30.2 us
    dot_general x10, matrix products, times(): return jnp.dot(left, right, preferred_element_type=F32)  24.8 us
  transfers between devices with their start and end apart: 3, of which 2 were waited for; matrix products, arithmetic and copies ran while one was open for 3% of the time, Pallas kernels for 0%

profile of v1, /device:TPU:0, one launch (start us, length us, event | category | flops | bytes accessed | tf_op | source)
XLA Modules:
  0.0 872.9 jit_solution(16279509944978141444)
XLA Ops:
  20.8 1.0 concatenate.21.refs_10_
  21.8 1.6 copy-done.9
  23.4 1.6 copy-done.10
  25.0 1.6 copy-done.11
  26.6 1.6 copy-done.12
  28.2 1.2 copy-done.13
  29.4 1.0 copy-done.16
  30.4 1.0 copy-done.17
  31.5 1.0 copy-done.18
  32.5 1.0 copy-done.19
  33.5 1.0 copy-done.20
  34.6 176.5 %gather_weights.1 = (bf16[2,2,2,2,2,2,16,4096]{7,6,5,4,3,2,1,0:T(8,128)(2,1)}, bf16[2,2,2,2,2,2,64,1024]{7,6,5,4,3,2,1,0:T(8,128)(2,1)}, bf16[2,2,2,2,2,2,16,102...) custom-call(bf16[2,2,2,2,16,4096]{5,4,3,2,1,0:T(8,128)(2,1)S(1)} %bi, ...), custom_call_target="tpu_custom_call" | custom-call | tf_op jit(solution)/shard_map/gather_weights/pallas_call | solution.py:184
  211.9 1.0 convert_bitcast_fusion.4
  213.2 1.0 fusion.147
  215.4 8.2 multiply_convert_fusion.1
  223.6 2.5 fusion.166
  230.1 20.8 %swap_0.1 = bf16[8,3,2,128,128]{4,3,2,1,0:T(8,128)(2,1)S(1)} custom-call(bf16[8,3,2,128,128]{4,3,2,1,0:T(8,128)(2,1)S(1)} %pad_maximum_fusion.x_ref), custom_call_target="tpu_custom_call" | custom-call | tf_op jit(solution)/shard_map/swap_0/pallas_call | solution.py:521
  251.6 1.3 gather_fusion
  253.3 17.7 %attention_forward.1 = (f32[2,1024,128]{2,1,0:T(8,128)S(1)}, f32[2,1024,128]{2,1,0:T(8,128)S(1)}) custom-call(bf16[2,1024,128]{2,1,0:T(8,128)(2,1)S(1)} %bitcast.420, bf16[2,1024,128]{2,1,0:T(8,128)(2,1)S(1)} %bitcast.422, bf16[2,1024,128]{2,1,0:T(8,128)(2,1)S(1)} %bitcast.424, bf16[512,128]{1,0:T(8,128)(2,1)S(1)} %copy.120.table_ref), custom_call_target="tpu_custom_call" | custom-call | tf_op jit(solution)/shard_map/attention_forward/pallas_call | solution.py:622
  272.0 9.3 %swap_1.1 = bf16[8,1,2,128,128]{4,3,2,1,0:T(8,128)(2,1)S(1)} custom-call(bf16[8,1,2,128,128]{4,3,2,1,0:T(8,128)(2,1)S(1)} %bitcast.433), custom_call_target="tpu_custom_call" | custom-call | tf_op jit(solution)/shard_map/swap_1/pallas_call | solution.py:521
  284.2 1.3 fusion.172
  286.6 2.2 collective-permute-start
  291.7 21.4 %fusion.160 = (f32[2,128]{1,0:T(2,128)S(1)}, f32[2,128,1024]{2,1,0:T(8,128)S(1)}) fusion(f32[2,128,1024]{2,1,0:T(8,128)} %bitcast.455, f32[1024]{0:T(1024)S(1)} %bitcast.509, f32[1024]{0:T(1024)S(1)} %bitcast.511, f32[2,30,1024]{2,1,0:T(8,128)S(1)} %convert_element_type.435, f32[1024]{0:T(1024)S(1)} %bitcast.513, f32[1024]{0:T(1024)S(1)} %bitcast.515, ...), kind=kLoop, calls=%fused_computation.517 | loop fusion | flops 24116992 | bytes 2470912 | tf_op jit(solution)/shard_map/reduce_sum | solution.py:773
  315.7 6.7 multiply_convert_fusion
  322.5 2.4 fusion.169
  327.2 7.3 fusion.171
  334.5 7.6 multiply_reduce_fusion.31
  342.2 1.3 multiply_convert_fusion.2
  343.5 1.9 fusion.159
  345.3 1.8 multiply_reduce_fusion.32
  348.4 1.4 multiply_reduce_fusion.1
  349.7 1.4 multiply_reduce_fusion.2
  351.1 1.3 multiply_reduce_fusion.3
  352.7 1.3 collective-permute-start.1
  357.0 20.5 %fusion.16 = f32[2,128,1024]{2,1,0:T(8,128)S(1)} fusion(f32[2,128,1024]{2,1,0:T(8,128)} %bitcast.461, f32[2,30,1024]{2,1,0:T(8,128)S(1)} %convert_element_type.465, f32[1024]{0:T(1024)S(1)} %bitcast.510, f32[1024]{0:T(1024)S(1)} %bitcast.512, f32[1024]{0:T(1024)S(1)} %bitcast.514, f32[1024]{0:T(1024)S(1)} %bitcast.516, f32[1024]{0:T(1024)S(1)} %bitcast.518, ...), kind=kLoop, calls=%fused_computation.159 | loop fusion | flops 23855104 | bytes 2469888 | tf_op jit(solution)/shard_map/add | solution.py:901
  378.8 4.5 multiply_reduce_fusion.33
  383.3 2.0 fusion.157
  386.2 13.2 %swap_2.1 = bf16[8,1,2,128,128]{4,3,2,1,0:T(8,128)(2,1)S(1)} custom-call(bf16[8,1,2,128,128]{4,3,2,1,0:T(8,128)(2,1)S(1)} %bitcast.435), custom_call_target="tpu_custom_call" | custom-call | tf_op jit(solution)/shard_map/swap_2/pallas_call | solution.py:521
  399.5 35.9 %attention_backward.1 = (bf16[2,1024,128]{2,1,0:T(8,128)(2,1)S(1)}, bf16[2,1024,128]{2,1,0:T(8,128)(2,1)S(1)}, bf16[2,1024,128]{2,1,0:T(8,128)(2,1)S(1)}, f32[512,128]{1,0:T(8,128)S(1)}) custom-call(bf16[2,1024,128]{2,1,0:T(8,128)(2,1)S(1)} %bitcast.421, bf16[2,1024,128]{2,1,0:T(8,128)(2,1)S(1)} %bitcast.423, bf16[2,1024,128]{2,1,0:T(8,128)(2,1)S(1)} %bitcast.425, ...), custom_call_target="tpu_custom_call" | custom-call | tf_op jit(solution)/shard_map/attention_backward/pallas_call | solution.py:747
  435.7 20.5 %swap_3.1 = bf16[8,3,2,128,128]{4,3,2,1,0:T(8,128)(2,1)S(1)} custom-call(bf16[8,3,2,128,128]{4,3,2,1,0:T(8,128)(2,1)S(1)} %pad_maximum_fusion.1.x_ref), custom_call_target="tpu_custom_call" | custom-call | tf_op jit(solution)/shard_map/swap_3/pallas_call | solution.py:521
  461.8 2.3 pad_maximum_fusion.4.refs_11_
  469.9 1.1 multiply_reduce_fusion.34
  471.1 1.4 fusion.158
  472.6 7.2 fusion.170
  479.9 3.8 multiply_reduce_fusion.35
  483.7 231.3 %reduce_grads.1 = bf16[23,2,2,2,2,16,1024]{6,5,4,3,2,1,0:T(8,128)(2,1)} custom-call(bf16[256,4096]{1,0:T(8,128)(2,1)} %copy-done.52, bf16[256,1024]{1,0:T(8,128)(2,1)} %copy-done.50, bf16[256,1024]{1,0:T(8,128)(2,1)} %get-tuple-element.220.refs_2_, bf16[256,1024]{1,0:T(8,128)(2,1)} %copy-done.49, bf16[256,1024]{1,0:T(8,128)(2,1)} %bitcast.472, ...), custom_call_target="tpu_custom_call" | custom-call | tf_op jit(solution)/shard_map/reduce_grads/pallas_call | solution.py:450
  715.0 5.9 fusion.161
  720.9 3.2 copy-done.23
  724.1 1.5 fusion.162
  727.9 2.2 convert_bitcast_fusion.1
  730.2 2.6 bitcast_convert_fusion.1
  732.8 1.1 bitcast_convert_fusion.6
  733.9 1.1 bitcast_convert_fusion.5
  735.0 1.1 bitcast_convert_fusion.4
  736.1 1.1 bitcast_convert_fusion.3
  738.7 2.6 bitcast_convert_fusion
  741.8 1.1 bitcast_convert_fusion.2
  742.9 2.0 copy.140
  745.0 2.3 copy.142
  747.3 1.5 copy.143
  748.7 2.3 copy.144
  751.0 98.4 %all-reduce.4.cloned.1.call-done = bf16[64,1024]{1,0:T(8,128)(2,1)} async-done(((bf16[64,1024]{1,0:T(8,128)(2,1)}), bf16[64,1024]{1,0:T(8,128)(2,1)}) %all-reduce.4.cloned.1.call-update) | async-done | bytes 131088 | tf_op jit(solution)/shard_map/psum | solution.py:864
  849.4 1.3 fusion.163
  856.2 1.1 slice.780
  (565 shorter events, 68.0 us)
Async XLA Ops:
  7.2 842.2 %all-reduce.4.cloned.1.call-start = ((), (), s32[]{:S(2)}) async-start(), calls=%async_computation | async-start | bytes 262144 | tf_op jit(solution)/shard_map/psum | solution.py:864
  34.6 178.4 %copy-start.37 = (bf16[2,128,1,1024]{3,1,2,0:T(8,128)(2,1)S(1)}, bf16[2,128,1,1024]{3,1,2,0:T(8,128)(2,1)}, u32[]{:S(2)}) copy-start(bf16[2,128,1,1024]{3,1,2,0:T(8,128)(2,1)} %param.33) | copy-start | bytes 1572868
  211.1 12.4 %copy-start.2 = (bf16[2,2,2,2,2,2,16,1024]{7,6,5,4,3,2,1,0:T(8,128)(2,1)}, bf16[2,2,2,2,2,2,16,1024]{7,6,5,4,3,2,1,0:T(8,128)(2,1)S(1)}, u32[]{:S(2)}) copy-start(bf16[2,2,2,2,2,2,16,1024]{7,6,5,4,3,2,1,0:T(8,128)(2,1)S(1)} %get-tuple-element.59) | copy-start | bytes 6291460
  211.1 12.4 %copy-start.6 = (bf16[2,2,2,2,2,2,16,1024]{7,6,5,4,3,2,1,0:T(8,128)(2,1)}, bf16[2,2,2,2,2,2,16,1024]{7,6,5,4,3,2,1,0:T(8,128)(2,1)S(1)}, u32[]{:S(2)}) copy-start(bf16[2,2,2,2,2,2,16,1024]{7,6,5,4,3,2,1,0:T(8,128)(2,1)S(1)} %get-tuple-element.57) | copy-start | bytes 6291460
  211.1 15.5 %copy-start.21 = (bf16[2,2,2,2,2,2,16,1024]{7,6,5,4,3,2,1,0:T(8,128)(2,1)}, bf16[2,2,2,2,2,2,16,1024]{7,6,5,4,3,2,1,0:T(8,128)(2,1)S(1)}, u32[]{:S(2)}) copy-start(bf16[2,2,2,2,2,2,16,1024]{7,6,5,4,3,2,1,0:T(8,128)(2,1)S(1)} %get-tuple-element.55) | copy-start | bytes 6291460
  211.1 16.4 %copy-start.4 = (bf16[2,2,2,2,2,2,16,1024]{7,6,5,4,3,2,1,0:T(8,128)(2,1)}, bf16[2,2,2,2,2,2,16,1024]{7,6,5,4,3,2,1,0:T(8,128)(2,1)S(1)}, u32[]{:S(2)}) copy-start(bf16[2,2,2,2,2,2,16,1024]{7,6,5,4,3,2,1,0:T(8,128)(2,1)S(1)} %get-tuple-element.54) | copy-start | bytes 6291460
  211.1 17.2 %copy-start = (bf16[2,2,2,2,2,2,16,1024]{7,6,5,4,3,2,1,0:T(8,128)(2,1)}, bf16[2,2,2,2,2,2,16,1024]{7,6,5,4,3,2,1,0:T(8,128)(2,1)S(1)}, u32[]{:S(2)}) copy-start(bf16[2,2,2,2,2,2,16,1024]{7,6,5,4,3,2,1,0:T(8,128)(2,1)S(1)} %get-tuple-element.53) | copy-start | bytes 6291460
  211.9 11.6 %copy-start.65 = (f32[4,1,256]{2,1,0:T(1,128)}, f32[4,1,256]{2,1,0:T(1,128)S(1)}, u32[]{:S(2)}) copy-start(f32[4,1,256]{2,1,0:T(1,128)S(1)} %get-tuple-element.290) | copy-start | bytes 12292
  211.9 11.6 %copy-start.131 = (f32[4,1,256]{2,1,0:T(1,128)}, f32[4,1,256]{2,1,0:T(1,128)S(1)}, u32[]{:S(2)}) copy-start(f32[4,1,256]{2,1,0:T(1,128)S(1)} %get-tuple-element.289) | copy-start | bytes 12292
  211.9 14.4 %copy-start.127 = (f32[4,1,256]{2,1,0:T(1,128)}, f32[4,1,256]{2,1,0:T(1,128)S(1)}, u32[]{:S(2)}) copy-start(f32[4,1,256]{2,1,0:T(1,128)S(1)} %get-tuple-element.287) | copy-start | bytes 12292
  211.9 70.9 %copy-start.129 = (f32[4,1,256]{2,1,0:T(1,128)}, f32[4,1,256]{2,1,0:T(1,128)S(1)}, u32[]{:S(2)}) copy-start(f32[4,1,256]{2,1,0:T(1,128)S(1)} %get-tuple-element.282) | copy-start | bytes 12292
  215.1 8.5 slice-start.3
  215.3 8.2 slice-start.4
  271.0 10.6 %copy-start.7 = (bf16[2,2,2,2,2,2,16,1024]{7,6,5,4,3,2,1,0:T(8,128)(2,1)S(1)}, bf16[2,2,2,2,2,2,16,1024]{7,6,5,4,3,2,1,0:T(8,128)(2,1)}, u32[]{:S(2)}) copy-start(bf16[2,2,2,2,2,2,16,1024]{7,6,5,4,3,2,1,0:T(8,128)(2,1)} %copy-done.6) | copy-start | bytes 6291460
  271.0 10.6 %copy-start.34 = (f32[256,1024]{1,0:T(8,128)S(1)}, f32[256,1024]{1,0:T(8,128)}, u32[]{:S(2)}) copy-start(f32[256,1024]{1,0:T(8,128)} %copy-done.33) | copy-start | bytes 3145732
  286.6 5.1 collective-permute-start
  288.9 24.2 %copy-start.67 = (f32[1,4,256]{2,0,1:T(1,128)}, f32[1,4,256]{2,0,1:T(1,128)S(1)}, u32[]{:S(2)}) copy-start(f32[1,4,256]{2,0,1:T(1,128)S(1)} %get-tuple-element.295) | copy-start | bytes 12292
  288.9 24.2 %copy-start.69 = (f32[1,4,256]{2,0,1:T(1,128)}, f32[1,4,256]{2,0,1:T(1,128)S(1)}, u32[]{:S(2)}) copy-start(f32[1,4,256]{2,0,1:T(1,128)S(1)} %get-tuple-element.296) | copy-start | bytes 12292
  288.9 24.2 %copy-start.71 = (f32[1,4,256]{2,0,1:T(1,128)}, f32[1,4,256]{2,0,1:T(1,128)S(1)}, u32[]{:S(2)}) copy-start(f32[1,4,256]{2,0,1:T(1,128)S(1)} %get-tuple-element.297) | copy-start | bytes 12292
  288.9 24.2 %copy-start.73 = (f32[1,4,256]{2,0,1:T(1,128)}, f32[1,4,256]{2,0,1:T(1,128)S(1)}, u32[]{:S(2)}) copy-start(f32[1,4,256]{2,0,1:T(1,128)S(1)} %get-tuple-element.298) | copy-start | bytes 12292
  288.9 24.2 %copy-start.75 = (f32[1,4,256]{2,0,1:T(1,128)}, f32[1,4,256]{2,0,1:T(1,128)S(1)}, u32[]{:S(2)}) copy-start(f32[1,4,256]{2,0,1:T(1,128)S(1)} %get-tuple-element.299) | copy-start | bytes 12292
  288.9 24.2 %copy-start.77 = (f32[1,4,256]{2,0,1:T(1,128)}, f32[1,4,256]{2,0,1:T(1,128)S(1)}, u32[]{:S(2)}) copy-start(f32[1,4,256]{2,0,1:T(1,128)S(1)} %get-tuple-element.300) | copy-start | bytes 12292
  288.9 24.2 %copy-start.79 = (f32[1,4,256]{2,0,1:T(1,128)}, f32[1,4,256]{2,0,1:T(1,128)S(1)}, u32[]{:S(2)}) copy-start(f32[1,4,256]{2,0,1:T(1,128)S(1)} %get-tuple-element.301) | copy-start | bytes 12292
  289.0 24.2 %copy-start.81 = (f32[1,4,256]{2,0,1:T(1,128)}, f32[1,4,256]{2,0,1:T(1,128)S(1)}, u32[]{:S(2)}) copy-start(f32[1,4,256]{2,0,1:T(1,128)S(1)} %get-tuple-element.302) | copy-start | bytes 12292
  289.0 24.2 %copy-start.83 = (f32[1,4,256]{2,0,1:T(1,128)}, f32[1,4,256]{2,0,1:T(1,128)S(1)}, u32[]{:S(2)}) copy-start(f32[1,4,256]{2,0,1:T(1,128)S(1)} %get-tuple-element.303) | copy-start | bytes 12292
  289.0 24.2 %copy-start.85 = (f32[1,4,256]{2,0,1:T(1,128)}, f32[1,4,256]{2,0,1:T(1,128)S(1)}, u32[]{:S(2)}) copy-start(f32[1,4,256]{2,0,1:T(1,128)S(1)} %get-tuple-element.304) | copy-start | bytes 12292
  289.0 24.2 %copy-start.87 = (f32[1,4,256]{2,0,1:T(1,128)}, f32[1,4,256]{2,0,1:T(1,128)S(1)}, u32[]{:S(2)}) copy-start(f32[1,4,256]{2,0,1:T(1,128)S(1)} %get-tuple-element.305) | copy-start | bytes 12292
  289.0 24.2 %copy-start.89 = (f32[1,4,256]{2,0,1:T(1,128)}, f32[1,4,256]{2,0,1:T(1,128)S(1)}, u32[]{:S(2)}) copy-start(f32[1,4,256]{2,0,1:T(1,128)S(1)} %get-tuple-element.306) | copy-start | bytes 12292
  289.0 24.2 %copy-start.91 = (f32[1,4,256]{2,0,1:T(1,128)}, f32[1,4,256]{2,0,1:T(1,128)S(1)}, u32[]{:S(2)}) copy-start(f32[1,4,256]{2,0,1:T(1,128)S(1)} %get-tuple-element.307) | copy-start | bytes 12292
  289.0 24.2 %copy-start.93 = (f32[1,4,256]{2,0,1:T(1,128)}, f32[1,4,256]{2,0,1:T(1,128)S(1)}, u32[]{:S(2)}) copy-start(f32[1,4,256]{2,0,1:T(1,128)S(1)} %get-tuple-element.308) | copy-start | bytes 12292
  289.0 24.2 %copy-start.95 = (f32[1,4,256]{2,0,1:T(1,128)}, f32[1,4,256]{2,0,1:T(1,128)S(1)}, u32[]{:S(2)}) copy-start(f32[1,4,256]{2,0,1:T(1,128)S(1)} %get-tuple-element.309) | copy-start | bytes 12292
  289.0 24.2 %copy-start.97 = (f32[1,4,256]{2,0,1:T(1,128)}, f32[1,4,256]{2,0,1:T(1,128)S(1)}, u32[]{:S(2)}) copy-start(f32[1,4,256]{2,0,1:T(1,128)S(1)} %get-tuple-element.310) | copy-start | bytes 12292
  289.0 24.2 %copy-start.99 = (f32[1,4,256]{2,0,1:T(1,128)}, f32[1,4,256]{2,0,1:T(1,128)S(1)}, u32[]{:S(2)}) copy-start(f32[1,4,256]{2,0,1:T(1,128)S(1)} %get-tuple-element.311) | copy-start | bytes 12292
  289.1 24.1 %copy-start.101 = (f32[1,4,256]{2,0,1:T(1,128)}, f32[1,4,256]{2,0,1:T(1,128)S(1)}, u32[]{:S(2)}) copy-start(f32[1,4,256]{2,0,1:T(1,128)S(1)} %get-tuple-element.312) | copy-start | bytes 12292
  289.1 24.1 %copy-start.103 = (f32[1,4,256]{2,0,1:T(1,128)}, f32[1,4,256]{2,0,1:T(1,128)S(1)}, u32[]{:S(2)}) copy-start(f32[1,4,256]{2,0,1:T(1,128)S(1)} %get-tuple-element.313) | copy-start | bytes 12292
  289.1 24.1 %copy-start.105 = (f32[1,4,256]{2,0,1:T(1,128)}, f32[1,4,256]{2,0,1:T(1,128)S(1)}, u32[]{:S(2)}) copy-start(f32[1,4,256]{2,0,1:T(1,128)S(1)} %get-tuple-element.314) | copy-start | bytes 12292
  289.1 24.1 %copy-start.107 = (f32[1,4,256]{2,0,1:T(1,128)}, f32[1,4,256]{2,0,1:T(1,128)S(1)}, u32[]{:S(2)}) copy-start(f32[1,4,256]{2,0,1:T(1,128)S(1)} %get-tuple-element.315) | copy-start | bytes 12292
  289.1 24.1 %copy-start.109 = (f32[1,4,256]{2,0,1:T(1,128)}, f32[1,4,256]{2,0,1:T(1,128)S(1)}, u32[]{:S(2)}) copy-start(f32[1,4,256]{2,0,1:T(1,128)S(1)} %get-tuple-element.316) | copy-start | bytes 12292
  289.2 24.1 %copy-start.111 = (f32[1,4,256]{2,0,1:T(1,128)}, f32[1,4,256]{2,0,1:T(1,128)S(1)}, u32[]{:S(2)}) copy-start(f32[1,4,256]{2,0,1:T(1,128)S(1)} %get-tuple-element.317) | copy-start | bytes 12292
  289.2 24.1 %copy-start.113 = (f32[1,4,256]{2,0,1:T(1,128)}, f32[1,4,256]{2,0,1:T(1,128)S(1)}, u32[]{:S(2)}) copy-start(f32[1,4,256]{2,0,1:T(1,128)S(1)} %get-tuple-element.318) | copy-start | bytes 12292
  289.2 24.1 %copy-start.115 = (f32[1,4,256]{2,0,1:T(1,128)}, f32[1,4,256]{2,0,1:T(1,128)S(1)}, u32[]{:S(2)}) copy-start(f32[1,4,256]{2,0,1:T(1,128)S(1)} %get-tuple-element.319) | copy-start | bytes 12292
  289.2 24.1 %copy-start.117 = (f32[1,4,256]{2,0,1:T(1,128)}, f32[1,4,256]{2,0,1:T(1,128)S(1)}, u32[]{:S(2)}) copy-start(f32[1,4,256]{2,0,1:T(1,128)S(1)} %get-tuple-element.320) | copy-start | bytes 12292
  289.2 24.1 %copy-start.119 = (f32[1,4,256]{2,0,1:T(1,128)}, f32[1,4,256]{2,0,1:T(1,128)S(1)}, u32[]{:S(2)}) copy-start(f32[1,4,256]{2,0,1:T(1,128)S(1)} %get-tuple-element.321) | copy-start | bytes 12292
  289.2 24.1 %copy-start.121 = (f32[1,4,256]{2,0,1:T(1,128)}, f32[1,4,256]{2,0,1:T(1,128)S(1)}, u32[]{:S(2)}) copy-start(f32[1,4,256]{2,0,1:T(1,128)S(1)} %get-tuple-element.322) | copy-start | bytes 12292
  289.2 24.1 %copy-start.123 = (f32[1,4,256]{2,0,1:T(1,128)}, f32[1,4,256]{2,0,1:T(1,128)S(1)}, u32[]{:S(2)}) copy-start(f32[1,4,256]{2,0,1:T(1,128)S(1)} %get-tuple-element.323) | copy-start | bytes 12292
  291.6 22.0 %copy-start.125 = (f32[4,1,256]{2,1,0:T(1,128)S(1)}, f32[4,1,256]{2,1,0:T(1,128)}, u32[]{:S(2)}) copy-start(f32[4,1,256]{2,1,0:T(1,128)} %get-tuple-element.279) | copy-start | bytes 12292
  291.7 22.4 %copy-start.3 = (bf16[2,2,2,2,2,2,16,1024]{7,6,5,4,3,2,1,0:T(8,128)(2,1)S(1)}, bf16[2,2,2,2,2,2,16,1024]{7,6,5,4,3,2,1,0:T(8,128)(2,1)}, u32[]{:S(2)}) copy-start(bf16[2,2,2,2,2,2,16,1024]{7,6,5,4,3,2,1,0:T(8,128)(2,1)} %copy-done.2) | copy-start | bytes 6291460
  291.7 22.4 %copy-start.28 = (f32[256,1024]{1,0:T(8,128)S(1)}, f32[256,1024]{1,0:T(8,128)}, u32[]{:S(2)}) copy-start(f32[256,1024]{1,0:T(8,128)} %copy-done.27) | copy-start | bytes 3145732
  315.0 7.5 slice-start.5
  315.5 6.9 copy-start.50
  327.2 7.3 copy-start.44
  334.5 7.6 copy-start.53
  352.7 3.9 collective-permute-start.1
  355.9 21.7 %copy-start.32 = (f32[256,2048]{1,0:T(8,128)S(1)}, f32[256,2048]{1,0:T(8,128)}, u32[]{:S(2)}) copy-start(f32[256,2048]{1,0:T(8,128)} %copy-done.30) | copy-start | bytes 6291460
  386.0 13.5 %copy-start.15 = (f32[2,1024,128]{2,1,0:T(8,128)S(1)}, f32[2,1024,128]{2,1,0:T(8,128)}, u32[]{:S(2)}) copy-start(f32[2,1024,128]{2,1,0:T(8,128)} %copy-done.14) | copy-start | bytes 3145732
  471.1 8.7 slice-start.1
  472.6 7.3 copy-start.47
  472.6 7.3 copy-start.38
  472.6 7.3 copy-start.66
  472.6 7.3 copy-start.132
  472.6 7.3 copy-start.151
  472.6 7.3 copy-start.152
  472.6 7.3 slice-start.2
  715.0 9.1 %copy-start.23 = (bf16[23,2,2,2,2,16,1024]{6,5,4,3,2,1,0:T(8,128)(2,1)S(1)}, bf16[23,2,2,2,2,16,1024]{6,5,4,3,2,1,0:T(8,128)(2,1)}, u32[]{:S(2)}) copy-start(bf16[23,2,2,2,2,16,1024]{6,5,4,3,2,1,0:T(8,128)(2,1)} %reduce_grads.1) | copy-start | bytes 36175876
  (111 other events, 300.3 us)
Sparse Core Ops, SparseCore 0:
  728.0 121.3 all-reduce.3

commit v2 on v1

--- a/solution.py
+++ b/solution.py
@@ -17,7 +17,7 @@
 MESH = pl.DeviceIdType.MESH
 BF = jnp.bfloat16
 F32 = jnp.float32
-ANY = pl.BlockSpec(memory_space=pl.ANY)
+ANY = pl.BlockSpec(memory_space=pltpu.HBM)
 VM = pl.BlockSpec(memory_space=pltpu.VMEM)
 
 
@@ -50,12 +50,29 @@
 GATHER_LAG = (0, 2, 3, 4, 5)
 
 
-def gather_kernel(chunks, n_arr, *refs):
-    ins, small = (refs[:n_arr], refs[n_arr])
-    outs, small_out = (refs[n_arr + 1 : 2 * n_arr + 1], refs[2 * n_arr + 1])
-    ssem, rsem, lsem, lsem2, qsem, psem = refs[2 * n_arr + 2 : 2 * n_arr + 8]
-    bufs = refs[2 * n_arr + 8 :]
+def fill_rows(packed, smalls):
+    width = packed.shape[1]
+    packed[...] = jnp.zeros_like(packed)
+    at = 0
+    for ref in smalls:
+        if len(ref.shape) == 1:
+            for k in range(ref.shape[0] // width):
+                packed[at, :] = ref[pl.ds(k * width, width)].astype(F32)
+                at += 1
+        else:
+            packed[at : at + ref.shape[0], 0 : ref.shape[1]] = ref[...].astype(F32)
+            at += ref.shape[0]
+
+
+def gather_kernel(chunks, n_arr, n_small, *refs):
+    ins, smalls = (refs[:n_arr], refs[n_arr : n_arr + n_small])
+    refs = refs[n_arr + n_small :]
+    outs, small_out = (refs[:n_arr], refs[n_arr])
+    ssem, rsem, lsem, lsem2, qsem, psem, packed, small = refs[n_arr + 1 : n_arr + 9]
+    bufs = refs[n_arr + 9 :]
     z, core, x, y, z0, z1, peers = here()
+    fill_rows(packed, smalls)
+    small[...] = packed[...].astype(BF)
     far = ((slice(None), 1 - z0), (1 - z1, z0))
     meet(peers)
     sent = []
@@ -73,7 +90,7 @@
         sent.append(copy)
         return copy
 
-    smalls = []
+    around = []
     for k, to in enumerate(("z0", "z1", "zz")):
         copy = pltpu.make_async_remote_copy(
             src_ref=small,
@@ -84,7 +101,7 @@
             device_id_type=MESH,
         )
         copy.start()
-        smalls.append(copy)
+        around.append(copy)
     small_own = pltpu.make_async_copy(small, small_out.at[z], lsem.at[n_arr])
     small_own.start()
     state = {}
@@ -157,9 +174,9 @@
                 local[a] = copy
     for c in range(len(chunks)):
         wait(c, "core")
-    for copy in sent + smalls:
+    for copy in sent + around:
         copy.wait_send()
-    for copy in smalls:
+    for copy in around:
         copy.wait_recv()
     small_own.wait()
     for copy in local:
@@ -174,17 +191,17 @@
     return chunks
 
 
-def gather_fast(shards, small):
-    count = len(shards)
+def gather_fast(shards, smalls, rows):
+    count, width = (len(shards), smalls[0].shape[0])
     ins = [w.reshape(2, 2, 2, 2, w.shape[0] // 16, w.shape[1]) for w in shards]
     chunks = gather_chunks([w.shape for w in shards])
     outs = [jax.ShapeDtypeStruct((2, 2) + w.shape, w.dtype) for w in ins]
-    outs.append(jax.ShapeDtypeStruct((4,) + small.shape, small.dtype))
+    outs.append(jax.ShapeDtypeStruct((4, rows, width), BF))
     dma = pltpu.SemaphoreType.DMA
     found = pl.pallas_call(
-        functools.partial(gather_kernel, chunks, count),
+        functools.partial(gather_kernel, chunks, count, len(smalls)),
         out_shape=outs,
-        in_specs=[ANY] * (count + 1),
+        in_specs=[ANY] * count + [VM] * len(smalls),
         out_specs=[ANY] * (count + 1),
         scratch_shapes=[
             dma((len(chunks), 13)),
@@ -193,23 +210,46 @@
             dma((count,)),
             dma((3,)),
             dma((3,)),
+            pltpu.VMEM((rows, width), F32),
+            pltpu.VMEM((rows, width), BF),
         ]
         + [pltpu.VMEM(w.shape, w.dtype) for w in ins],
         compiler_params=pltpu.CompilerParams(
-            collective_id=0, has_side_effects=True, vmem_limit_bytes=32 << 20
+            collective_id=0, has_side_effects=True, vmem_limit_bytes=58 << 20
         ),
         name="gather_weights",
-    )(*ins, small)
+    )(*ins, *smalls)
     return [w.reshape(-1, w.shape[-1]) for w in found[:count]], found[count]
 
 
+def fill_sums(total, smalls):
+    width = total.shape[1] // 4
+    total[...] = jnp.zeros_like(total)
+    at = 0
+    for ref in smalls:
+        if len(ref.shape) > 1:
+            total[at : at + ref.shape[0], :] = ref[...]
+            at += ref.shape[0]
+        elif ref.shape[0] == 4 * width:
+            total[at, :] = ref[...]
+            at += 1
+        else:
+            each = ref.shape[0] // (4 * width)
+            for k in range(each):
+                for z in range(4):
+                    total[at, pl.ds(z * width, width)] = ref[pl.ds((z * each + k) * width, width)]
+                at += 1
+
+
 REDUCE_LAG = (0, 1, 2, 3, 4, 5, 6, 7)
 
 
-def reduce_kernel(groups, units, n_left, n_right, *refs):
+def reduce_kernel(groups, units, n_left, n_right, n_small, *refs):
     lefts, rights = (refs[:n_left], refs[n_left : n_left + n_right])
-    out = refs[n_left + n_right]
-    lbuf, rbuf, sbuf, b1, b2, b3, b4, b5, lsem, ssem, rsem, osem = refs[n_left + n_right + 1 :]
+    refs = refs[n_left + n_right :]
+    smalls, outs, small_out = (refs[:n_small], refs[n_small:-18], refs[-18])
+    lbuf, rbuf, sbuf, b1, b2, b3, b4, b5, hop_out, hop_in, hop_total = refs[-17:-6]
+    lsem, ssem, rsem, osem, hsem, isem = refs[-6:]
     z, core, x, y, z0, z1, peers = here()
     del peers["zz"]
     meet(peers)
@@ -245,26 +285,39 @@
             remote(u, 6, b4.at[u, 1, 1 - x], b5.at[u, 1], "x"),
         ]
 
-    def copy_own(u):
+    def block(group, k, *at):
+        if groups[group][4]:
+            return outs[group].at[(k,) + at]
+        at = at + (slice(None),) * (5 - len(at))
+        return outs[group].at[at + (pl.ds(pl.multiple_of(k * 1024, 1024), 1024),)]
+
+    def copy_own(u, group=0, k=0):
         return [
-            pltpu.make_async_copy(b5.at[u, 0], out.at[u, core, 0, x, y], osem.at[u, 0]),
-            pltpu.make_async_copy(b5.at[u, 1], out.at[u, core, 1, y, x], osem.at[u, 1]),
+            pltpu.make_async_copy(b5.at[u, 0], block(group, k, core, 0, x, y), osem.at[u, 0]),
+            pltpu.make_async_copy(b5.at[u, 1], block(group, k, core, 1, y, x), osem.at[u, 1]),
         ]
 
-    def spread_second(u):
+    def spread_second(u, group=0, k=0):
         return [
-            remote(u, 7, b5.at[u, 0], out.at[u, core, 0, x, y], "y"),
-            remote(u, 8, b5.at[u, 1], out.at[u, core, 1, y, x], "x"),
+            remote(u, 7, b5.at[u, 0], block(group, k, core, 0, x, y), "y"),
+            remote(u, 8, b5.at[u, 1], block(group, k, core, 1, y, x), "x"),
         ]
 
-    def spread_first(u):
-        return [
-            remote(u, 9, out.at[u, core, 0, x], out.at[u, core, 0, x], "x"),
-            remote(u, 10, out.at[u, core, 1, y], out.at[u, core, 1, y], "y"),
-        ]
-
-    def spread_core(u):
-        return [remote(u, 11, out.at[u, core], out.at[u, core], "c")]
+    def spread_first(u, group=0, k=0):
+        a, b = (block(group, k, core, 0, x), block(group, k, core, 1, y))
+        return [remote(u, 9, a, a, "x"), remote(u, 10, b, b, "y")]
+
+    def spread_core(u, group=0, k=0):
+        a = block(group, k, core)
+        return [remote(u, 11, a, a, "c")]
+
+    def start_out(u, *makers):
+        for group, (_, _, first, count, _) in enumerate(groups):
+
+            @pl.when(jnp.logical_and(u >= first, u < first + count))
+            def _():
+                for make in makers:
+                    start(make(u, group, u - first))
 
     def start(copies):
         for copy in copies:
@@ -371,18 +424,17 @@
         arrive(copy_second(u))
         for half, bit in ((0, y), (1, x)):
             b5[u, half] = (b5[u, half].astype(F32) + b4[u, half, bit].astype(F32)).astype(BF)
-        start(copy_own(u))
-        start(spread_second(u))
+        start_out(u, copy_own, spread_second)
 
     def stage_spread(u):
         arrive(spread_second(u))
         for copy in copy_own(u):
             copy.wait()
-        start(spread_first(u))
+        start_out(u, spread_first)
 
     def stage_core(u):
         arrive(spread_first(u))
-        start(spread_core(u))
+        start_out(u, spread_core)
 
     stages = (
         stage_multiply,
@@ -395,7 +447,40 @@
         stage_core,
     )
 
+    hops = ("c", "x", "y", "z0", "z1")
+
+    def hop(k):
+        return pltpu.make_async_remote_copy(
+            src_ref=hop_out.at[k],
+            dst_ref=hop_in.at[k],
+            send_sem=hsem.at[k],
+            recv_sem=isem.at[k],
+            device_id=peers[hops[k]],
+            device_id_type=MESH,
+        )
+
+    fill_sums(hop_total, smalls)
+    hop_out[0] = hop_total[...].astype(BF)
+    hop(0).start()
+
+    def stage_hop(k):
+        hop(k).wait_recv()
+        total = hop_out[k].astype(F32) + hop_in[k].astype(F32)
+        if k + 1 < len(hops):
+            hop_out[k + 1] = total.astype(BF)
+            hop(k + 1).start()
+        else:
+            width = small_out.shape[1]
+            hop_total[...] = total
+            small_out[...] = hop_total[:, pl.ds(pl.multiple_of(z * width, width), width)]
+
     def step(i, carry):
+        for k in range(len(hops)):
+
+            @pl.when(i == 2 * k + 1)
+            def _():
+                stage_hop(k)
+
         for stage, lag in zip(stages, REDUCE_LAG):
             u = i - lag
 
@@ -429,9 +514,11 @@
         return carry
 
     lax.fori_loop(0, units, finish, 0)
-
-
-def reduce_fast(pairs):
+    for k in range(len(hops)):
+        hop(k).wait_send()
+
+
+def reduce_fast(pairs, smalls):
     lefts, rights, groups, units = ([], [], [], 0)
 
     def index_of(arrays, array):
@@ -447,11 +534,17 @@
         groups.append((index_of(lefts, left), index_of(rights, right), units, count, by_rows))
         units += count
     dma = pltpu.SemaphoreType.DMA
+    rows = sum(a.shape[0] if a.ndim > 1 else a.shape[0] // 1024 for a in smalls)
+    rows = -(-rows // 16) * 16
+    outs = []
+    for _, _, _, count, by_rows in groups:
+        shape = (count, 2, 2, 2, 2, 16, 1024) if by_rows else (2, 2, 2, 2, 16, count * 1024)
+        outs.append(jax.ShapeDtypeStruct(shape, BF))
     found = pl.pallas_call(
-        functools.partial(reduce_kernel, groups, units, len(lefts), len(rights)),
-        out_shape=jax.ShapeDtypeStruct((units, 2, 2, 2, 2, 16, 1024), BF),
-        in_specs=[ANY] * (len(lefts) + len(rights)),
-        out_specs=ANY,
+        functools.partial(reduce_kernel, groups, units, len(lefts), len(rights), len(smalls)),
+        out_shape=outs + [jax.ShapeDtypeStruct((rows, 256), F32)],
+        in_specs=[ANY] * (len(lefts) + len(rights)) + [VM] * len(smalls),
+        out_specs=[ANY] * len(outs) + [VM],
         scratch_shapes=[
             pltpu.VMEM((3, 4, 256, 256), BF),
             pltpu.VMEM((3, 256, 1024), BF),
@@ -461,33 +554,34 @@
             pltpu.VMEM((units, 2, 2, 2, 16, 1024), BF),
             pltpu.VMEM((units, 2, 2, 16, 1024), BF),
             pltpu.VMEM((units, 2, 16, 1024), BF),
+            pltpu.VMEM((5, rows, 1024), BF),
+            pltpu.VMEM((5, rows, 1024), BF),
+            pltpu.VMEM((rows, 1024), F32),
             dma((3, 5)),
             dma((units, 12)),
             dma((units, 12)),
             dma((units, 2)),
+            dma((5,)),
+            dma((5,)),
         ],
         compiler_params=pltpu.CompilerParams(
             collective_id=1, has_side_effects=True, vmem_limit_bytes=60 << 20
         ),
         name="reduce_grads",
-    )(*lefts, *rights)
-    found = found.reshape(units, 256, 1024)
-    grads = []
-    for li, ri, first, count, by_rows in groups:
-        part = found[first : first + count]
-        if not by_rows:
-            part = jnp.transpose(part, (1, 0, 2))
-        grads.append(part.reshape((count * 256, 1024) if by_rows else (256, -1)).astype(F32))
-    return grads
-
-
-def reduce_plain(pairs):
+    )(*lefts, *rights, *smalls)
+    return [w.reshape(-1, w.shape[-1]).astype(F32) for w in found[:-1]], found[-1]
+
+
+def reduce_plain(pairs, small):
+    small = pack_sums(small, lax.axis_size("shard"))
     grads = []
     for left, right in pairs:
         full = lax.dot_general(left, right, (((0,), (0,)), ((), ())), preferred_element_type=F32)
         part = lax.psum_scatter(full.astype(BF), "shard", scatter_dimension=0, tiled=True)
         grads.append(lax.psum(part, "rep").astype(F32))
-    return grads
+    summed = lax.psum(small.astype(BF), ("rep", "shard")).astype(F32)
+    width = small.shape[1] // lax.axis_size("shard")
+    return grads, lax.dynamic_slice_in_dim(summed, lax.axis_index("shard") * width, width, 1)
 
 
 def swap_kernel(n, x_ref, o_ref, ssem, rsem):
@@ -562,7 +656,7 @@
     ]
 
 
-QROWS = 256
+QROWS = 128
 
 
 def head_mask(shape, head):
@@ -821,17 +915,24 @@
 TAPS_AT = 19
 
 
+SMALLS = VECTORS + OFFSETS + (TAPS_AT, TABLE_AT)
+
+
+def small_rows(shards):
+    width = shards[0].shape[0]
+    count = len(VECTORS) + sum(shards[i].shape[0] // width for i in OFFSETS)
+    count += shards[TAPS_AT].shape[0] + shards[TABLE_AT].shape[0]
+    return -(-count // 16) * 16
+
+
 def pack_small(shards):
     width = shards[0].shape[0]
-    rows = [shards[i].reshape(1, width) for i in VECTORS]
-    rows += [shards[i].reshape(-1, width) for i in OFFSETS]
+    rows = [shards[i].reshape(-1, width) for i in VECTORS + OFFSETS]
     rows.append(shards[TAPS_AT])
-    table = shards[TABLE_AT].reshape(-1)
-    spare = -table.shape[0] % width
-    rows.append(jnp.pad(table, (0, spare)).reshape(-1, width))
-    count = sum(r.shape[0] for r in rows)
-    rows.append(jnp.zeros((-count % 16, width), rows[0].dtype))
-    return jnp.concatenate(rows, axis=0)
+    table = shards[TABLE_AT]
+    rows.append(jnp.pad(table, ((0, 0), (0, width - table.shape[1]))))
+    packed = jnp.concatenate(rows, axis=0)
+    return jnp.pad(packed, ((0, small_rows(shards) - packed.shape[0]), (0, 0)))
 
 
 def unpack_small(gathered, shards):
@@ -849,29 +950,66 @@
     full[TAPS_AT] = jnp.transpose(gathered[:, at : at + count], (1, 0, 2)).reshape(count, -1)
     at += count
     rows, cols = shards[TABLE_AT].shape
-    count = -(-rows * cols // width)
-    table = gathered[:, at : at + count].reshape(n, -1)[:, : rows * cols].reshape(n, rows, cols)
+    table = gathered[:, at : at + rows, :cols]
     full[TABLE_AT] = jnp.transpose(table, (1, 0, 2)).reshape(rows, n * cols)
     return full
 
 
-def sum_small(grads, shards):
-    n = lax.axis_size("shard")
-    order = VECTORS + OFFSETS + (TAPS_AT, TABLE_AT)
-    flat = jnp.concatenate([grads[i].reshape(-1) for i in order])
-    spare = -flat.shape[0] % 16384
-    flat = jnp.pad(flat, (0, spare)).astype(BF).reshape(-1, 1024)
-    flat = lax.psum(flat, ("rep", "shard")).astype(F32).reshape(-1)
-    z = lax.axis_index("shard")
-    found = {}
+def list_sums(grads, n):
+    table = grads[TABLE_AT]
+    width = grads[0].shape[0] // n
+    parts = jnp.transpose(table.reshape(table.shape[0], n, -1), (1, 0, 2)).reshape(n, -1)
+    parts = jnp.pad(parts, ((0, 0), (0, -parts.shape[1] % width))).reshape(n, -1, width)
+    parts = jnp.transpose(parts, (1, 0, 2)).reshape(-1, n * width)
+    return [grads[i] for i in VECTORS + OFFSETS + (TAPS_AT,)] + [parts]
+
+
+def pack_sums(smalls, n):
+    features = smalls[0].shape[0]
+    rows = []
+    for a in smalls:
+        if a.ndim == 1:
+            a = jnp.transpose(a.reshape(n, -1, features // n), (1, 0, 2)).reshape(-1, features)
+        rows.append(a)
+    return jnp.concatenate(rows, axis=0)
+
+
+def split_kernel(offset_rows, tap_rows, x_ref, *outs):
+    width = x_ref.shape[1]
     at = 0
-    for i in order:
-        size = grads[i].size
-        whole = flat[at : at + size].reshape(grads[i].shape)
-        at += size
-        axis = whole.ndim - 1
-        part = whole.shape[axis] // n
-        found[i] = lax.dynamic_slice_in_dim(whole, z * part, part, axis)
+    for i in range(len(VECTORS)):
+        outs[i][...] = x_ref[at, :]
+        at += 1
+    for i in range(len(OFFSETS)):
+        for k in range(offset_rows):
+            outs[len(VECTORS) + i][pl.ds(k * width, width)] = x_ref[at, :]
+            at += 1
+    outs[len(VECTORS) + len(OFFSETS)][...] = x_ref[at : at + tap_rows, :]
+
+
+def split_sums(summed, shards):
+    width = summed.shape[1]
+    order = VECTORS + OFFSETS + (TAPS_AT,)
+    offset_rows = shards[OFFSETS[0]].shape[0] // width
+    tap_rows = shards[TAPS_AT].shape[0]
+    if width % 128 == 0:
+        parts = pl.pallas_call(
+            functools.partial(split_kernel, offset_rows, tap_rows),
+            out_shape=[jax.ShapeDtypeStruct(shards[i].shape, F32) for i in order],
+            in_specs=[VM],
+            out_specs=[VM] * len(order),
+            name="split_sums",
+        )(summed)
+        at = sum(shards[i].size for i in order) // width
+    else:
+        parts, at = ([], 0)
+        for i in order:
+            count = shards[i].size // width
+            parts.append(summed[at : at + count].reshape(shards[i].shape))
+            at += count
+    found = dict(zip(order, parts))
+    table = shards[TABLE_AT]
+    found[TABLE_AT] = summed[at:].reshape(-1)[: table.size].reshape(table.shape)
     return found
 
 
@@ -895,11 +1033,201 @@
     )
 
 
-def conv_taps(padded, taps, local):
-    total = padded[:, 0:local] * taps[0]
-    for j in range(1, taps.shape[0]):
-        total = total + padded[:, j : j + local] * taps[j]
-    return total
+def sigmoid(values):
+    return 1.0 / (1.0 + jnp.exp(-values))
+
+
+def conv_forward_kernel(doubled_ref, rim_ref, taps_ref, gain_ref, shift_ref, depth_ref, acted_ref, padded):
+    local, features = (depth_ref.shape[1], depth_ref.shape[2])
+    rim = rim_ref.shape[1]
+    taps = taps_ref.shape[0]
+    padded[32 - rim : 32, :] = rim_ref[0].astype(F32)
+
+    def gate_rows(i, carry):
+        rows = pl.ds(pl.multiple_of(i * 32, 32), 32)
+        both = doubled_ref[0, rows, :]
+        padded[pl.ds(pl.multiple_of(32 + i * 32, 32), 32), :] = both[:, :features] * sigmoid(
+            both[:, features:]
+        )
+        return carry
+
+    lax.fori_loop(0, local // 32, gate_rows, 0)
+
+    def columns(i, carry):
+        cols = pl.ds(pl.multiple_of(i * 128, 128), 128)
+        first = 32 - (taps - 1)
+        total = padded[first : first + local, cols] * taps_ref[0:1, cols]
+        for j in range(1, taps):
+            total = total + padded[first + j : first + j + local, cols] * taps_ref[j : j + 1, cols]
+        depth_ref[0, :, cols] = total
+        return carry
+
+    lax.fori_loop(0, features // 128, columns, 0)
+
+    def norm_rows(i, carry):
+        rows = pl.ds(pl.multiple_of(i * 32, 32), 32)
+        normed = norm(depth_ref[0, rows, :], gain_ref[...], shift_ref[...])
+        acted_ref[0, rows, :] = (normed * sigmoid(normed)).astype(BF)
+        return carry
+
+    lax.fori_loop(0, local // 32, norm_rows, 0)
+
+
+def block_spec(shape):
+    return pl.BlockSpec((1,) + shape[1:], lambda b: (b,) + (0,) * (len(shape) - 1))
+
+
+def fixed_spec(shape):
+    return pl.BlockSpec(shape, lambda b: (0,) * len(shape))
+
+
+def conv_forward(doubled, rim_in, taps, gain, shift):
+    batch, local, features = (doubled.shape[0], doubled.shape[1], taps.shape[1])
+    shape = (batch, local, features)
+    return pl.pallas_call(
+        conv_forward_kernel,
+        out_shape=[jax.ShapeDtypeStruct(shape, F32), jax.ShapeDtypeStruct(shape, BF)],
+        grid=(batch,),
+        in_specs=[
+            block_spec(doubled.shape),
+            block_spec(rim_in.shape),
+            fixed_spec(taps.shape),
+            fixed_spec(gain.shape),
+            fixed_spec(shift.shape),
+        ],
+        out_specs=[block_spec(shape), block_spec(shape)],
+        scratch_shapes=[pltpu.VMEM((32 + local, features), F32)],
+        compiler_params=pltpu.CompilerParams(vmem_limit_bytes=32 << 20),
+        name="conv_forward",
+    )(doubled, rim_in, taps, gain, shift)
+
+
+def depth_backward_kernel(depth_ref, grad_ref, gain_ref, shift_ref, back_ref, sums_ref):
+    local = depth_ref.shape[1]
+
+    @pl.when(pl.program_id(0) == 0)
+    def _():
+        sums_ref[...] = jnp.zeros_like(sums_ref)
+
+    def body(i, carry):
+        rows = pl.ds(pl.multiple_of(i * 32, 32), 32)
+        values = depth_ref[0, rows, :]
+        centre, scale = statistics(values)
+        hat = (values - centre) * scale
+        gain = gain_ref[...]
+        normed = hat * gain + shift_ref[...]
+        gate = sigmoid(normed)
+        grad = grad_ref[0, rows, :] * gate * (1.0 + normed * (1.0 - gate))
+        weighed = grad * gain
+        back_ref[0, rows, :] = (
+            weighed
+            - jnp.mean(weighed, axis=-1, keepdims=True)
+            - hat * jnp.mean(weighed * hat, axis=-1, keepdims=True)
+        ) * scale
+        sums_ref[0:1, :] += jnp.sum(grad * hat, axis=0, keepdims=True)
+        sums_ref[1:2, :] += jnp.sum(grad, axis=0, keepdims=True)
+        return carry
+
+    lax.fori_loop(0, local // 32, body, 0)
+
+
+def depth_backward(depth, grad, gain, shift):
+    return pl.pallas_call(
+        depth_backward_kernel,
+        out_shape=[
+            jax.ShapeDtypeStruct(depth.shape, F32),
+            jax.ShapeDtypeStruct((8, depth.shape[2]), F32),
+        ],
+        grid=(depth.shape[0],),
+        in_specs=[
+            block_spec(depth.shape),
+            block_spec(grad.shape),
+            fixed_spec(gain.shape),
+            fixed_spec(shift.shape),
+        ],
+        out_specs=[block_spec(depth.shape), fixed_spec((8, depth.shape[2]))],
+        compiler_params=pltpu.CompilerParams(vmem_limit_bytes=32 << 20),
+        name="depth_backward",
+    )(depth, grad, gain, shift)
+
+
+def conv_backward_kernel(
+    back_ref, after_ref, doubled_ref, rim_ref, taps_ref, out_ref, dtaps_ref, padded, behind
+):
+    local, features = (back_ref.shape[1], back_ref.shape[2])
+    rim = rim_ref.shape[1]
+    taps = taps_ref.shape[0]
+
+    @pl.when(pl.program_id(0) == 0)
+    def _():
+        dtaps_ref[...] = jnp.zeros_like(dtaps_ref)
+
+    padded[32 - rim : 32, :] = rim_ref[0].astype(F32)
+    behind[local : local + rim, :] = after_ref[0].astype(F32)
+
+    def gate_rows(i, carry):
+        rows = pl.ds(pl.multiple_of(i * 32, 32), 32)
+        both = doubled_ref[0, rows, :]
+        padded[pl.ds(pl.multiple_of(32 + i * 32, 32), 32), :] = both[:, :features] * sigmoid(
+            both[:, features:]
+        )
+        behind[rows, :] = back_ref[0, rows, :]
+        return carry
+
+    lax.fori_loop(0, local // 32, gate_rows, 0)
+
+    def columns(i, carry):
+        cols = pl.ds(pl.multiple_of(i * 128, 128), 128)
+        first = 32 - (taps - 1)
+        own = back_ref[0, :, cols]
+        total = own * taps_ref[taps - 1 : taps, cols]
+        dtaps_ref[taps - 1 : taps, cols] += jnp.sum(
+            own * padded[first + taps - 1 : first + taps - 1 + local, cols], axis=0, keepdims=True
+        )
+        for j in range(taps - 1):
+            ahead = taps - 1 - j
+            total = total + behind[ahead : ahead + local, cols] * taps_ref[j : j + 1, cols]
+            dtaps_ref[j : j + 1, cols] += jnp.sum(
+                own * padded[first + j : first + j + local, cols], axis=0, keepdims=True
+            )
+        side = doubled_ref[0, :, cols]
+        gate = sigmoid(doubled_ref[0, :, pl.ds(pl.multiple_of(features + i * 128, 128), 128)])
+        gated = total * gate
+        out_ref[0, :, cols] = gated.astype(BF)
+        out_ref[0, :, pl.ds(pl.multiple_of(features + i * 128, 128), 128)] = (
+            gated * side * (1.0 - gate)
+        ).astype(BF)
+        return carry
+
+    lax.fori_loop(0, features // 128, columns, 0)
+
+
+def conv_backward(back, after, doubled, rim_in, taps):
+    batch, local, features = back.shape
+    padded_taps = (-(-taps.shape[0] // 8) * 8, features)
+    found, dtaps = pl.pallas_call(
+        conv_backward_kernel,
+        out_shape=[
+            jax.ShapeDtypeStruct(doubled.shape, BF),
+            jax.ShapeDtypeStruct(padded_taps, F32),
+        ],
+        grid=(batch,),
+        in_specs=[
+            block_spec(back.shape),
+            block_spec(after.shape),
+            block_spec(doubled.shape),
+            block_spec(rim_in.shape),
+            fixed_spec(taps.shape),
+        ],
+        out_specs=[block_spec(doubled.shape), fixed_spec(padded_taps)],
+        scratch_shapes=[
+            pltpu.VMEM((32 + local, features), F32),
+            pltpu.VMEM((32 + local, features), F32),
+        ],
+        compiler_params=pltpu.CompilerParams(vmem_limit_bytes=32 << 20),
+        name="conv_backward",
+    )(back, after, doubled, rim_in, taps)
+    return found, dtaps[: taps.shape[0]]
 
 
 def on_device(*arguments):
@@ -921,10 +1249,11 @@
     def whole_of(rows):
         return jnp.transpose(rows.reshape(micro, seqs, local, features), (0, 2, 1, 3))
 
-    small = pack_small(shards)
     if fast:
-        full, gathered = gather_fast([shards[i] for i in MATRICES], small)
+        smalls = [shards[i] for i in SMALLS]
+        full, gathered = gather_fast([shards[i] for i in MATRICES], smalls, small_rows(shards))
     else:
+        small = pack_small(shards)
         full = [lax.all_gather(shards[i], "shard", axis=0, tiled=True) for i in MATRICES]
         gathered = lax.all_gather(small, "shard", axis=0, tiled=False)
     w = dict(zip(MATRICES, full))
@@ -948,16 +1277,14 @@
 
     conv_in = norm(level2, w[16], w[17]).astype(BF)
     doubled = times(conv_in, w[18])
-    side_a, side_b = (doubled[:, :features], doubled[:, features:])
-    gate = jax.nn.sigmoid(side_b)
-    gated = (side_a * gate).reshape(batch, local, features)
+    doubled = doubled.reshape(batch, local, 2 * features)
     taps = w[TAPS_AT].astype(F32)
     rim = taps.shape[0] - 1
-    rim_in = shifted(gated[:, local - rim :].astype(BF), "rep", 1).astype(F32)
-    padded = jnp.concatenate([rim_in, gated], axis=1)
-    depth = conv_taps(padded, taps, local).reshape(batch * local, features)
-    depth_normed = norm(depth, w[20], w[21])
-    acted = swish(depth_normed).astype(BF)
+    edge = doubled[:, local - rim :]
+    edge = (edge[:, :, :features] * jax.nn.sigmoid(edge[:, :, features:])).astype(BF)
+    rim_in = shifted(edge, "rep", 1)
+    depth, acted = conv_forward(doubled, rim_in, taps, w[20][None], w[21][None])
+    acted = acted.reshape(batch * local, features)
     level3 = level2 + times(acted, w[22])
 
     level4, later = feed_forward(level3, w[23], w[24], w[25], w[26], w[27], w[28])
@@ -970,18 +1297,12 @@
     grads[23], grads[24], grads[26], grads[28] = found
 
     conv_out = back3.astype(BF)
-    depth_mid = times_back(conv_out, w[22]) * swish_slope(depth_normed)
-    depth_back, grads[20], grads[21] = norm_back(depth, w[20], depth_mid)
-    depth_back = depth_back.reshape(batch, local, features)
-    rim_back = shifted(depth_back[:, :rim].astype(BF), "rep", -1).astype(F32)
-    after = jnp.concatenate([depth_back, rim_back], axis=1)
-    grads[TAPS_AT] = jnp.stack(
-        [jnp.sum(depth_back * padded[:, j : j + local], axis=(0, 1)) for j in range(rim + 1)]
-    )
-    gated_back = conv_taps(after, taps[::-1], local).reshape(batch * local, features)
-    doubled_back = jnp.concatenate(
-        [gated_back * gate, gated_back * side_a * gate * (1.0 - gate)], axis=1
-    ).astype(BF)
+    acted_grad = times_back(conv_out, w[22]).reshape(batch, local, features)
+    depth_back, sums = depth_backward(depth, acted_grad, w[20][None], w[21][None])
+    grads[20], grads[21] = (sums[0], sums[1])
+    after = shifted(depth_back[:, :rim].astype(BF), "rep", -1)
+    doubled_back, grads[TAPS_AT] = conv_backward(depth_back, after, doubled, rim_in, taps)
+    doubled_back = doubled_back.reshape(batch * local, 2 * features)
     conv_back = times_back(doubled_back, w[18])
     back, grads[16], grads[17] = norm_back(level2, w[16], conv_back)
     back2 = back3 + back
@@ -1027,8 +1348,9 @@
         (2, early_pairs[1]),
     )
     reduce = reduce_fast if fast else reduce_plain
-    summed = dict(zip([i for i, _ in pairs], reduce([pair for _, pair in pairs])))
-    summed.update(sum_small(grads, shards))
+    matrices, smalls = reduce([pair for _, pair in pairs], list_sums(grads, n_shard))
+    summed = dict(zip([i for i, _ in pairs], matrices))
+    summed.update(split_sums(smalls, shards))
     return (whole_of(output), whole_of(back0)) + tuple(summed[i] for i in range(31))
 
 

time: 884 us -> 699 us (0.79)
  waiting for transfers between devices: 99.2 us -> 2.09 us
  local copies, waits for them, and re-layouts: 81 us -> 20.3 us
  other arithmetic: 86 us -> 40.2 us
  Pallas kernels: 525 us -> 562 us
  between operations: 17.5 us -> 1.92 us
    psum x1 -> x0, waiting for transfers between devices: 98.4 us -> none  [sum_small(): flat = lax.psum(flat, ('rep', 'shard')).astype(F32).reshape(-1)]
    pallas_call x1 -> x5, Pallas kernels: 176 us -> 203 us  [the longest x1 180 us: gather_fast(): pl.pallas_call(functools.partial(gather_kernel, chunks, count, len(smalls...]
    reduce_sum x2 -> x1, other arithmetic: 21.5 us -> 0.15 us  [statistics(): centre = jnp.mean(values, axis=-1, keepdims=True)]
    unnamed x380 -> x105, local copies, waits for them, and re-layouts: 30.2 us -> 9.48 us
    add x1 -> x0, other arithmetic: 20.5 us -> none  [conv_taps(): total = total + padded[:, j:j + local] * taps[j]]
    reshape x25 -> x2, local copies, waits for them, and re-layouts: 14.3 us -> 0.76 us  [the longest x1 0.63 us: list_sums(): jnp.pad(parts, ((0, 0), (0, -parts.shape[1] % width))).reshape(n, -1, width)]
    dynamic_slice x21 -> x0, local copies, waits for them, and re-layouts: 11.5 us -> none  [sum_small(): found[i] = lax.dynamic_slice_in_dim(whole, z * part, part, axis)]
    slice x12 -> x5, local copies, waits for them, and re-layouts: 11.4 us -> 1.41 us  [the longest x3 0.78 us: split_sums(): found[TABLE_AT] = summed[at:].reshape(-1)[:table.size].reshape(table.shape)]
  transfers between devices with their start and end apart: 3 -> 2, of which waited for: 2 -> 1; matrix products, arithmetic and copies ran while one was open for 3% -> 0% of each run, Pallas kernels for 0% -> 0%
where the time goes in v2:
time: 699 us; the launch traced here: 691 us
  Pallas kernels  562 us (80%)
  matrix products  61.2 us (9%)
  other arithmetic  40.2 us (6%)
  local copies, waits for them, and re-layouts  20.3 us (3%)
    pallas_call x1, Pallas kernels, reduce_fast(): pl.pallas_call(functools.partial(reduce_kernel, groups, units, len(lefts)...  236 us
    pallas_call x1, Pallas kernels, gather_fast(): pl.pallas_call(functools.partial(gather_kernel, chunks, count, len(smalls...  180 us
    pallas_call x4, Pallas kernels, swap(): pl.pallas_call(functools.partial(swap_kernel, n), out_shape=jax.ShapeDtyp...  63.9 us
    pallas_call x1, Pallas kernels, attention_backward(): pl.pallas_call(backward_kernel, out_shape=[shape, shape, shape, jax.Shape...  39 us
    dot_general x10, matrix products, times_back(): lax.dot_general(left, right, (((1,), (1,)), ((), ())), preferred_element_...  34.4 us
    dot_general x10, matrix products, times(): return jnp.dot(left, right, preferred_element_type=F32)  26.9 us
    convert_element_type x10, other arithmetic, reduce_fast(): w.reshape(-1, w.shape[-1]).astype(F32)  20.3 us
    pallas_call x1, Pallas kernels, attention_forward(): pl.pallas_call(forward_kernel, out_shape=[shape, shape], grid=(batch, tot...  19.4 us
  transfers between devices with their start and end apart: 2, of which 1 were waited for; matrix products, arithmetic and copies ran while one was open for 0% of the time, Pallas kernels for 0%

profile of v2, /device:TPU:0, one launch (start us, length us, event | category | flops | bytes accessed | tf_op | source)
XLA Modules:
  0.0 690.9 jit_solution(10657722492393776642)
XLA Ops:
  0.7 1.4 copy.110.refs_30_
  2.1 180.2 %gather_weights.1 = (bf16[2,2,2,2,2,2,16,4096]{7,6,5,4,3,2,1,0:T(8,128)(2,1)}, bf16[2,2,2,2,2,2,64,1024]{7,6,5,4,3,2,1,0:T(8,128)(2,1)}, bf16[2,2,2,2,2,2,16,102...) custom-call(bf16[2,2,2,2,16,4096]{5,4,3,2,1,0:T(8,128)(2,1)} %bitcas, ...), custom_call_target="tpu_custom_call" | custom-call | tf_op jit(solution)/shard_map/gather_weights/pallas_call | solution.py:201
  182.3 0.8 convert_bitcast_fusion.1
  183.1 1.3 slice_convert_fusion.2
  184.4 0.9 slice_bitcast_fusion.6
  187.1 1.5 gather_fusion
  189.3 8.2 %multiply_convert_fusion.1 = (bf16[256,4096]{1,0:T(8,128)(2,1)S(1)}, f32[256,4096]{1,0:T(8,128)}) fusion(f32[4096]{0:T(1024)S(1)} %bitcast.414, bf16[256,1024]{1,0:T(8,128)(2,1)S(1)} %bitcast.378, bf16[1024,4096]{1,0:T(8,128)(2,1)} %bitcast.420), kind=kOutput, calls=%fused_computation.11 | convolution fusion | flops 2153775104 | bytes 15220736 | tf_op jit(solution)/shard_map/dot_general | solution.py:900
  197.5 2.5 fusion.31
  204.2 20.9 %swap_0.1 = bf16[8,3,2,128,128]{4,3,2,1,0:T(8,128)(2,1)S(1)} custom-call(bf16[8,3,2,128,128]{4,3,2,1,0:T(8,128)(2,1)S(1)} %pad_maximum_fusion.x_ref), custom_call_target="tpu_custom_call" | custom-call | tf_op jit(solution)/shard_map/swap_0/pallas_call | solution.py:615
  225.5 19.4 %attention_forward.1 = (f32[2,1024,128]{2,1,0:T(8,128)S(1)}, f32[2,1024,128]{2,1,0:T(8,128)S(1)}) custom-call(bf16[2,1024,128]{2,1,0:T(8,128)(2,1)S(1)} %bitcast.314, bf16[2,1024,128]{2,1,0:T(8,128)(2,1)S(1)} %bitcast.312, bf16[2,1024,128]{2,1,0:T(8,128)(2,1)S(1)} %bitcast.310, bf16[512,128]{1,0:T(8,128)(2,1)S(1)} %copy.120.table_ref), custom_call_target="tpu_custom_call" | custom-call | tf_op jit(solution)/shard_map/attention_forward/pallas_call | solution.py:716
  245.1 9.3 %swap_1.1 = bf16[8,1,2,128,128]{4,3,2,1,0:T(8,128)(2,1)S(1)} custom-call(bf16[8,1,2,128,128]{4,3,2,1,0:T(8,128)(2,1)S(1)} %bitcast.319), custom_call_target="tpu_custom_call" | custom-call | tf_op jit(solution)/shard_map/swap_1/pallas_call | solution.py:615
  254.7 0.8 fusion.32
  256.5 1.3 fusion.35.doubled_ref
  257.9 2.4 collective-permute-start
  260.3 0.9 convert_bitcast_fusion
  261.2 0.9 copy.174
  263.1 7.9 %conv_forward.1 = (f32[2,128,1024]{2,1,0:T(8,128)S(1)}, bf16[2,128,1024]{2,1,0:T(8,128)(2,1)S(1)}) custom-call(f32[2,128,2048]{2,1,0:T(8,128)S(1)} %fusion.35.doubled_ref, bf16[2,30,1024]{2,1,0:T(8,128)(2,1)S(1)} %collective-permute-done.rim_ref, f32[31,1024]{1,0:T(8,128)S(1)} %bitcast.323, f32[1,1024]{1,0:T(1,128)S(1)} %convert.37.gain_ref, ...), custom_call_target="tpu_custom_call" | custom-call | tf_op jit(solution)/shard_map/conv_forward/pallas_call | solution.py:1087
  271.0 0.8 fusion.33
  272.4 4.6 multiply_convert_fusion
  277.0 6.6 fusion.34
  283.9 1.0 fusion.19
  284.9 1.8 convert_reduce_fusion.3
  286.7 8.3 %convert_reduce_fusion = (f32[4096]{0:T(1024)}, bf16[256,4096]{1,0:T(8,128)(2,1)S(1)}) fusion(f32[256,4096]{1,0:T(8,128)} %get-tuple-element.314, bf16[256,1024]{1,0:T(8,128)(2,1)} %get-tuple-element.263.refs_8_, bf16[4096,1024]{1,0:T(8,128)(2,1)} %bitcast.433), kind=kOutput, calls=%fused_computation.7 | convolution fusion | flops 2159013888 | bytes 15220736 | tf_op jit(solution)/shard_map/dot_general | solution.py:904
  295.1 7.4 %multiply_reduce_fusion = (f32[1024]{0:T(1024)}, f32[256]{0:T(256)S(1)}, f32[256]{0:T(256)S(1)}, f32[1024]{0:T(1024)}, f32[256,1024]{1,0:T(8,128)S(1)}) fusion(f32[256,1024]{1,0:T(8,128)S(1)} %get-tuple-element.312, f32[256]{0:T(256)S(1)} %add_rsqrt_fusion.1, f32[256]{0:T(256)S(1)} %broadcast_multiply_fusion.10, f32[1024]{0:T(1024)S(1)} %bitcast.392, ...), kind=kOutput, calls=%fused_computation.55 | convolution fusion | flops 2149840384 | bytes 12599296 | tf_op jit(solution)/shard_map/dot_general | solution.py:904
  302.5 2.0 fusion.29
  304.5 0.7 fusion.36.grad_ref
  305.3 3.0 depth_backward.1
  308.3 1.3 collective-permute-start.1
  310.2 2.1 collective-permute-done.1.after_ref
  312.3 10.6 %conv_backward.1 = (bf16[2,128,2048]{2,1,0:T(8,128)(2,1)S(1)}, f32[32,1024]{1,0:T(8,128)S(1)}) custom-call(f32[2,128,1024]{2,1,0:T(8,128)S(1)} %get-tuple-element.101.back_ref, bf16[2,30,1024]{2,1,0:T(8,128)(2,1)S(1)} %collective-permute-done.1.after_ref, f32[2,128,2048]{2,1,0:T(8,128)S(1)} %fusion.35.doubled_ref, ...), custom_call_target="tpu_custom_call" | custom-call | tf_op jit(solution)/shard_map/conv_backward/pallas_call | solution.py:1208
  322.9 2.1 multiply_reduce_fusion.1
  325.0 2.0 convert_reduce_fusion.4
  327.0 0.7 fusion.12
  328.0 13.2 %swap_2.1 = bf16[8,1,2,128,128]{4,3,2,1,0:T(8,128)(2,1)S(1)} custom-call(bf16[8,1,2,128,128]{4,3,2,1,0:T(8,128)(2,1)S(1)} %bitcast.321), custom_call_target="tpu_custom_call" | custom-call | tf_op jit(solution)/shard_map/swap_2/pallas_call | solution.py:615
  341.3 39.0 %attention_backward.1 = (bf16[2,1024,128]{2,1,0:T(8,128)(2,1)S(1)}, bf16[2,1024,128]{2,1,0:T(8,128)(2,1)S(1)}, bf16[2,1024,128]{2,1,0:T(8,128)(2,1)S(1)}, f32[512,128]{1,0:T(8,128)S(1)}) custom-call(bf16[2,1024,128]{2,1,0:T(8,128)(2,1)S(1)} %bitcast.315, bf16[2,1024,128]{2,1,0:T(8,128)(2,1)S(1)} %bitcast.313, bf16[2,1024,128]{2,1,0:T(8,128)(2,1)S(1)} %bitcast.311, ...), custom_call_target="tpu_custom_call" | custom-call | tf_op jit(solution)/shard_map/attention_backward/pallas_call | solution.py:841
  380.2 0.8 copy.133
  381.1 1.0 reduce_sum.452
  382.9 20.5 %swap_3.1 = bf16[8,3,2,128,128]{4,3,2,1,0:T(8,128)(2,1)S(1)} custom-call(bf16[8,3,2,128,128]{4,3,2,1,0:T(8,128)(2,1)S(1)} %pad_maximum_fusion.1.x_ref), custom_call_target="tpu_custom_call" | custom-call | tf_op jit(solution)/shard_map/swap_3/pallas_call | solution.py:615
  403.4 0.7 convert_reduce_fusion.5
  404.1 0.9 slice_bitcast_fusion
  405.4 0.8 fusion.28
  406.2 0.9 copy.173
  408.4 1.5 copy.132
  409.9 0.9 copy.171
  411.2 0.9 copy.172
  412.1 0.8 convolution_add_fusion.3
  412.9 1.6 multiply_reduce_fusion.2
  414.6 1.0 convert_reduce_fusion.7
  415.6 7.5 %convert_reduce_fusion.1 = (f32[4096]{0:T(1024)}, bf16[256,4096]{1,0:T(8,128)(2,1)S(1)}) fusion(f32[256,4096]{1,0:T(8,128)S(1)} %copy-done.38, bf16[256,1024]{1,0:T(8,128)(2,1)S(1)} %get-tuple-element.268.refs_16_, bf16[4096,1024]{1,0:T(8,128)(2,1)} %bitcast.424), kind=kOutput, calls=%fused_computation.8 | convolution fusion | flops 2159013888 | bytes 15220736 | tf_op jit(solution)/shard_map/dot_general | solution.py:904
  423.1 4.4 multiply_reduce_fusion.3
  427.5 236.0 %reduce_grads.1 = (bf16[4,2,2,2,2,16,1024]{6,5,4,3,2,1,0:T(8,128)(2,1)}, bf16[2,2,2,2,16,4096]{5,4,3,2,1,0:T(8,128)(2,1)}, bf16[2,2,2,2,16,1024]{5,4,3,2,1,0:T(8...) custom-call(bf16[256,4096]{1,0:T(8,128)(2,1)} %copy-done.11, ...), custom_call_target="tpu_custom_call" | custom-call | tf_op jit(solution)/shard_map/reduce_grads/pallas_call | solution.py:543
  664.2 1.5 split_sums.1
  665.8 1.7 multiply_add_fusion
  667.5 2.0 copy.138
  670.3 2.1 bitcast_convert_fusion.9
  672.4 1.1 bitcast_convert_fusion.8
  673.6 1.1 bitcast_convert_fusion.7
  674.7 1.1 bitcast_convert_fusion.6
  675.8 1.1 bitcast_convert_fusion.5
  676.9 4.2 bitcast_convert_fusion.3
  681.2 1.6 bitcast_convert_fusion.4
  682.8 2.6 bitcast_convert_fusion.2
  685.4 2.6 bitcast_convert_fusion.1
  688.1 2.6 bitcast_convert_fusion
  (185 shorter events, 15.3 us)
Async XLA Ops:
  2.1 183.2 %copy-start.4 = (bf16[2,128,1,1024]{3,1,2,0:T(8,128)(2,1)S(1)}, bf16[2,128,1,1024]{3,1,2,0:T(8,128)(2,1)}, u32[]{:S(2)}) copy-start(bf16[2,128,1,1024]{3,1,2,0:T(8,128)(2,1)} %param.33) | copy-start | bytes 1572868
  189.0 8.5 %slice-start.2 = ((s8[8388608]{0:T(1024)(128)(4,1)}), s8[4194304]{0:T(1024)(128)(4,1)S(1)}, s32[]{:S(2)}) async-start(s8[8388608]{0:T(1024)(128)(4,1)} %bitcast.425), calls=%async_computation.2 | async-start | bytes 8388608
  189.3 8.2 %slice-start.3 = ((s8[8388608]{0:T(1024)(128)(4,1)}), s8[4194304]{0:T(1024)(128)(4,1)S(1)}, s32[]{:S(2)}) async-start(s8[8388608]{0:T(1024)(128)(4,1)} %bitcast.425), calls=%async_computation.3 | async-start | bytes 8388608
  197.5 2.5 copy-start.10
  197.5 3.0 copy-start.36
  200.0 1.8 copy-start.17
  200.3 2.2 copy-start.32
  200.5 2.1 copy-start.19
  201.3 1.7 copy-start.21
  225.4 29.3 %copy-start.23 = (bf16[2,2,2,2,2,2,16,1024]{7,6,5,4,3,2,1,0:T(8,128)(2,1)S(1)}, bf16[2,2,2,2,2,2,16,1024]{7,6,5,4,3,2,1,0:T(8,128)(2,1)}, u32[]{:S(2)}) copy-start(bf16[2,2,2,2,2,2,16,1024]{7,6,5,4,3,2,1,0:T(8,128)(2,1)} %get-tuple-element.94) | copy-start | bytes 6291460
  254.3 2.2 copy-start.8
  256.1 6.0 copy-start.7
  256.5 5.8 copy-start.5
  256.5 15.8 %slice-start.4 = ((s8[8388608]{0:T(1024)(128)(4,1)}), s8[4194304]{0:T(1024)(128)(4,1)S(1)}, s32[]{:S(2)}) async-start(s8[8388608]{0:T(1024)(128)(4,1)} %bitcast.429), calls=%async_computation.4 | async-start | bytes 8388608
  257.8 13.2 %copy-start.3 = (bf16[2,2,2,2,2,2,16,1024]{7,6,5,4,3,2,1,0:T(8,128)(2,1)S(1)}, bf16[2,2,2,2,2,2,16,1024]{7,6,5,4,3,2,1,0:T(8,128)(2,1)}, u32[]{:S(2)}) copy-start(bf16[2,2,2,2,2,2,16,1024]{7,6,5,4,3,2,1,0:T(8,128)(2,1)} %get-tuple-element.97) | copy-start | bytes 6291460
  257.9 5.1 collective-permute-start
  262.3 10.1 %slice-start.5 = ((s8[8388608]{0:T(1024)(128)(4,1)}), s8[4194304]{0:T(1024)(128)(4,1)S(1)}, s32[]{:S(2)}) async-start(s8[8388608]{0:T(1024)(128)(4,1)} %bitcast.429), calls=%async_computation.5 | async-start | bytes 8388608
  271.0 6.0 copy-start
  272.4 4.7 copy-start.20
  277.0 6.6 copy-start.11
  295.1 7.4 %copy-start.12 = (bf16[256,4096]{1,0:T(8,128)(2,1)}, bf16[256,4096]{1,0:T(8,128)(2,1)S(1)}, u32[]{:S(2)}) copy-start(bf16[256,4096]{1,0:T(8,128)(2,1)S(1)} %get-tuple-element.324.refs_9_) | copy-start | bytes 6291460
  304.5 5.7 copy-start.6
  308.3 4.0 collective-permute-start.1
  322.9 2.1 copy-start.1
  322.9 2.1 copy-start.2
  325.0 2.0 copy-start.24
  327.0 14.2 %copy-start.25 = (bf16[256,1024]{1,0:T(8,128)(2,1)}, bf16[256,1024]{1,0:T(8,128)(2,1)S(1)}, u32[]{:S(2)}) copy-start(bf16[256,1024]{1,0:T(8,128)(2,1)S(1)} %get-tuple-element.265.refs_12_) | copy-start | bytes 1572868
  382.9 22.6 %copy-start.18 = (bf16[2,2,2,2,2,2,16,1024]{7,6,5,4,3,2,1,0:T(8,128)(2,1)S(1)}, bf16[2,2,2,2,2,2,16,1024]{7,6,5,4,3,2,1,0:T(8,128)(2,1)}, u32[]{:S(2)}) copy-start(bf16[2,2,2,2,2,2,16,1024]{7,6,5,4,3,2,1,0:T(8,128)(2,1)} %get-tuple-element.90) | copy-start | bytes 6291460
  408.4 3.7 copy-start.22
  409.9 3.0 copy-start.33
  409.9 3.0 copy-start.37
  412.1 2.5 copy-start.9
  412.9 2.7 copy-start.38
  414.6 8.5 %slice-start = ((s8[8388608]{0:T(1024)(128)(4,1)}), s8[4194304]{0:T(1024)(128)(4,1)S(1)}, s32[]{:S(2)}) async-start(s8[8388608]{0:T(1024)(128)(4,1)} %bitcast.421), calls=%async_computation | async-start | bytes 8388608
  415.6 7.5 %copy-start.26 = (bf16[256,1024]{1,0:T(8,128)(2,1)}, bf16[256,1024]{1,0:T(8,128)(2,1)S(1)}, u32[]{:S(2)}) copy-start(bf16[256,1024]{1,0:T(8,128)(2,1)S(1)} %get-tuple-element.268.refs_16_) | copy-start | bytes 1572868
  415.6 7.5 %copy-start.34 = (f32[256]{0:T(256)S(1)}, f32[256]{0:T(256)}, u32[]{:S(2)}) copy-start(f32[256]{0:T(256)} %get-tuple-element.301) | copy-start | bytes 3076
  415.6 7.5 %copy-start.35 = (f32[256]{0:T(256)S(1)}, f32[256]{0:T(256)}, u32[]{:S(2)}) copy-start(f32[256]{0:T(256)} %get-tuple-element.303) | copy-start | bytes 3076
  415.6 7.5 %slice-start.1 = ((s8[8388608]{0:T(1024)(128)(4,1)}), s8[4194304]{0:T(1024)(128)(4,1)S(1)}, s32[]{:S(2)}) async-start(s8[8388608]{0:T(1024)(128)(4,1)} %bitcast.421), calls=%async_computation.1 | async-start | bytes 8388608
  423.1 4.4 copy-start.16
  665.8 7.8 %copy-start.30 = (bf16[2,2,2,2,16,1024]{5,4,3,2,1,0:T(8,128)(2,1)S(1)}, bf16[2,2,2,2,16,1024]{5,4,3,2,1,0:T(8,128)(2,1)}, u32[]{:S(2)}) copy-start(bf16[2,2,2,2,16,1024]{5,4,3,2,1,0:T(8,128)(2,1)} %get-tuple-element.122) | copy-start | bytes 1572868
  667.5 5.0 copy-start.31
  667.5 7.2 %copy-start.29 = (bf16[2,2,2,2,16,1024]{5,4,3,2,1,0:T(8,128)(2,1)S(1)}, bf16[2,2,2,2,16,1024]{5,4,3,2,1,0:T(8,128)(2,1)}, u32[]{:S(2)}) copy-start(bf16[2,2,2,2,16,1024]{5,4,3,2,1,0:T(8,128)(2,1)} %get-tuple-element.124) | copy-start | bytes 1572868
  667.5 8.3 %copy-start.28 = (bf16[2,2,2,2,16,1024]{5,4,3,2,1,0:T(8,128)(2,1)S(1)}, bf16[2,2,2,2,16,1024]{5,4,3,2,1,0:T(8,128)(2,1)}, u32[]{:S(2)}) copy-start(bf16[2,2,2,2,16,1024]{5,4,3,2,1,0:T(8,128)(2,1)} %get-tuple-element.132) | copy-start | bytes 1572868
  675.8 5.4 copy-start.27
  676.9 5.9 copy-start.15
  681.2 4.3 copy-start.14
  685.4 2.7 copy-start.13

commit v3 on v2

--- a/solution.py
+++ b/solution.py
@@ -47,7 +47,7 @@
     pl.semaphore_wait(barrier, len(peers))
 
 
-GATHER_LAG = (0, 2, 3, 4, 5)
+GATHER_LAG = (0, 1, 2, 3, 4)
 
 
 def fill_rows(packed, smalls):
@@ -71,8 +71,6 @@
     ssem, rsem, lsem, lsem2, qsem, psem, packed, small = refs[n_arr + 1 : n_arr + 9]
     bufs = refs[n_arr + 9 :]
     z, core, x, y, z0, z1, peers = here()
-    fill_rows(packed, smalls)
-    small[...] = packed[...].astype(BF)
     far = ((slice(None), 1 - z0), (1 - z1, z0))
     meet(peers)
     sent = []
@@ -91,19 +89,6 @@
         return copy
 
     around = []
-    for k, to in enumerate(("z0", "z1", "zz")):
-        copy = pltpu.make_async_remote_copy(
-            src_ref=small,
-            dst_ref=small_out.at[z],
-            send_sem=qsem.at[k],
-            recv_sem=psem.at[k],
-            device_id=peers[to],
-            device_id_type=MESH,
-        )
-        copy.start()
-        around.append(copy)
-    small_own = pltpu.make_async_copy(small, small_out.at[z], lsem.at[n_arr])
-    small_own.start()
     state = {}
 
     def place(c):
@@ -166,7 +151,22 @@
                 copy = pltpu.make_async_copy(ins[a], bufs[a], lsem.at[a])
                 copy.start()
                 local.append(copy)
-        if step == 3:
+            fill_rows(packed, smalls)
+            small[...] = packed[...].astype(BF)
+            for k, to in enumerate(("z0", "z1", "zz")):
+                copy = pltpu.make_async_remote_copy(
+                    src_ref=small,
+                    dst_ref=small_out.at[z],
+                    send_sem=qsem.at[k],
+                    recv_sem=psem.at[k],
+                    device_id=peers[to],
+                    device_id_type=MESH,
+                )
+                copy.start()
+                around.append(copy)
+            small_own = pltpu.make_async_copy(small, small_out.at[z], lsem.at[n_arr])
+            small_own.start()
+        if step == 2:
             for a in range(n_arr):
                 local[a].wait()
                 copy = pltpu.make_async_copy(bufs[a], outs[a].at[z1, z0], lsem2.at[a])
@@ -584,20 +584,22 @@
     return grads, lax.dynamic_slice_in_dim(summed, lax.axis_index("shard") * width, width, 1)
 
 
-def swap_kernel(n, x_ref, o_ref, ssem, rsem):
+def greet(n):
     rep = lax.axis_index("rep")
+    others = [jnp.bitwise_xor(rep, d) for d in range(1, n)]
     barrier = pltpu.get_barrier_semaphore()
-    for d in range(1, n):
-        pl.semaphore_signal(
-            barrier, inc=1, device_id={"rep": jnp.bitwise_xor(rep, d)}, device_id_type=MESH
-        )
+    for other in others:
+        pl.semaphore_signal(barrier, inc=1, device_id={"rep": other}, device_id_type=MESH)
     pl.semaphore_wait(barrier, n - 1)
+    return rep, others
+
+
+def send_all(others, src_of, dst, ssem, rsem):
     copies = []
-    for d in range(1, n):
-        other = jnp.bitwise_xor(rep, d)
+    for d, other in enumerate(others):
         copy = pltpu.make_async_remote_copy(
-            src_ref=x_ref.at[other],
-            dst_ref=o_ref.at[rep],
+            src_ref=src_of(other),
+            dst_ref=dst,
             send_sem=ssem.at[d],
             recv_sem=rsem.at[d],
             device_id={"rep": other},
@@ -605,24 +607,7 @@
         )
         copy.start()
         copies.append(copy)
-    o_ref[rep] = x_ref[rep]
-    for copy in copies:
-        copy.wait()
-
-
-def swap(array, which):
-    n = array.shape[0]
-    return pl.pallas_call(
-        functools.partial(swap_kernel, n),
-        out_shape=jax.ShapeDtypeStruct(array.shape, array.dtype),
-        in_specs=[VM],
-        out_specs=VM,
-        scratch_shapes=[pltpu.SemaphoreType.DMA((n,)), pltpu.SemaphoreType.DMA((n,))],
-        compiler_params=pltpu.CompilerParams(
-            collective_id=2 + which, has_side_effects=True, vmem_limit_bytes=32 << 20
-        ),
-        name="swap_%d" % which,
-    )(array)
+    return copies
 
 
 def to_heads(arrays, n):
@@ -630,22 +615,6 @@
     parts = [a.reshape(batch, local, n, features // n) for a in arrays]
     stacked = jnp.stack([jnp.transpose(p, (2, 0, 1, 3)) for p in parts], axis=1)
     return stacked
-
-
-def from_positions(swapped):
-    n, k, batch, local, width = swapped.shape
-    return [
-        jnp.transpose(swapped[:, i], (1, 0, 2, 3)).reshape(batch, n * local, width)
-        for i in range(k)
-    ]
-
-
-def to_positions(arrays, n):
-    batch, total, width = arrays[0].shape
-    parts = [
-        jnp.transpose(a.reshape(batch, n, total // n, width), (1, 0, 2, 3)) for a in arrays
-    ]
-    return jnp.stack(parts, axis=1)
 
 
 def from_heads(swapped):
@@ -656,9 +625,6 @@
     ]
 
 
-QROWS = 128
-
-
 def head_mask(shape, head):
     lane = lax.broadcasted_iota(jnp.int32, shape, 1)
     return jnp.logical_and(lane >= head * HD, lane < (head + 1) * HD)
@@ -672,99 +638,140 @@
     bias[:, pl.ds(pl.multiple_of(block * 128, 128), 384)] = rolled[:, 0:384]
 
 
-def forward_kernel(q_ref, k_ref, v_ref, table_ref, mixed_ref, lse_ref, bias):
-    step = pl.program_id(1)
-    total, width = (k_ref.shape[1], k_ref.shape[2])
-    heads = width // HD
-    keys = k_ref[0]
-    values = v_ref[0]
-    ones = jnp.ones((total, 128), BF)
-    wide_values = jnp.concatenate([values, ones], axis=1) if width == 128 else None
-    for sub in range(QROWS // 128):
-        rows = slice(sub * 128, (sub + 1) * 128)
-        query = q_ref[0, rows, :] * jnp.asarray(0.125, BF)
-        block = step * (QROWS // 128) + sub
-        for head in range(heads):
-            mask = head_mask((128, width), head)
-            part = jnp.where(mask, query, jnp.zeros_like(query))
-            spread = lax.dot_general(
-                part, table_ref[...], (((1,), (1,)), ((), ())), preferred_element_type=F32
+def forward_kernel(
+    x_ref, table_ref, heads_ref, mixed_ref, lse_ref, out_ref, bias, low, ssem, rsem, tsem, usem
+):
+    batch, _, n, local, width = heads_ref.shape
+    total = n * local
+    rep, others = greet(n)
+    arriving, leaving = ([], [])
+    for b in range(batch):
+        arriving.append(
+            send_all(
+                others,
+                lambda other: x_ref.at[other, :, b],
+                heads_ref.at[b, :, rep],
+                ssem.at[b],
+                rsem.at[b],
             )
-            spread_bias(bias, spread.astype(BF).astype(F32), block)
-            scores = lax.dot_general(
-                part, keys, (((1,), (1,)), ((), ())), preferred_element_type=F32
+        )
+    for b in range(batch):
+        for part in range(3):
+            heads_ref[b, part, rep] = x_ref[rep, part, b]
+    for b in range(batch):
+        for copy in arriving[b]:
+            copy.wait_recv()
+
+        def one_block(block, carry):
+            keys = heads_ref[b, 1].reshape(total, width)
+            values = heads_ref[b, 2].reshape(total, width)
+            query = heads_ref[b, 0, block] * jnp.asarray(0.125, BF)
+            mixed, logsum = (None, None)
+            for head in range(width // HD):
+                mask = head_mask((128, width), head)
+                part = jnp.where(mask, query, jnp.zeros_like(query))
+                spread = lax.dot_general(
+                    part, table_ref[...], (((1,), (1,)), ((), ())), preferred_element_type=F32
+                )
+                spread_bias(bias, spread.astype(BF).astype(F32), block)
+                scores = lax.dot_general(
+                    part, keys, (((1,), (1,)), ((), ())), preferred_element_type=F32
+                )
+                scores = scores + bias[:, 128 : 128 + total]
+                top = jnp.max(scores, axis=1, keepdims=True)
+                weight = jnp.exp(scores - top)
+                summed = jnp.sum(weight, axis=1, keepdims=True)
+                one = jnp.dot(weight.astype(BF), values, preferred_element_type=F32) / summed
+                own = jnp.broadcast_to(top + jnp.log(summed), (128, width))
+                mixed = one if mixed is None else jnp.where(mask, one, mixed)
+                logsum = own if logsum is None else jnp.where(mask, own, logsum)
+            mixed_ref[b, block] = mixed
+            lse_ref[b, block] = logsum
+            low[b, block] = mixed.astype(BF)
+            return carry
+
+        lax.fori_loop(0, n, one_block, 0)
+        leaving.append(
+            send_all(
+                others, lambda other: low.at[b, other], out_ref.at[rep, b], tsem.at[b], usem.at[b]
             )
-            scores = scores + bias[:, 128 : 128 + total]
-            top = jnp.max(scores, axis=1, keepdims=True)
-            weight = jnp.exp(scores - top)
-            summed = jnp.sum(weight, axis=1, keepdims=True)
-            mixed = jnp.dot(weight.astype(BF), values, preferred_element_type=F32) / summed
-            logsum = jnp.broadcast_to(top + jnp.log(summed), (128, width))
-            if head == 0:
-                mixed_ref[0, rows, :] = mixed
-                lse_ref[0, rows, :] = logsum
-            else:
-                mixed_ref[0, rows, :] = jnp.where(mask, mixed, mixed_ref[0, rows, :])
-                lse_ref[0, rows, :] = jnp.where(mask, logsum, lse_ref[0, rows, :])
-
-
-def attention_forward(query, keys, values, table):
-    batch, total, width = query.shape
-    part = pl.BlockSpec((1, QROWS, width), lambda b, i: (b, i, 0))
-    whole = pl.BlockSpec((1, total, width), lambda b, i: (b, 0, 0))
-    shape = jax.ShapeDtypeStruct((batch, total, width), F32)
+        )
+        out_ref[rep, b] = low[b, rep]
+    for copies in arriving:
+        for copy in copies:
+            copy.wait_send()
+    for copies in leaving:
+        for copy in copies:
+            copy.wait()
+
+
+def attention_forward(stacked, table):
+    n, _, batch, local, width = stacked.shape
+    shape = jax.ShapeDtypeStruct((batch, n, local, width), F32)
+    dma = pltpu.SemaphoreType.DMA
     return pl.pallas_call(
         forward_kernel,
-        out_shape=[shape, shape],
-        grid=(batch, total // QROWS),
-        in_specs=[part, whole, whole, pl.BlockSpec(table.shape, lambda b, i: (0, 0))],
-        out_specs=[part, part],
-        scratch_shapes=[pltpu.VMEM((128, total + 256), F32)],
-        compiler_params=pltpu.CompilerParams(vmem_limit_bytes=32 << 20),
+        out_shape=[
+            jax.ShapeDtypeStruct((batch, 3, n, local, width), BF),
+            shape,
+            shape,
+            jax.ShapeDtypeStruct((n, batch, local, width), BF),
+        ],
+        in_specs=[VM, VM],
+        out_specs=[VM] * 4,
+        scratch_shapes=[
+            pltpu.VMEM((128, n * local + 256), F32),
+            pltpu.VMEM((batch, n, local, width), BF),
+        ]
+        + [dma((batch, n - 1))] * 4,
+        compiler_params=pltpu.CompilerParams(
+            collective_id=2, has_side_effects=True, vmem_limit_bytes=40 << 20
+        ),
         name="attention_forward",
-    )(query, keys, values, table)
+    )(stacked, table)
 
 
 def backward_kernel(
-    q_ref,
-    k_ref,
-    v_ref,
+    x_ref,
+    heads_ref,
     table_ref,
     mixed_ref,
     lse_ref,
-    g_ref,
-    dq_ref,
-    dk_ref,
-    dv_ref,
+    out_ref,
     dtable_ref,
+    grads,
+    low,
     bias,
     keyx,
     dscore,
     prob,
     dkt,
     dvt,
+    ssem,
+    rsem,
+    tsem,
+    usem,
 ):
-    batch_at, step = (pl.program_id(0), pl.program_id(1))
-    total, width = (k_ref.shape[1], k_ref.shape[2])
-    heads = width // HD
-
-    @pl.when(jnp.logical_and(batch_at == 0, step == 0))
-    def _():
-        dtable_ref[...] = jnp.zeros_like(dtable_ref)
-
-    @pl.when(step == 0)
-    def _():
-        dkt[...] = jnp.zeros_like(dkt)
-        dvt[...] = jnp.zeros_like(dvt)
-        keyx[:, 0:width] = k_ref[0]
-        row = lax.broadcasted_iota(jnp.int32, (total, 128), 0) // 128
-        lane = lax.broadcasted_iota(jnp.int32, (total, 128), 1)
-        keyx[:, width : width + 128] = (row == lane).astype(BF)
-        dscore[:, 0:128] = jnp.zeros((128, 128), BF)
-        dscore[:, 128 + total : 256 + total] = jnp.zeros((128, 128), BF)
-
-    keys = k_ref[0]
-    values = v_ref[0]
+    batch, _, n, local, width = heads_ref.shape
+    total = n * local
+    rep, others = greet(n)
+    arriving, leaving = ([], [])
+    for b in range(batch):
+        arriving.append(
+            send_all(
+                others,
+                lambda other: x_ref.at[other, 0, b],
+                grads.at[b, rep],
+                ssem.at[b],
+                rsem.at[b],
+            )
+        )
+    dtable_ref[...] = jnp.zeros_like(dtable_ref)
+    dscore[:, 0:128] = jnp.zeros((128, 128), BF)
+    dscore[:, 128 + total : 256 + total] = jnp.zeros((128, 128), BF)
+    row = lax.broadcasted_iota(jnp.int32, (total, 128), 0) // 128
+    lane = lax.broadcasted_iota(jnp.int32, (total, 128), 1)
+    keyx[:, width : width + 128] = (row == lane).astype(BF)
     flip = (
         lax.broadcasted_iota(jnp.int32, (128, 128), 0)
         + lax.broadcasted_iota(jnp.int32, (128, 128), 1)
@@ -772,89 +779,121 @@
     ).astype(BF)
     lane_at = lax.broadcasted_iota(jnp.int32, (128, 128), 1)
     band_at = lax.broadcasted_iota(jnp.int32, (128, BAND), 1)
-    for sub in range(QROWS // 128):
-        rows = slice(sub * 128, (sub + 1) * 128)
-        block = step * (QROWS // 128) + sub
-        query = q_ref[0, rows, :] * jnp.asarray(0.125, BF)
-        grad = g_ref[0, rows, :]
-        weighed = grad.astype(F32) * mixed_ref[0, rows, :]
-        query_t = jnp.transpose(query.astype(F32)).astype(BF)
-        grad_t = jnp.transpose(grad.astype(F32)).astype(BF)
-        for head in range(heads):
-            mask = head_mask((128, width), head)
-            lanes = slice(head * HD, (head + 1) * HD)
-            part = jnp.where(mask, query, jnp.zeros_like(query))
-            grad_part = jnp.where(mask, grad, jnp.zeros_like(grad))
-            balance = jnp.sum(jnp.where(mask, weighed, 0.0), axis=1, keepdims=True)
-            logsum = lse_ref[0, rows, head * HD : head * HD + 1]
-            spread = lax.dot_general(
-                part, table_ref[...], (((1,), (1,)), ((), ())), preferred_element_type=F32
+    for b in range(batch):
+        grads[b, rep] = x_ref[rep, 0, b]
+    for b in range(batch):
+        dkt[...] = jnp.zeros_like(dkt)
+        dvt[...] = jnp.zeros_like(dvt)
+        keyx[:, 0:width] = heads_ref[b, 1].reshape(total, width)
+        for copy in arriving[b]:
+            copy.wait_recv()
+
+        def one_block(block, carry):
+            keys = heads_ref[b, 1].reshape(total, width)
+            values = heads_ref[b, 2].reshape(total, width)
+            query = heads_ref[b, 0, block] * jnp.asarray(0.125, BF)
+            grad = grads[b, block]
+            weighed = grad.astype(F32) * mixed_ref[b, block]
+            logsums = lse_ref[b, block]
+            query_t = jnp.transpose(query.astype(F32)).astype(BF)
+            grad_t = jnp.transpose(grad.astype(F32)).astype(BF)
+            found = None
+            for head in range(width // HD):
+                mask = head_mask((128, width), head)
+                lanes = slice(head * HD, (head + 1) * HD)
+                part = jnp.where(mask, query, jnp.zeros_like(query))
+                grad_part = jnp.where(mask, grad, jnp.zeros_like(grad))
+                balance = jnp.sum(jnp.where(mask, weighed, 0.0), axis=1, keepdims=True)
+                logsum = logsums[:, head * HD : head * HD + 1]
+                spread = lax.dot_general(
+                    part, table_ref[...], (((1,), (1,)), ((), ())), preferred_element_type=F32
+                )
+                spread_bias(bias, spread.astype(BF).astype(F32), block)
+                scores = lax.dot_general(
+                    part, keys, (((1,), (1,)), ((), ())), preferred_element_type=F32
+                )
+                chance = jnp.exp(scores + bias[:, 128 : 128 + total] - logsum)
+                back = lax.dot_general(
+                    grad_part, values, (((1,), (1,)), ((), ())), preferred_element_type=F32
+                )
+                prob[...] = chance.astype(BF)
+                dscore[:, 128 : 128 + total] = (chance * (back - balance)).astype(BF)
+                score_back = dscore[:, 128 : 128 + total]
+                dkt[lanes, :] += jnp.dot(
+                    query_t[lanes, :], score_back, preferred_element_type=F32
+                )
+                dvt[lanes, :] += jnp.dot(grad_t[lanes, :], prob[...], preferred_element_type=F32)
+                wide = jnp.dot(score_back, keyx[...], preferred_element_type=F32)
+                sums = wide[:, width : width + 128]
+                before = jnp.sum(jnp.where(lane_at < block - 1, sums, 0.0), axis=1, keepdims=True)
+                after = jnp.sum(jnp.where(lane_at > block + 1, sums, 0.0), axis=1, keepdims=True)
+                near = dscore[:, pl.ds(pl.multiple_of(block * 128, 128), 384)]
+                near = jnp.dot(flip, near, preferred_element_type=F32)
+                near = jnp.concatenate([near, jnp.zeros((128, BAND - 384), F32)], axis=1)
+                near = pltpu.roll(near, BAND - 127, 1, stride=1, stride_axis=0)
+                near = jnp.dot(flip, near.astype(BF), preferred_element_type=F32)
+                near = near + jnp.where(band_at == 0, before, 0.0)
+                near = (near + jnp.where(band_at == 383, after, 0.0)).astype(BF)
+                query_back = wide[:, 0:width] + jnp.dot(
+                    near, table_ref[...], preferred_element_type=F32
+                )
+                dtable_ref[...] += lax.dot_general(
+                    near, part, (((0,), (0,)), ((), ())), preferred_element_type=F32
+                )
+                found = query_back if found is None else jnp.where(mask, query_back, found)
+            low[b, 0, block] = (found * 0.125).astype(BF)
+            return carry
+
+        lax.fori_loop(0, n, one_block, 0)
+        low[b, 1] = jnp.transpose(dkt[...]).astype(BF).reshape(n, local, width)
+        low[b, 2] = jnp.transpose(dvt[...]).astype(BF).reshape(n, local, width)
+        leaving.append(
+            send_all(
+                others,
+                lambda other: low.at[b, :, other],
+                out_ref.at[rep, :, b],
+                tsem.at[b],
+                usem.at[b],
             )
-            spread_bias(bias, spread.astype(BF).astype(F32), block)
-            scores = lax.dot_general(
-                part, keys, (((1,), (1,)), ((), ())), preferred_element_type=F32
-            )
-            chance = jnp.exp(scores + bias[:, 128 : 128 + total] - logsum)
-            back = lax.dot_general(
-                grad_part, values, (((1,), (1,)), ((), ())), preferred_element_type=F32
-            )
-            prob[...] = chance.astype(BF)
-            dscore[:, 128 : 128 + total] = (chance * (back - balance)).astype(BF)
-            score_back = dscore[:, 128 : 128 + total]
-            dkt[lanes, :] += jnp.dot(query_t[lanes, :], score_back, preferred_element_type=F32)
-            dvt[lanes, :] += jnp.dot(grad_t[lanes, :], prob[...], preferred_element_type=F32)
-            wide = jnp.dot(score_back, keyx[...], preferred_element_type=F32)
-            sums = wide[:, width : width + 128]
-            before = jnp.sum(jnp.where(lane_at < block - 1, sums, 0.0), axis=1, keepdims=True)
-            after = jnp.sum(jnp.where(lane_at > block + 1, sums, 0.0), axis=1, keepdims=True)
-            near = dscore[:, pl.ds(pl.multiple_of(block * 128, 128), 384)]
-            near = jnp.dot(flip, near, preferred_element_type=F32)
-            near = jnp.concatenate([near, jnp.zeros((128, BAND - 384), F32)], axis=1)
-            near = pltpu.roll(near, BAND - 127, 1, stride=1, stride_axis=0)
-            near = jnp.dot(flip, near.astype(BF), preferred_element_type=F32)
-            near = near + jnp.where(band_at == 0, before, 0.0)
-            near = (near + jnp.where(band_at == 383, after, 0.0)).astype(BF)
-            query_back = wide[:, 0:width] + jnp.dot(
-                near, table_ref[...], preferred_element_type=F32
-            )
-            dtable_ref[...] += lax.dot_general(
-                near, part, (((0,), (0,)), ((), ())), preferred_element_type=F32
-            )
-            query_back = (query_back * 0.125).astype(BF)
-            if head == 0:
-                dq_ref[0, rows, :] = query_back
-            else:
-                dq_ref[0, rows, :] = jnp.where(mask, query_back, dq_ref[0, rows, :])
-
-    @pl.when(step == pl.num_programs(1) - 1)
-    def _():
-        dk_ref[0] = jnp.transpose(dkt[...]).astype(BF)
-        dv_ref[0] = jnp.transpose(dvt[...]).astype(BF)
-
-
-def attention_backward(query, keys, values, table, mixed, logsum, grad):
-    batch, total, width = query.shape
-    part = pl.BlockSpec((1, QROWS, width), lambda b, i: (b, i, 0))
-    whole = pl.BlockSpec((1, total, width), lambda b, i: (b, 0, 0))
-    fixed = pl.BlockSpec(table.shape, lambda b, i: (0, 0))
-    shape = jax.ShapeDtypeStruct((batch, total, width), BF)
+        )
+        for part in range(3):
+            out_ref[rep, part, b] = low[b, part, rep]
+    for copies in arriving:
+        for copy in copies:
+            copy.wait_send()
+    for copies in leaving:
+        for copy in copies:
+            copy.wait()
+
+
+def attention_backward(stacked, heads, table, mixed, logsum):
+    batch, _, n, local, width = heads.shape
+    total = n * local
+    dma = pltpu.SemaphoreType.DMA
     return pl.pallas_call(
         backward_kernel,
-        out_shape=[shape, shape, shape, jax.ShapeDtypeStruct(table.shape, F32)],
-        grid=(batch, total // QROWS),
-        in_specs=[part, whole, whole, fixed, part, part, part],
-        out_specs=[part, whole, whole, fixed],
+        out_shape=[
+            jax.ShapeDtypeStruct((n, 3, batch, local, width), BF),
+            jax.ShapeDtypeStruct(table.shape, F32),
+        ],
+        in_specs=[VM] * 5,
+        out_specs=[VM] * 2,
         scratch_shapes=[
+            pltpu.VMEM((batch, n, local, width), BF),
+            pltpu.VMEM((batch, 3, n, local, width), BF),
             pltpu.VMEM((128, total + 256), F32),
             pltpu.VMEM((total, width + 128), BF),
             pltpu.VMEM((128, total + 256), BF),
             pltpu.VMEM((128, total), BF),
             pltpu.VMEM((width, total), F32),
             pltpu.VMEM((width, total), F32),
-        ],
-        compiler_params=pltpu.CompilerParams(vmem_limit_bytes=40 << 20),
+        ]
+        + [dma((batch, n - 1))] * 4,
+        compiler_params=pltpu.CompilerParams(
+            collective_id=3, has_side_effects=True, vmem_limit_bytes=48 << 20
+        ),
         name="attention_backward",
-    )(query, keys, values, table, mixed, logsum, grad)
+    )(stacked, heads, table, mixed, logsum)
 
 
 def shifted(value, axis, steps):
@@ -1266,13 +1305,14 @@
     query = (times(attend_in, w[8]) + w[9]).astype(BF).reshape(batch, local, features)
     keys = times(attend_in, w[10]).astype(BF).reshape(batch, local, features)
     values = (times(attend_in, w[11]) + w[12]).astype(BF).reshape(batch, local, features)
-    query_h, keys_h, values_h = from_positions(swap(to_heads([query, keys, values], n_rep), 0))
     place = jnp.clip(jnp.arange(BAND) - 64, 0, TABLE - 1)
     place = jnp.where(jnp.arange(BAND) >= 384, 0, place)
     table = w[TABLE_AT]
-    spread_table = jnp.tile(jnp.take(table, place, axis=0), (1, query_h.shape[2] // HD))
-    mixed_h, logsum = attention_forward(query_h, keys_h, values_h, spread_table)
-    mixed = from_heads(swap(to_positions([mixed_h.astype(BF)], n_rep), 1))[0]
+    spread_table = jnp.tile(jnp.take(table, place, axis=0), (1, features // n_rep // HD))
+    heads, mixed_h, logsum, mixed = attention_forward(
+        to_heads([query, keys, values], n_rep), spread_table
+    )
+    mixed = from_heads(mixed[:, None])[0]
     level2 = level1 + times(mixed, w[13]) + w[14]
 
     conv_in = norm(level2, w[16], w[17]).astype(BF)
@@ -1310,13 +1350,10 @@
     mixer_out = back2.astype(BF)
     grads[14] = column_sum(mixer_out)
     mixed_back = times_back(mixer_out, w[13]).astype(BF).reshape(batch, local, features)
-    grad_h = from_positions(swap(to_heads([mixed_back], n_rep), 2))[0]
-    query_b, keys_b, values_b, table_b = attention_backward(
-        query_h, keys_h, values_h, spread_table, mixed_h, logsum, grad_h
+    found, table_b = attention_backward(
+        to_heads([mixed_back], n_rep), heads, spread_table, mixed_h, logsum
     )
-    query_back, key_back, value_back = from_heads(
-        swap(to_positions([query_b, keys_b, values_b], n_rep), 3)
-    )
+    query_back, key_back, value_back = from_heads(found)
     folded = table_b.reshape(BAND, -1, HD).sum(axis=1)
     grads[TABLE_AT] = jnp.concatenate(
         [

time: 699 us -> 672 us (0.961)
  Pallas kernels: 562 us -> 537 us
    pallas_call x6 -> x2, Pallas kernels: 122 us -> 99 us  [the longest x1 60.5 us: attention_backward(): pl.pallas_call(backward_kernel, out_shape=[jax.ShapeDtypeStruct((n, 3, ba...]
where the time goes in v3:
time: 672 us; the launch traced here: 666 us
  Pallas kernels  537 us (80%)
  matrix products  65.2 us (10%)
  other arithmetic  34.9 us (5%)
  local copies, waits for them, and re-layouts  21.6 us (3%)
    pallas_call x1, Pallas kernels, reduce_fast(): pl.pallas_call(functools.partial(reduce_kernel, groups, units, len(lefts)...  238 us
    pallas_call x1, Pallas kernels, gather_fast(): pl.pallas_call(functools.partial(gather_kernel, chunks, count, len(smalls...  178 us
    pallas_call x1, Pallas kernels, attention_backward(): pl.pallas_call(backward_kernel, out_shape=[jax.ShapeDtypeStruct((n, 3, ba...  60.5 us
    pallas_call x1, Pallas kernels, attention_forward(): pl.pallas_call(forward_kernel, out_shape=[jax.ShapeDtypeStruct((batch, 3,...  38.5 us
    dot_general x10, matrix products, times_back(): lax.dot_general(left, right, (((1,), (1,)), ((), ())), preferred_element_...  38.3 us
    dot_general x10, matrix products, times(): return jnp.dot(left, right, preferred_element_type=F32)  26.9 us
    convert_element_type x10, other arithmetic, reduce_fast(): w.reshape(-1, w.shape[-1]).astype(F32)  20.8 us
  transfers between devices with their start and end apart: 2, of which 1 were waited for; matrix products, arithmetic and copies ran while one was open for 0% of the time, Pallas kernels for 0%

profile of v3, /device:TPU:0, one launch (start us, length us, event | category | flops | bytes accessed | tf_op | source)
XLA Modules:
  0.0 666.4 jit_solution(15337478673260997801)
XLA Ops:
  0.7 1.4 copy.98.refs_30_
  2.1 177.9 %gather_weights.1 = (bf16[2,2,2,2,2,2,16,4096]{7,6,5,4,3,2,1,0:T(8,128)(2,1)}, bf16[2,2,2,2,2,2,64,1024]{7,6,5,4,3,2,1,0:T(8,128)(2,1)}, bf16[2,2,2,2,2,2,16,102...) custom-call(bf16[2,2,2,2,16,4096]{5,4,3,2,1,0:T(8,128)(2,1)} %bitcas, ...), custom_call_target="tpu_custom_call" | custom-call | tf_op jit(solution)/shard_map/gather_weights/pallas_call | solution.py:201
  180.1 0.8 convert_bitcast_fusion.1
  180.9 1.3 slice_convert_fusion.2
  182.2 0.9 slice_bitcast_fusion.3
  183.8 1.6 gather_fusion
  186.0 8.2 %multiply_convert_fusion.1 = (bf16[256,4096]{1,0:T(8,128)(2,1)S(1)}, f32[256,4096]{1,0:T(8,128)}) fusion(f32[4096]{0:T(1024)S(1)} %bitcast.353, bf16[256,1024]{1,0:T(8,128)(2,1)S(1)} %bitcast.317, bf16[1024,4096]{1,0:T(8,128)(2,1)} %bitcast.359), kind=kOutput, calls=%fused_computation.11 | convolution fusion | flops 2153775104 | bytes 15220736 | tf_op jit(solution)/shard_map/dot_general | solution.py:939
  194.2 2.5 fusion.31
  197.3 0.7 fusion.9
  198.1 0.8 copy-done.20
  198.9 0.7 fusion.10
  199.9 0.7 fusion.11
  201.1 38.5 %attention_forward.1 = (bf16[2,3,8,128,128]{4,3,2,1,0:T(8,128)(2,1)S(1)}, f32[2,8,128,128]{3,2,1,0:T(8,128)S(1)}, f32[2,8,128,128]{3,2,1,0:T(8,128)S(1)}, bf16[8,2,128,128]{3,2,1,0:T(8,128)(2,1)S(1)}) custom-call(bf16[8,3,2,128,128]{4,3,2,1,0:T(8,128)(2,1)S(1)} %pad_maximum_fusion.x_ref, bf16[512,128]{1,0:T(8,128)(2,1)S(1)} %copy.105.table_ref), custom_call_target="tpu_custom_call" | custom-call | tf_op jit(solution)/shard_map/attention_forward/pallas_call | solution.py:712
  239.9 0.8 fusion.32
  241.8 1.3 fusion.35.doubled_ref
  243.1 2.0 collective-permute-start
  245.1 0.9 convert_bitcast_fusion
  246.0 0.9 copy.150
  247.2 0.7 convert_reduce_fusion.2
  247.9 7.7 %conv_forward.1 = (f32[2,128,1024]{2,1,0:T(8,128)S(1)}, bf16[2,128,1024]{2,1,0:T(8,128)(2,1)S(1)}) custom-call(f32[2,128,2048]{2,1,0:T(8,128)S(1)} %fusion.35.doubled_ref, bf16[2,30,1024]{2,1,0:T(8,128)(2,1)S(1)} %collective-permute-done.rim_ref, f32[31,1024]{1,0:T(8,128)S(1)} %bitcast.268, f32[1,1024]{1,0:T(1,128)S(1)} %convert.37.gain_ref, ...), custom_call_target="tpu_custom_call" | custom-call | tf_op jit(solution)/shard_map/conv_forward/pallas_call | solution.py:1126
  255.6 0.8 fusion.33
  257.0 4.6 multiply_convert_fusion
  261.6 6.6 fusion.34
  268.5 1.0 fusion.19
  269.5 1.0 convert_reduce_fusion.3
  270.6 11.1 %convert_reduce_fusion = (f32[4096]{0:T(1024)}, bf16[256,4096]{1,0:T(8,128)(2,1)S(1)}) fusion(f32[256,4096]{1,0:T(8,128)} %get-tuple-element.311, bf16[256,1024]{1,0:T(8,128)(2,1)S(1)} %get-tuple-element.263.refs_8_, bf16[4096,1024]{1,0:T(8,128)(2,1)} %bitcast.372), kind=kOutput, calls=%fused_computation.7 | convolution fusion | flops 2159013888 | bytes 15220736 | tf_op jit(solution)/shard_map/dot_general | solution.py:943
  281.6 7.4 %multiply_reduce_fusion = (f32[1024]{0:T(1024)}, f32[256]{0:T(256)S(1)}, f32[256]{0:T(256)S(1)}, f32[1024]{0:T(1024)}, f32[256,1024]{1,0:T(8,128)S(1)}) fusion(f32[256,1024]{1,0:T(8,128)S(1)} %get-tuple-element.309, f32[256]{0:T(256)S(1)} %add_rsqrt_fusion.1, f32[256]{0:T(256)S(1)} %broadcast_multiply_fusion.10, f32[1024]{0:T(1024)S(1)} %bitcast.331, ...), kind=kOutput, calls=%fused_computation.54 | convolution fusion | flops 2149840384 | bytes 12599296 | tf_op jit(solution)/shard_map/dot_general | solution.py:943
  289.1 1.6 fusion.29
  290.6 0.7 fusion.36.grad_ref
  291.4 3.0 depth_backward.1
  294.4 1.3 collective-permute-start.1
  296.3 2.1 collective-permute-done.1.after_ref
  298.4 10.6 %conv_backward.1 = (bf16[2,128,2048]{2,1,0:T(8,128)(2,1)S(1)}, f32[32,1024]{1,0:T(8,128)S(1)}) custom-call(f32[2,128,1024]{2,1,0:T(8,128)S(1)} %get-tuple-element.101.back_ref, bf16[2,30,1024]{2,1,0:T(8,128)(2,1)S(1)} %collective-permute-done.1.after_ref, f32[2,128,2048]{2,1,0:T(8,128)S(1)} %fusion.35.doubled_ref, ...), custom_call_target="tpu_custom_call" | custom-call | tf_op jit(solution)/shard_map/conv_backward/pallas_call | solution.py:1247
  309.1 2.1 multiply_reduce_fusion.1
  311.2 1.0 convert_reduce_fusion.4
  312.8 0.7 fusion.12
  313.8 60.5 %attention_backward.1 = (bf16[8,3,2,128,128]{4,3,2,1,0:T(8,128)(2,1)S(1)}, f32[512,128]{1,0:T(8,128)S(1)}) custom-call(bf16[8,1,2,128,128]{4,3,2,1,0:T(8,128)(2,1)S(1)} %bitcast.267, bf16[2,3,8,128,128]{4,3,2,1,0:T(8,128)(2,1)S(1)} %get-tuple-element.103.heads_ref, bf16[512,128]{1,0:T(8,128)(2,1)S(1)} %copy.105.table_ref, ...), custom_call_target="tpu_custom_call" | custom-call | tf_op jit(solution)/shard_map/attention_backward/pallas_call | solution.py:873
  374.9 0.8 convert_reduce_fusion.5
  375.7 0.9 slice_bitcast_fusion
  377.0 0.8 fusion.28
  377.7 0.9 copy.149
  378.6 1.1 copy.112
  381.1 2.1 copy.147
  383.2 1.4 copy.111
  384.6 0.9 copy.148
  385.4 2.3 convolution_add_fusion.3
  387.8 1.6 multiply_reduce_fusion.2
  389.5 1.0 convert_reduce_fusion.7
  390.5 7.4 %convert_reduce_fusion.1 = (f32[4096]{0:T(1024)}, bf16[256,4096]{1,0:T(8,128)(2,1)S(1)}) fusion(f32[256,4096]{1,0:T(8,128)S(1)} %copy-done.36, bf16[256,1024]{1,0:T(8,128)(2,1)S(1)} %get-tuple-element.268.refs_16_, bf16[4096,1024]{1,0:T(8,128)(2,1)} %bitcast.363), kind=kOutput, calls=%fused_computation.8 | convolution fusion | flops 2159013888 | bytes 15220736 | tf_op jit(solution)/shard_map/dot_general | solution.py:943
  398.0 4.0 multiply_reduce_fusion.3
  402.0 237.6 %reduce_grads.1 = (bf16[4,2,2,2,2,16,1024]{6,5,4,3,2,1,0:T(8,128)(2,1)}, bf16[2,2,2,2,16,4096]{5,4,3,2,1,0:T(8,128)(2,1)}, bf16[2,2,2,2,16,1024]{5,4,3,2,1,0:T(8...) custom-call(bf16[256,4096]{1,0:T(8,128)(2,1)} %copy-done.13, ...), custom_call_target="tpu_custom_call" | custom-call | tf_op jit(solution)/shard_map/reduce_grads/pallas_call | solution.py:543
  639.7 0.7 slice.149
  640.4 1.5 split_sums.1
  642.3 2.0 copy.118
  645.2 2.1 bitcast_convert_fusion.9
  647.3 2.1 bitcast_convert_fusion.8
  649.4 2.1 bitcast_convert_fusion.7
  651.5 1.1 bitcast_convert_fusion.6
  652.7 1.1 bitcast_convert_fusion.5
  653.8 2.6 bitcast_convert_fusion.3
  656.4 1.6 bitcast_convert_fusion.4
  658.1 2.6 bitcast_convert_fusion.2
  660.7 2.6 bitcast_convert_fusion.1
  663.3 2.6 bitcast_convert_fusion
  (166 shorter events, 9.9 us)
Async XLA Ops:
  2.1 180.9 %copy-start.6 = (bf16[2,128,1,1024]{3,1,2,0:T(8,128)(2,1)S(1)}, bf16[2,128,1,1024]{3,1,2,0:T(8,128)(2,1)}, u32[]{:S(2)}) copy-start(bf16[2,128,1,1024]{3,1,2,0:T(8,128)(2,1)} %param.33) | copy-start | bytes 1572868
  185.7 8.5 %slice-start.2 = ((s8[8388608]{0:T(1024)(128)(4,1)}), s8[4194304]{0:T(1024)(128)(4,1)S(1)}, s32[]{:S(2)}) async-start(s8[8388608]{0:T(1024)(128)(4,1)} %bitcast.364), calls=%async_computation.2 | async-start | bytes 8388608
  186.0 8.2 %slice-start.3 = ((s8[8388608]{0:T(1024)(128)(4,1)}), s8[4194304]{0:T(1024)(128)(4,1)S(1)}, s32[]{:S(2)}) async-start(s8[8388608]{0:T(1024)(128)(4,1)} %bitcast.364), calls=%async_computation.3 | async-start | bytes 8388608
  194.2 2.6 copy-start.12
  194.2 3.1 copy-start.34
  196.7 43.2 %copy-start.3 = (f32[256,1024]{1,0:T(8,128)}, f32[256,1024]{1,0:T(8,128)S(1)}, u32[]{:S(2)}) copy-start(f32[256,1024]{1,0:T(8,128)S(1)} %get-tuple-element.305) | copy-start | bytes 3145732
  196.7 2.2 copy-start.20
  197.3 2.5 copy-start.22
  198.0 1.8 copy-start.24
  200.7 39.3 %copy-start.27 = (bf16[2,2,2,2,2,2,16,1024]{7,6,5,4,3,2,1,0:T(8,128)(2,1)S(1)}, bf16[2,2,2,2,2,2,16,1024]{7,6,5,4,3,2,1,0:T(8,128)(2,1)}, u32[]{:S(2)}) copy-start(bf16[2,2,2,2,2,2,16,1024]{7,6,5,4,3,2,1,0:T(8,128)(2,1)} %get-tuple-element.94) | copy-start | bytes 6291460
  239.6 2.2 copy-start.11
  241.3 5.6 copy-start.10
  241.8 5.4 copy-start.8
  241.8 15.2 %slice-start.4 = ((s8[8388608]{0:T(1024)(128)(4,1)}), s8[4194304]{0:T(1024)(128)(4,1)S(1)}, s32[]{:S(2)}) async-start(s8[8388608]{0:T(1024)(128)(4,1)} %bitcast.368), calls=%async_computation.4 | async-start | bytes 8388608
  243.0 12.6 %copy-start.5 = (bf16[2,2,2,2,2,2,16,1024]{7,6,5,4,3,2,1,0:T(8,128)(2,1)S(1)}, bf16[2,2,2,2,2,2,16,1024]{7,6,5,4,3,2,1,0:T(8,128)(2,1)}, u32[]{:S(2)}) copy-start(bf16[2,2,2,2,2,2,16,1024]{7,6,5,4,3,2,1,0:T(8,128)(2,1)} %get-tuple-element.97) | copy-start | bytes 6291460
  243.1 4.8 collective-permute-start
  247.1 9.8 %slice-start.5 = ((s8[8388608]{0:T(1024)(128)(4,1)}), s8[4194304]{0:T(1024)(128)(4,1)S(1)}, s32[]{:S(2)}) async-start(s8[8388608]{0:T(1024)(128)(4,1)} %bitcast.368), calls=%async_computation.5 | async-start | bytes 8388608
  255.6 6.1 copy-start
  257.0 4.7 copy-start.23
  261.6 6.6 copy-start.13
  270.5 11.1 %copy-start.25 = (bf16[256,1024]{1,0:T(8,128)(2,1)}, bf16[256,1024]{1,0:T(8,128)(2,1)S(1)}, u32[]{:S(2)}) copy-start(bf16[256,1024]{1,0:T(8,128)(2,1)S(1)} %get-tuple-element.263.refs_8_) | copy-start | bytes 1572868
  281.6 7.4 %copy-start.14 = (bf16[256,4096]{1,0:T(8,128)(2,1)}, bf16[256,4096]{1,0:T(8,128)(2,1)S(1)}, u32[]{:S(2)}) copy-start(bf16[256,4096]{1,0:T(8,128)(2,1)S(1)} %get-tuple-element.321.refs_9_) | copy-start | bytes 6291460
  290.6 18.4 %copy-start.9 = (bf16[256,1024]{1,0:T(8,128)(2,1)}, bf16[256,1024]{1,0:T(8,128)(2,1)S(1)}, u32[]{:S(2)}) copy-start(bf16[256,1024]{1,0:T(8,128)(2,1)S(1)} %get-tuple-element.270.refs_10_) | copy-start | bytes 1572868
  294.4 4.0 collective-permute-start.1
  309.0 2.1 copy-start.1
  309.1 2.1 copy-start.2
  311.2 1.6 copy-start.28
  312.2 1.5 copy-start.29
  374.4 2.5 copy-start.21
  380.2 7.6 %copy-start.4 = (f32[256,1024]{1,0:T(8,128)S(1)}, f32[256,1024]{1,0:T(8,128)}, u32[]{:S(2)}) copy-start(f32[256,1024]{1,0:T(8,128)} %copy-done.3) | copy-start | bytes 3145732
  381.1 6.7 %copy-start.26 = (bf16[2,128,8,128]{3,2,1,0:T(8,128)(2,1)S(1)}, bf16[2,128,8,128]{3,2,1,0:T(8,128)(2,1)}, u32[]{:S(2)}) copy-start(bf16[2,128,8,128]{3,2,1,0:T(8,128)(2,1)} %copy.112) | copy-start | bytes 1572868
  381.1 6.7 %copy-start.35 = (bf16[2,2,2,2,2,2,16,1024]{7,6,5,4,3,2,1,0:T(8,128)(2,1)S(1)}, bf16[2,2,2,2,2,2,16,1024]{7,6,5,4,3,2,1,0:T(8,128)(2,1)}, u32[]{:S(2)}) copy-start(bf16[2,2,2,2,2,2,16,1024]{7,6,5,4,3,2,1,0:T(8,128)(2,1)} %get-tuple-element.92) | copy-start | bytes 6291460
  387.8 2.7 copy-start.36
  389.5 8.5 %slice-start = ((s8[8388608]{0:T(1024)(128)(4,1)}), s8[4194304]{0:T(1024)(128)(4,1)S(1)}, s32[]{:S(2)}) async-start(s8[8388608]{0:T(1024)(128)(4,1)} %bitcast.360), calls=%async_computation | async-start | bytes 8388608
  390.5 7.5 %copy-start.30 = (bf16[256,1024]{1,0:T(8,128)(2,1)}, bf16[256,1024]{1,0:T(8,128)(2,1)S(1)}, u32[]{:S(2)}) copy-start(bf16[256,1024]{1,0:T(8,128)(2,1)S(1)} %get-tuple-element.268.refs_16_) | copy-start | bytes 1572868
  390.5 7.5 %copy-start.7 = (bf16[2,128,1,1024]{3,1,2,0:T(8,128)(2,1)S(1)}, bf16[2,128,1,1024]{3,1,2,0:T(8,128)(2,1)}, u32[]{:S(2)}) copy-start(bf16[2,128,1,1024]{3,1,2,0:T(8,128)(2,1)} %param.33) | copy-start | bytes 1572868
  390.5 7.5 %slice-start.1 = ((s8[8388608]{0:T(1024)(128)(4,1)}), s8[4194304]{0:T(1024)(128)(4,1)S(1)}, s32[]{:S(2)}) async-start(s8[8388608]{0:T(1024)(128)(4,1)} %bitcast.360), calls=%async_computation.1 | async-start | bytes 8388608
  398.0 4.0 copy-start.19
  642.3 9.2 %copy-start.33 = (bf16[2,2,2,2,16,1024]{5,4,3,2,1,0:T(8,128)(2,1)S(1)}, bf16[2,2,2,2,16,1024]{5,4,3,2,1,0:T(8,128)(2,1)}, u32[]{:S(2)}) copy-start(bf16[2,2,2,2,16,1024]{5,4,3,2,1,0:T(8,128)(2,1)} %get-tuple-element.124) | copy-start | bytes 1572868
  642.3 10.3 %copy-start.32 = (bf16[2,2,2,2,16,1024]{5,4,3,2,1,0:T(8,128)(2,1)S(1)}, bf16[2,2,2,2,16,1024]{5,4,3,2,1,0:T(8,128)(2,1)}, u32[]{:S(2)}) copy-start(bf16[2,2,2,2,16,1024]{5,4,3,2,1,0:T(8,128)(2,1)} %get-tuple-element.132) | copy-start | bytes 1572868
  644.4 9.4 %copy-start.18 = (bf16[2,2,2,2,16,4096]{5,4,3,2,1,0:T(8,128)(2,1)S(1)}, bf16[2,2,2,2,16,4096]{5,4,3,2,1,0:T(8,128)(2,1)}, u32[]{:S(2)}) copy-start(bf16[2,2,2,2,16,4096]{5,4,3,2,1,0:T(8,128)(2,1)} %get-tuple-element.113) | copy-start | bytes 6291460
  652.7 3.8 copy-start.31
  653.8 4.3 copy-start.17
  656.4 4.3 copy-start.16
  660.7 2.7 copy-start.15

commit v4 on v3

--- a/solution.py
+++ b/solution.py
@@ -242,17 +242,12 @@
 
 
 REDUCE_LAG = (0, 1, 2, 3, 4, 5, 6, 7)
-
-
-def reduce_kernel(groups, units, n_left, n_right, n_small, *refs):
-    lefts, rights = (refs[:n_left], refs[n_left : n_left + n_right])
-    refs = refs[n_left + n_right :]
-    smalls, outs, small_out = (refs[:n_small], refs[n_small:-18], refs[-18])
-    lbuf, rbuf, sbuf, b1, b2, b3, b4, b5, hop_out, hop_in, hop_total = refs[-17:-6]
-    lsem, ssem, rsem, osem, hsem, isem = refs[-6:]
+BESIDE_LAG = (0, 1, 2, 4, 6, 7, 8, 9)
+
+
+def reducer(groups, units, lefts, rights, outs, buffers, lags):
+    lbuf, rbuf, sbuf, b1, b2, b3, b4, b5, lsem, ssem, rsem, osem = buffers
     z, core, x, y, z0, z1, peers = here()
-    del peers["zz"]
-    meet(peers)
 
     def remote(u, slot, src, dst, to):
         return pltpu.make_async_remote_copy(
@@ -351,8 +346,9 @@
             left, rbuf[slot], (((0,), (0,)), ((), ())), preferred_element_type=F32
         ).reshape(2, 2, 2, 16, 1024)
 
-    load(0)
-    load(1)
+    def begin():
+        load(0)
+        load(1)
 
     def stage_multiply(u):
         slot = lax.rem(u, 3)
@@ -447,52 +443,15 @@
         stage_core,
     )
 
-    hops = ("c", "x", "y", "z0", "z1")
-
-    def hop(k):
-        return pltpu.make_async_remote_copy(
-            src_ref=hop_out.at[k],
-            dst_ref=hop_in.at[k],
-            send_sem=hsem.at[k],
-            recv_sem=isem.at[k],
-            device_id=peers[hops[k]],
-            device_id_type=MESH,
-        )
-
-    fill_sums(hop_total, smalls)
-    hop_out[0] = hop_total[...].astype(BF)
-    hop(0).start()
-
-    def stage_hop(k):
-        hop(k).wait_recv()
-        total = hop_out[k].astype(F32) + hop_in[k].astype(F32)
-        if k + 1 < len(hops):
-            hop_out[k + 1] = total.astype(BF)
-            hop(k + 1).start()
-        else:
-            width = small_out.shape[1]
-            hop_total[...] = total
-            small_out[...] = hop_total[:, pl.ds(pl.multiple_of(z * width, width), width)]
-
-    def step(i, carry):
-        for k in range(len(hops)):
-
-            @pl.when(i == 2 * k + 1)
-            def _():
-                stage_hop(k)
-
-        for stage, lag in zip(stages, REDUCE_LAG):
+    def step(i):
+        for stage, lag in zip(stages, lags):
             u = i - lag
 
             @pl.when(jnp.logical_and(u >= 0, u < units))
             def _():
                 stage(u)
 
-        return carry
-
-    lax.fori_loop(0, units + REDUCE_LAG[-1], step, 0)
-
-    def finish(u, carry):
+    def finish_one(u, carry):
         arrive(spread_core(u))
         for copies in (
             copy_first,
@@ -513,12 +472,31 @@
 
         return carry
 
-    lax.fori_loop(0, units, finish, 0)
-    for k in range(len(hops)):
-        hop(k).wait_send()
-
-
-def reduce_fast(pairs, smalls):
+    def finish():
+        lax.fori_loop(0, units, finish_one, 0)
+
+    return begin, step, finish
+
+
+def reducer_buffers(units):
+    dma = pltpu.SemaphoreType.DMA
+    return [
+        pltpu.VMEM((3, 4, 256, 256), BF),
+        pltpu.VMEM((3, 256, 1024), BF),
+        pltpu.VMEM((2, 2, 2, 2, 2, 2, 16, 1024), BF),
+        pltpu.VMEM((units, 2, 2, 2, 2, 2, 16, 1024), BF),
+        pltpu.VMEM((units, 2, 2, 2, 2, 16, 1024), BF),
+        pltpu.VMEM((units, 2, 2, 2, 16, 1024), BF),
+        pltpu.VMEM((units, 2, 2, 16, 1024), BF),
+        pltpu.VMEM((units, 2, 16, 1024), BF),
+        dma((3, 5)),
+        dma((units, 12)),
+        dma((units, 12)),
+        dma((units, 2)),
+    ]
+
+
+def reducer_plan(pairs):
     lefts, rights, groups, units = ([], [], [], 0)
 
     def index_of(arrays, array):
@@ -533,43 +511,113 @@
         count = left.shape[1] // 1024 if by_rows else right.shape[1] // 1024
         groups.append((index_of(lefts, left), index_of(rights, right), units, count, by_rows))
         units += count
-    dma = pltpu.SemaphoreType.DMA
-    rows = sum(a.shape[0] if a.ndim > 1 else a.shape[0] // 1024 for a in smalls)
-    rows = -(-rows // 16) * 16
     outs = []
     for _, _, _, count, by_rows in groups:
         shape = (count, 2, 2, 2, 2, 16, 1024) if by_rows else (2, 2, 2, 2, 16, count * 1024)
         outs.append(jax.ShapeDtypeStruct(shape, BF))
+    return lefts, rights, groups, units, outs
+
+
+def reduce_kernel(groups, units, n_left, n_right, n_small, *refs):
+    lefts, rights = (refs[:n_left], refs[n_left : n_left + n_right])
+    refs = refs[n_left + n_right :]
+    smalls, outs, small_out = (refs[:n_small], refs[n_small:-18], refs[-18])
+    hop_out, hop_in, hop_total, hsem, isem = refs[-17:-12]
+    z, _, _, _, _, _, peers = here()
+    del peers["zz"]
+    begin, step, finish = reducer(groups, units, lefts, rights, outs, refs[-12:], REDUCE_LAG)
+    begin()
+    meet(peers)
+    hops = ("c", "x", "y", "z0", "z1")
+
+    def hop(k):
+        return pltpu.make_async_remote_copy(
+            src_ref=hop_out.at[k],
+            dst_ref=hop_in.at[k],
+            send_sem=hsem.at[k],
+            recv_sem=isem.at[k],
+            device_id=peers[hops[k]],
+            device_id_type=MESH,
+        )
+
+    def stage_hop(k):
+        hop(k).wait_recv()
+        total = hop_out[k].astype(F32) + hop_in[k].astype(F32)
+        if k + 1 < len(hops):
+            hop_out[k + 1] = total.astype(BF)
+            hop(k + 1).start()
+        else:
+            width = small_out.shape[1]
+            hop_total[...] = total
+            small_out[...] = hop_total[:, pl.ds(pl.multiple_of(z * width, width), width)]
+
+    def body(i, carry):
+        step(i)
+
+        @pl.when(i == 0)
+        def _():
+            fill_sums(hop_total, smalls)
+            hop_out[0] = hop_total[...].astype(BF)
+            hop(0).start()
+
+        for k in range(len(hops)):
+
+            @pl.when(i == 2 * k + 2)
+            def _():
+                stage_hop(k)
+
+        return carry
+
+    lax.fori_loop(0, units + REDUCE_LAG[-1], body, 0)
+    finish()
+    for k in range(len(hops)):
+        hop(k).wait_send()
+
+
+def reduce_fast(pairs, smalls, before=()):
+    lefts, rights, groups, units, outs = reducer_plan(pairs)
+    dma = pltpu.SemaphoreType.DMA
+    rows = sum(a.shape[0] if a.ndim > 1 else a.shape[0] // 1024 for a in smalls)
+    rows = -(-rows // 16) * 16
     found = pl.pallas_call(
         functools.partial(reduce_kernel, groups, units, len(lefts), len(rights), len(smalls)),
         out_shape=outs + [jax.ShapeDtypeStruct((rows, 256), F32)],
         in_specs=[ANY] * (len(lefts) + len(rights)) + [VM] * len(smalls),
         out_specs=[ANY] * len(outs) + [VM],
         scratch_shapes=[
-            pltpu.VMEM((3, 4, 256, 256), BF),
-            pltpu.VMEM((3, 256, 1024), BF),
-            pltpu.VMEM((2, 2, 2, 2, 2, 2, 16, 1024), BF),
-            pltpu.VMEM((units, 2, 2, 2, 2, 2, 16, 1024), BF),
-            pltpu.VMEM((units, 2, 2, 2, 2, 16, 1024), BF),
-            pltpu.VMEM((units, 2, 2, 2, 16, 1024), BF),
-            pltpu.VMEM((units, 2, 2, 16, 1024), BF),
-            pltpu.VMEM((units, 2, 16, 1024), BF),
             pltpu.VMEM((5, rows, 1024), BF),
             pltpu.VMEM((5, rows, 1024), BF),
             pltpu.VMEM((rows, 1024), F32),
-            dma((3, 5)),
-            dma((units, 12)),
-            dma((units, 12)),
-            dma((units, 2)),
             dma((5,)),
             dma((5,)),
-        ],
+        ]
+        + reducer_buffers(units),
         compiler_params=pltpu.CompilerParams(
             collective_id=1, has_side_effects=True, vmem_limit_bytes=60 << 20
         ),
         name="reduce_grads",
     )(*lefts, *rights, *smalls)
-    return [w.reshape(-1, w.shape[-1]).astype(F32) for w in found[:-1]], found[-1]
+    found, summed = (list(before) + list(found[:-1]), found[-1])
+    return widened([w.reshape(-1, w.shape[-1]) for w in found]), summed
+
+
+def widen_kernel(*refs):
+    count = len(refs) // 2
+    for i in range(count):
+        refs[count + i][...] = refs[i][...].astype(F32)
+
+
+def widened(arrays):
+    specs = [pl.BlockSpec((a.shape[0] // 16, a.shape[1]), lambda i: (i, 0)) for a in arrays]
+    return pl.pallas_call(
+        widen_kernel,
+        out_shape=[jax.ShapeDtypeStruct(a.shape, F32) for a in arrays],
+        grid=(16,),
+        in_specs=specs,
+        out_specs=specs,
+        compiler_params=pltpu.CompilerParams(vmem_limit_bytes=60 << 20),
+        name="widen_sums",
+    )(*arrays)
 
 
 def reduce_plain(pairs, small):
@@ -584,13 +632,15 @@
     return grads, lax.dynamic_slice_in_dim(summed, lax.axis_index("shard") * width, width, 1)
 
 
-def greet(n):
+def greet(n, more=()):
     rep = lax.axis_index("rep")
     others = [jnp.bitwise_xor(rep, d) for d in range(1, n)]
     barrier = pltpu.get_barrier_semaphore()
     for other in others:
         pl.semaphore_signal(barrier, inc=1, device_id={"rep": other}, device_id_type=MESH)
-    pl.semaphore_wait(barrier, n - 1)
+    for other in more:
+        pl.semaphore_signal(barrier, inc=1, device_id=other, device_id_type=MESH)
+    pl.semaphore_wait(barrier, n - 1 + len(more))
     return rep, others
 
 
@@ -618,6 +668,9 @@
 
 
 def from_heads(swapped):
+    if swapped.ndim == 4:
+        k, batch, local, features = swapped.shape
+        return [swapped[i].reshape(batch * local, features) for i in range(k)]
     n, k, batch, local, width = swapped.shape
     return [
         jnp.transpose(swapped[:, i], (1, 2, 0, 3)).reshape(batch * local, n * width)
@@ -636,6 +689,12 @@
     bias[...] = jnp.where(lane < (block + 1) * 128, spread[:, 0:1], spread[:, 383:384])
     rolled = pltpu.roll(spread, 0, 1, stride=1, stride_axis=0)
     bias[:, pl.ds(pl.multiple_of(block * 128, 128), 384)] = rolled[:, 0:384]
+
+
+def features_of(out_ref, rep, width):
+    if width % 128:
+        return None
+    return pl.ds(pl.multiple_of(rep * width, width), width)
 
 
 def forward_kernel(
@@ -691,18 +750,24 @@
             return carry
 
         lax.fori_loop(0, n, one_block, 0)
+        place = features_of(out_ref, rep, width)
+        target = out_ref.at[rep, 0, b] if place is None else out_ref.at[0, b, :, place]
         leaving.append(
-            send_all(
-                others, lambda other: low.at[b, other], out_ref.at[rep, b], tsem.at[b], usem.at[b]
-            )
+            send_all(others, lambda other: low.at[b, other], target, tsem.at[b], usem.at[b])
         )
-        out_ref[rep, b] = low[b, rep]
+        target[...] = low[b, rep]
     for copies in arriving:
         for copy in copies:
             copy.wait_send()
     for copies in leaving:
         for copy in copies:
             copy.wait()
+
+
+def sent_shape(count, n, batch, local, width):
+    if width % 128:
+        return (n, count, batch, local, width)
+    return (count, batch, local, n * width)
 
 
 def attention_forward(stacked, table):
@@ -715,7 +780,7 @@
             jax.ShapeDtypeStruct((batch, 3, n, local, width), BF),
             shape,
             shape,
-            jax.ShapeDtypeStruct((n, batch, local, width), BF),
+            jax.ShapeDtypeStruct(sent_shape(1, n, batch, local, width), BF),
         ],
         in_specs=[VM, VM],
         out_specs=[VM] * 4,
@@ -731,30 +796,29 @@
     )(stacked, table)
 
 
-def backward_kernel(
-    x_ref,
-    heads_ref,
-    table_ref,
-    mixed_ref,
-    lse_ref,
-    out_ref,
-    dtable_ref,
-    grads,
-    low,
-    bias,
-    keyx,
-    dscore,
-    prob,
-    dkt,
-    dvt,
-    ssem,
-    rsem,
-    tsem,
-    usem,
-):
+def backward_kernel(plan, *refs):
+    x_ref, heads_ref, table_ref, mixed_ref, lse_ref = refs[:5]
+    refs = refs[5:]
     batch, _, n, local, width = heads_ref.shape
     total = n * local
-    rep, others = greet(n)
+    if plan is None:
+        out_ref, dtable_ref = refs[:2]
+        refs = refs[2:]
+        rep, others = greet(n)
+    else:
+        n_left, n_right, groups, units = plan
+        lefts, rights = (refs[:n_left], refs[n_left : n_left + n_right])
+        refs = refs[n_left + n_right :]
+        out_ref, dtable_ref = refs[:2]
+        outs = refs[2 : 2 + len(groups)]
+        refs = refs[2 + len(groups) :]
+        begin, step, finish = reducer(
+            groups, units, lefts, rights, outs, refs[12:], BESIDE_LAG
+        )
+        begin()
+        peers = here()[-1]
+        rep, others = greet(n, (peers["z0"], peers["z1"]))
+    grads, low, bias, keyx, dscore, prob, dkt, dvt, ssem, rsem, tsem, usem = refs[:12]
     arriving, leaving = ([], [])
     for b in range(batch):
         arriving.append(
@@ -842,42 +906,54 @@
                 )
                 found = query_back if found is None else jnp.where(mask, query_back, found)
             low[b, 0, block] = (found * 0.125).astype(BF)
+            if plan is not None:
+                step(b * n + block)
             return carry
 
         lax.fori_loop(0, n, one_block, 0)
         low[b, 1] = jnp.transpose(dkt[...]).astype(BF).reshape(n, local, width)
         low[b, 2] = jnp.transpose(dvt[...]).astype(BF).reshape(n, local, width)
+        place = features_of(out_ref, rep, width)
+        target = out_ref.at[rep, :, b] if place is None else out_ref.at[:, b, :, place]
         leaving.append(
-            send_all(
-                others,
-                lambda other: low.at[b, :, other],
-                out_ref.at[rep, :, b],
-                tsem.at[b],
-                usem.at[b],
-            )
+            send_all(others, lambda other: low.at[b, :, other], target, tsem.at[b], usem.at[b])
         )
         for part in range(3):
-            out_ref[rep, part, b] = low[b, part, rep]
+            target[part] = low[b, part, rep]
     for copies in arriving:
         for copy in copies:
             copy.wait_send()
     for copies in leaving:
         for copy in copies:
             copy.wait()
-
-
-def attention_backward(stacked, heads, table, mixed, logsum):
+    if plan is not None:
+
+        def rest(i, carry):
+            step(i)
+            return carry
+
+        lax.fori_loop(batch * n, max(batch * n, units + BESIDE_LAG[-1]), rest, 0)
+        finish()
+
+
+def attention_backward(stacked, heads, table, mixed, logsum, pairs):
     batch, _, n, local, width = heads.shape
     total = n * local
     dma = pltpu.SemaphoreType.DMA
-    return pl.pallas_call(
-        backward_kernel,
+    plan, lefts, rights, outs, buffers = (None, [], [], [], [])
+    if pairs:
+        lefts, rights, groups, units, outs = reducer_plan(pairs)
+        plan = (len(lefts), len(rights), groups, units)
+        buffers = reducer_buffers(units)
+    found = pl.pallas_call(
+        functools.partial(backward_kernel, plan),
         out_shape=[
-            jax.ShapeDtypeStruct((n, 3, batch, local, width), BF),
+            jax.ShapeDtypeStruct(sent_shape(3, n, batch, local, width), BF),
             jax.ShapeDtypeStruct(table.shape, F32),
-        ],
-        in_specs=[VM] * 5,
-        out_specs=[VM] * 2,
+        ]
+        + outs,
+        in_specs=[VM] * 5 + [ANY] * (len(lefts) + len(rights)),
+        out_specs=[VM] * 2 + [ANY] * len(outs),
         scratch_shapes=[
             pltpu.VMEM((batch, n, local, width), BF),
             pltpu.VMEM((batch, 3, n, local, width), BF),
@@ -888,12 +964,14 @@
             pltpu.VMEM((width, total), F32),
             pltpu.VMEM((width, total), F32),
         ]
-        + [dma((batch, n - 1))] * 4,
+        + [dma((batch, n - 1))] * 4
+        + buffers,
         compiler_params=pltpu.CompilerParams(
             collective_id=3, has_side_effects=True, vmem_limit_bytes=48 << 20
         ),
         name="attention_backward",
-    )(stacked, heads, table, mixed, logsum)
+    )(stacked, heads, table, mixed, logsum, *lefts, *rights)
+    return found[0], found[1], list(found[2:])
 
 
 def shifted(value, axis, steps):
@@ -1312,7 +1390,7 @@
     heads, mixed_h, logsum, mixed = attention_forward(
         to_heads([query, keys, values], n_rep), spread_table
     )
-    mixed = from_heads(mixed[:, None])[0]
+    mixed = from_heads(mixed)[0]
     level2 = level1 + times(mixed, w[13]) + w[14]
 
     conv_in = norm(level2, w[16], w[17]).astype(BF)
@@ -1350,8 +1428,21 @@
     mixer_out = back2.astype(BF)
     grads[14] = column_sum(mixer_out)
     mixed_back = times_back(mixer_out, w[13]).astype(BF).reshape(batch, local, features)
-    found, table_b = attention_backward(
-        to_heads([mixed_back], n_rep), heads, spread_table, mixed_h, logsum
+    ahead = 2 if fast else 0
+    pairs = [
+        (27, later_pairs[0]),
+        (25, later_pairs[1]),
+        (22, (acted, conv_out)),
+        (18, (conv_in, doubled_back)),
+        (13, (mixed, mixer_out)),
+    ]
+    found, table_b, before = attention_backward(
+        to_heads([mixed_back], n_rep),
+        heads,
+        spread_table,
+        mixed_h,
+        logsum,
+        [pair for _, pair in pairs[:ahead]],
     )
     query_back, key_back, value_back = from_heads(found)
     folded = table_b.reshape(BAND, -1, HD).sum(axis=1)
@@ -1372,20 +1463,18 @@
     back0, found, early_pairs = feed_backward(level0, w[0], w[2], w[4], early, back1)
     grads[0], grads[1], grads[3], grads[5] = found
 
-    pairs = (
-        (27, later_pairs[0]),
-        (25, later_pairs[1]),
-        (22, (acted, conv_out)),
-        (18, (conv_in, doubled_back)),
-        (13, (mixed, mixer_out)),
+    pairs += [
         (8, (attend_in, query_back)),
         (10, (attend_in, key_back)),
         (11, (attend_in, value_back)),
         (4, early_pairs[0]),
         (2, early_pairs[1]),
-    )
-    reduce = reduce_fast if fast else reduce_plain
-    matrices, smalls = reduce([pair for _, pair in pairs], list_sums(grads, n_shard))
+    ]
+    kept, sums = ([pair for _, pair in pairs[ahead:]], list_sums(grads, n_shard))
+    if fast:
+        matrices, smalls = reduce_fast(kept, sums, before)
+    else:
+        matrices, smalls = reduce_plain(kept, sums)
     summed = dict(zip([i for i, _ in pairs], matrices))
     summed.update(split_sums(smalls, shards))
     return (whole_of(output), whole_of(back0)) + tuple(summed[i] for i in range(31))

time: 672 us -> 658 us (0.979)
  other arithmetic: 34.9 us -> 16.8 us
  Pallas kernels: 537 us -> 547 us
  local copies, waits for them, and re-layouts: 21.6 us -> 13.2 us
    pallas_call x1 -> x2, Pallas kernels: 60.5 us -> 140 us  [the longest x1 124 us: attention_backward(): pl.pallas_call(functools.partial(backward_kernel, plan), out_shape=[jax.S...]
    pallas_call x1, Pallas kernels: 238 us -> 167 us  [reduce_fast(): pl.pallas_call(functools.partial(reduce_kernel, groups, units, len(lefts)...]
    convert_element_type x10 -> x0, other arithmetic: 20.8 us -> none  [reduce_fast(): w.reshape(-1, w.shape[-1]).astype(F32)]
where the time goes in v4:
time: 658 us; the launch traced here: 650 us
  Pallas kernels  547 us (83%)
  matrix products  66 us (10%)
  other arithmetic  16.8 us (3%)
  local copies, waits for them, and re-layouts  13.2 us (2%)
    pallas_call x1, Pallas kernels, gather_fast(): pl.pallas_call(functools.partial(gather_kernel, chunks, count, len(smalls...  178 us
    pallas_call x1, Pallas kernels, reduce_fast(): pl.pallas_call(functools.partial(reduce_kernel, groups, units, len(lefts)...  167 us
    pallas_call x1, Pallas kernels, attention_backward(): pl.pallas_call(functools.partial(backward_kernel, plan), out_shape=[jax.S...  124 us
    dot_general x10, matrix products, times_back(): lax.dot_general(left, right, (((1,), (1,)), ((), ())), preferred_element_...  38.6 us
    pallas_call x1, Pallas kernels, attention_forward(): pl.pallas_call(forward_kernel, out_shape=[jax.ShapeDtypeStruct((batch, 3,...  38.3 us
    dot_general x10, matrix products, times(): return jnp.dot(left, right, preferred_element_type=F32)  27.3 us
    pallas_call x1, Pallas kernels, widened(): pl.pallas_call(widen_kernel, out_shape=[jax.ShapeDtypeStruct(a.shape, F32...  16.7 us
  transfers between devices with their start and end apart: 2, of which 1 were waited for; matrix products, arithmetic and copies ran while one was open for 0% of the time, Pallas kernels for 0%

profile of v4, /device:TPU:0, one launch (start us, length us, event | category | flops | bytes accessed | tf_op | source)
XLA Modules:
  0.0 649.8 jit_solution(12508241739845571213)
XLA Ops:
  0.7 1.4 copy.90.refs_30_
  2.1 177.9 %gather_weights.1 = (bf16[2,2,2,2,2,2,16,4096]{7,6,5,4,3,2,1,0:T(8,128)(2,1)}, bf16[2,2,2,2,2,2,64,1024]{7,6,5,4,3,2,1,0:T(8,128)(2,1)}, bf16[2,2,2,2,2,2,16,102...) custom-call(bf16[2,2,2,2,16,4096]{5,4,3,2,1,0:T(8,128)(2,1)} %bitcas, ...), custom_call_target="tpu_custom_call" | custom-call | tf_op jit(solution)/shard_map/gather_weights/pallas_call | solution.py:201
  180.1 0.8 convert_bitcast_fusion.1
  180.9 1.2 slice_convert_fusion.2
  182.1 0.9 slice_bitcast_fusion
  183.2 0.3 multiply_reduce_fusion.12
  183.7 1.9 gather_fusion
  186.0 0.3 add_convert_fusion.5
  186.3 8.2 %multiply_convert_fusion.1 = (bf16[256,4096]{1,0:T(8,128)(2,1)S(1)}, f32[256,4096]{1,0:T(8,128)}) fusion(f32[4096]{0:T(1024)S(1)} %bitcast.299, bf16[256,1024]{1,0:T(8,128)(2,1)S(1)} %bitcast.265, bf16[1024,4096]{1,0:T(8,128)(2,1)} %bitcast.305), kind=kOutput, calls=%fused_computation.11 | convolution fusion | flops 2153775104 | bytes 15220736 | tf_op jit(solution)/shard_map/dot_general | solution.py:1017
  194.5 2.5 fusion.31
  197.0 0.2 multiply_reduce_fusion.11
  197.3 0.3 add_convert_fusion.4.refs_3_
  197.6 0.7 fusion.9
  198.4 0.7 copy-done.18
  199.2 0.7 fusion.10
  200.1 0.7 fusion.11
  201.0 0.2 copy_bitcast_fusion.1
  201.4 38.3 %attention_forward.1 = (bf16[2,3,8,128,128]{4,3,2,1,0:T(8,128)(2,1)S(1)}, f32[2,8,128,128]{3,2,1,0:T(8,128)S(1)}, f32[2,8,128,128]{3,2,1,0:T(8,128)S(1)}, bf16[1,2,128,1024]{3,2,1,0:T(8,128)(2,1)S(1)}) custom-call(bf16[8,3,2,128,128]{4,3,2,1,0:T(8,128)(2,1)S(1)} %pad_maximum_fusion.x_ref, bf16[512,128]{1,0:T(8,128)(2,1)S(1)} %copy.97.table_ref.refs_2_), custom_call_target="tpu_custom_call" | custom-call | tf_op jit(solution)/shard_map/attention_forward/pallas_call | solution.py:777
  239.7 0.8 fusion.32
  240.6 0.3 multiply_reduce_fusion.10
  240.8 0.3 add_convert_fusion.3.refs_1_
  241.1 1.3 fusion.35.doubled_ref
  242.5 2.0 collective-permute-start
  244.5 0.9 convert_bitcast_fusion
  245.7 0.7 convert_reduce_fusion.2
  246.4 7.7 %conv_forward.1 = (f32[2,128,1024]{2,1,0:T(8,128)S(1)}, bf16[2,128,1024]{2,1,0:T(8,128)(2,1)S(1)}) custom-call(f32[2,128,2048]{2,1,0:T(8,128)S(1)} %fusion.35.doubled_ref, bf16[2,30,1024]{2,1,0:T(8,128)(2,1)S(1)} %collective-permute-done.rim_ref, f32[31,1024]{1,0:T(8,128)S(1)} %bitcast.211, f32[1,1024]{1,0:T(1,128)S(1)} %convert.27.gain_ref, ...), custom_call_target="tpu_custom_call" | custom-call | tf_op jit(solution)/shard_map/conv_forward/pallas_call | solution.py:1204
  254.1 0.8 fusion.33
  254.9 0.3 multiply_reduce_fusion.9
  255.2 0.3 add_convert_fusion.2.refs_6_
  255.5 4.9 multiply_convert_fusion
  260.4 6.7 %fusion.34 = (f32[256]{0:T(256)S(1)}, f32[256,1024]{1,0:T(8,128)S(1)}) fusion(f32[256,1024]{1,0:T(8,128)S(1)} %get-tuple-element.329, f32[1024]{0:T(1024)S(1)} %bitcast.301, bf16[256,4096]{1,0:T(8,128)(2,1)S(1)} %get-tuple-element.330.refs_5_, bf16[4096,1024]{1,0:T(8,128)(2,1)} %bitcast.317), kind=kOutput, calls=%fused_computation.156 | convolution fusion | flops 2148531968 | bytes 12588032 | tf_op jit(solution)/shard_map/dot_general | solution.py:1017
  267.1 0.2 multiply_reduce_fusion.8
  267.3 1.0 fusion.19
  268.4 1.0 convert_reduce_fusion.3
  269.4 12.0 %convert_reduce_fusion = (f32[4096]{0:T(1024)}, bf16[256,4096]{1,0:T(8,128)(2,1)}) fusion(f32[256,4096]{1,0:T(8,128)} %get-tuple-element.331, bf16[256,1024]{1,0:T(8,128)(2,1)S(1)} %get-tuple-element.283.refs_7_, bf16[4096,1024]{1,0:T(8,128)(2,1)} %bitcast.318), kind=kOutput, calls=%fused_computation.7 | convolution fusion | flops 2159013888 | bytes 15220736 | tf_op jit(solution)/shard_map/dot_general | solution.py:1021
  281.4 7.3 %multiply_reduce_fusion = (f32[1024]{0:T(1024)}, f32[256]{0:T(256)S(1)}, f32[256]{0:T(256)S(1)}, f32[1024]{0:T(1024)}, f32[256,1024]{1,0:T(8,128)S(1)}) fusion(f32[256,1024]{1,0:T(8,128)S(1)} %get-tuple-element.329, f32[256]{0:T(256)S(1)} %add_rsqrt_fusion.1, f32[256]{0:T(256)S(1)} %broadcast_multiply_fusion.10, f32[1024]{0:T(1024)S(1)} %bitcast.282, ...), kind=kOutput, calls=%fused_computation.49 | convolution fusion | flops 2149840384 | bytes 12599296 | tf_op jit(solution)/shard_map/dot_general | solution.py:1021
  288.8 1.6 fusion.28
  290.4 0.7 fusion.36.grad_ref
  291.1 3.0 depth_backward.1
  294.1 1.3 collective-permute-start.1
  295.4 0.6 fusion.30
  296.0 2.2 collective-permute-done.1.after_ref
  298.2 10.6 %conv_backward.1 = (bf16[2,128,2048]{2,1,0:T(8,128)(2,1)S(1)}, f32[32,1024]{1,0:T(8,128)S(1)}) custom-call(f32[2,128,1024]{2,1,0:T(8,128)S(1)} %get-tuple-element.111.back_ref, bf16[2,30,1024]{2,1,0:T(8,128)(2,1)S(1)} %collective-permute-done.1.after_ref, f32[2,128,2048]{2,1,0:T(8,128)S(1)} %fusion.35.doubled_ref, ...), custom_call_target="tpu_custom_call" | custom-call | tf_op jit(solution)/shard_map/conv_backward/pallas_call | solution.py:1325
  308.9 2.1 multiply_reduce_fusion.1
  311.0 2.0 convert_reduce_fusion.4
  313.0 0.7 fusion.12
  313.9 123.7 %attention_backward.1 = (bf16[3,2,128,1024]{3,2,1,0:T(8,128)(2,1)S(1)}, f32[512,128]{1,0:T(8,128)S(1)}, bf16[4,2,2,2,2,16,1024]{6,5,4,3,2,1,0:T(8,128)(2,1)}, bf16[2,2,2,2,16,4096]{5,4,3,2,1,0:T(8,128)(2,1)}) custom-call(bf16[8,1,2,128,128]{4,3,2,1,0:T(8,128)(2,1)S(1)} %bitcast.208, bf16[2,3,8,128,128]{4,3,2,1,0:T(8,128)(2,1)} %copy-done.2, ...), custom_call_target="tpu_custom_call" | custom-call | tf_op jit(solution)/shard_map/attention_backward/pallas_call | solution.py:948
  438.3 0.8 convert_reduce_fusion.5
  439.4 0.7 fusion.37
  440.1 0.7 convolution_add_fusion.3
  440.9 0.3 copy-done.6
  441.2 0.7 copy-done.26
  441.9 2.6 multiply_reduce_fusion.2
  445.1 0.6 reshape.598
  445.7 2.7 convert_reduce_fusion.7
  448.5 7.6 %convert_reduce_fusion.1 = (f32[4096]{0:T(1024)}, bf16[256,4096]{1,0:T(8,128)(2,1)S(1)}) fusion(f32[256,4096]{1,0:T(8,128)S(1)} %copy-done.30, bf16[256,1024]{1,0:T(8,128)(2,1)S(1)} %get-tuple-element.288.refs_12_, bf16[4096,1024]{1,0:T(8,128)(2,1)} %bitcast.309), kind=kOutput, calls=%fused_computation.8 | convolution fusion | flops 2159013888 | bytes 15220736 | tf_op jit(solution)/shard_map/dot_general | solution.py:1021
  456.1 4.0 multiply_reduce_fusion.3
  460.2 167.1 %reduce_grads.1 = (bf16[2,2,2,2,16,1024]{5,4,3,2,1,0:T(8,128)(2,1)}, bf16[2,2,2,2,16,2048]{5,4,3,2,1,0:T(8,128)(2,1)}, bf16[2,2,2,2,16,1024]{5,4,3,2,1,0:T(8,128...) custom-call(bf16[256,1024]{1,0:T(8,128)(2,1)} %bitcast.207, ...), custom_call_target="tpu_custom_call" | custom-call | tf_op jit(solution)/shard_map/reduce_grads/pallas_call | solution.py:582
  627.3 0.7 slice.149
  628.0 1.5 split_sums.1
  629.6 0.4 multiply_add_fusion
  630.0 2.0 copy.106
  632.1 0.7 copy.107
  632.8 16.7 %widen_sums.1 = (f32[1024,1024]{1,0:T(8,128)}, f32[256,4096]{1,0:T(8,128)}, f32[256,1024]{1,0:T(8,128)}, f32[256,2048]{1,0:T(8,128)}, f32[256,1024]{1,0:T(8,128)...) custom-call(bf16[1024,1024]{1,0:T(8,128)(2,1)} %bitcast.247, ...), custom_call_target="tpu_custom_call" | custom-call | tf_op jit(solution)/shard_map/widen_sums/pallas_call | solution.py:612
  (137 shorter events, 3.7 us)
Async XLA Ops:
  2.1 180.9 %copy-start.8 = (bf16[2,128,1,1024]{3,1,2,0:T(8,128)(2,1)S(1)}, bf16[2,128,1,1024]{3,1,2,0:T(8,128)(2,1)}, u32[]{:S(2)}) copy-start(bf16[2,128,1,1024]{3,1,2,0:T(8,128)(2,1)} %param.33) | copy-start | bytes 1572868
  186.0 8.5 %slice-start.2 = ((s8[8388608]{0:T(1024)(128)(4,1)}), s8[4194304]{0:T(1024)(128)(4,1)S(1)}, s32[]{:S(2)}) async-start(s8[8388608]{0:T(1024)(128)(4,1)} %bitcast.310), calls=%async_computation.2 | async-start | bytes 8388608
  186.3 8.2 %slice-start.3 = ((s8[8388608]{0:T(1024)(128)(4,1)}), s8[4194304]{0:T(1024)(128)(4,1)S(1)}, s32[]{:S(2)}) async-start(s8[8388608]{0:T(1024)(128)(4,1)} %bitcast.310), calls=%async_computation.3 | async-start | bytes 8388608
  194.5 2.5 copy-start.16
  194.5 3.1 copy-start.25
  197.0 42.7 %copy-start.5 = (f32[256,1024]{1,0:T(8,128)}, f32[256,1024]{1,0:T(8,128)S(1)}, u32[]{:S(2)}) copy-start(f32[256,1024]{1,0:T(8,128)S(1)} %get-tuple-element.325) | copy-start | bytes 3145732
  197.0 2.2 copy-start.18
  197.6 2.5 copy-start.20
  198.3 1.8 copy-start.21
  200.9 38.9 %copy-start.23 = (bf16[2,2,2,2,2,2,16,1024]{7,6,5,4,3,2,1,0:T(8,128)(2,1)S(1)}, bf16[2,2,2,2,2,2,16,1024]{7,6,5,4,3,2,1,0:T(8,128)(2,1)}, u32[]{:S(2)}) copy-start(bf16[2,2,2,2,2,2,16,1024]{7,6,5,4,3,2,1,0:T(8,128)(2,1)} %get-tuple-element.104) | copy-start | bytes 6291460
  201.4 39.7 %copy-start.15 = (bf16[2,2,2,2,2,2,16,2048]{7,6,5,4,3,2,1,0:T(8,128)(2,1)S(1)}, bf16[2,2,2,2,2,2,16,2048]{7,6,5,4,3,2,1,0:T(8,128)(2,1)}, u32[]{:S(2)}) copy-start(bf16[2,2,2,2,2,2,16,2048]{7,6,5,4,3,2,1,0:T(8,128)(2,1)} %get-tuple-element.105) | copy-start | bytes 12582916
  239.7 2.7 copy-start.1
  239.7 2.7 copy-start.2
  241.1 4.6 copy-start.13
  241.1 4.5 copy-start.9
  241.1 13.0 %copy-start.7 = (bf16[2,2,2,2,2,2,16,1024]{7,6,5,4,3,2,1,0:T(8,128)(2,1)S(1)}, bf16[2,2,2,2,2,2,16,1024]{7,6,5,4,3,2,1,0:T(8,128)(2,1)}, u32[]{:S(2)}) copy-start(bf16[2,2,2,2,2,2,16,1024]{7,6,5,4,3,2,1,0:T(8,128)(2,1)} %get-tuple-element.107) | copy-start | bytes 6291460
  241.1 14.3 %slice-start.4 = ((s8[8388608]{0:T(1024)(128)(4,1)}), s8[4194304]{0:T(1024)(128)(4,1)S(1)}, s32[]{:S(2)}) async-start(s8[8388608]{0:T(1024)(128)(4,1)} %bitcast.314), calls=%async_computation.4 | async-start | bytes 8388608
  242.5 3.9 collective-permute-start
  246.4 9.1 %slice-start.5 = ((s8[8388608]{0:T(1024)(128)(4,1)}), s8[4194304]{0:T(1024)(128)(4,1)S(1)}, s32[]{:S(2)}) async-start(s8[8388608]{0:T(1024)(128)(4,1)} %bitcast.314), calls=%async_computation.5 | async-start | bytes 8388608
  254.1 6.3 copy-start
  260.4 6.7 %copy-start.27 = (bf16[256,4096]{1,0:T(8,128)(2,1)}, bf16[256,4096]{1,0:T(8,128)(2,1)S(1)}, u32[]{:S(2)}) copy-start(bf16[256,4096]{1,0:T(8,128)(2,1)S(1)} %get-tuple-element.330.refs_5_) | copy-start | bytes 6291460
  290.4 18.4 %copy-start.10 = (bf16[256,1024]{1,0:T(8,128)(2,1)}, bf16[256,1024]{1,0:T(8,128)(2,1)S(1)}, u32[]{:S(2)}) copy-start(bf16[256,1024]{1,0:T(8,128)(2,1)S(1)} %get-tuple-element.290.refs_6_) | copy-start | bytes 1572868
  294.1 4.1 collective-permute-start.1
  308.8 2.1 copy-start.3
  308.8 2.1 copy-start.4
  311.0 2.0 copy-start.24
  313.0 124.6 %copy-start.28 = (bf16[256,1024]{1,0:T(8,128)(2,1)}, bf16[256,1024]{1,0:T(8,128)(2,1)S(1)}, u32[]{:S(2)}) copy-start(bf16[256,1024]{1,0:T(8,128)(2,1)S(1)} %get-tuple-element.285.refs_8_) | copy-start | bytes 1572868
  437.8 1.6 copy-start.19
  437.8 2.3 copy-start.22
  439.2 1.7 copy-start.11
  439.2 1.7 copy-start.12
  439.3 1.7 copy-start.14
  439.4 1.8 copy-start.6
  439.4 2.5 copy-start.26
  445.7 2.8 copy-start.30
  445.7 10.4 %slice-start = ((s8[8388608]{0:T(1024)(128)(4,1)}), s8[4194304]{0:T(1024)(128)(4,1)S(1)}, s32[]{:S(2)}) async-start(s8[8388608]{0:T(1024)(128)(4,1)} %bitcast.306), calls=%async_computation | async-start | bytes 8388608
  448.4 7.7 %copy-start.29 = (bf16[256,1024]{1,0:T(8,128)(2,1)}, bf16[256,1024]{1,0:T(8,128)(2,1)S(1)}, u32[]{:S(2)}) copy-start(bf16[256,1024]{1,0:T(8,128)(2,1)S(1)} %get-tuple-element.288.refs_12_) | copy-start | bytes 1572868
  448.5 7.6 %slice-start.1 = ((s8[8388608]{0:T(1024)(128)(4,1)}), s8[4194304]{0:T(1024)(128)(4,1)S(1)}, s32[]{:S(2)}) async-start(s8[8388608]{0:T(1024)(128)(4,1)} %bitcast.306), calls=%async_computation.1 | async-start | bytes 8388608
  456.1 4.0 copy-start.17

commit v5 on v4

--- a/solution.py
+++ b/solution.py
@@ -608,11 +608,11 @@
 
 
 def widened(arrays):
-    specs = [pl.BlockSpec((a.shape[0] // 16, a.shape[1]), lambda i: (i, 0)) for a in arrays]
+    specs = [pl.BlockSpec((a.shape[0] // 8, a.shape[1]), lambda i: (i, 0)) for a in arrays]
     return pl.pallas_call(
         widen_kernel,
         out_shape=[jax.ShapeDtypeStruct(a.shape, F32) for a in arrays],
-        grid=(16,),
+        grid=(8,),
         in_specs=specs,
         out_specs=specs,
         compiler_params=pltpu.CompilerParams(vmem_limit_bytes=60 << 20),

time: 658 us -> 654 us (level)
  no operation moved by 1% of the time
where the time goes in v5:
time: 654 us; the launch traced here: 647 us
  Pallas kernels  543 us (83%)
  matrix products  66 us (10%)
  other arithmetic  16.8 us (3%)
  local copies, waits for them, and re-layouts  13.2 us (2%)
    pallas_call x1, Pallas kernels, gather_fast(): pl.pallas_call(functools.partial(gather_kernel, chunks, count, len(smalls...  178 us
    pallas_call x1, Pallas kernels, reduce_fast(): pl.pallas_call(functools.partial(reduce_kernel, groups, units, len(lefts)...  167 us
    pallas_call x1, Pallas kernels, attention_backward(): pl.pallas_call(functools.partial(backward_kernel, plan), out_shape=[jax.S...  124 us
    dot_general x10, matrix products, times_back(): lax.dot_general(left, right, (((1,), (1,)), ((), ())), preferred_element_...  38.6 us
    pallas_call x1, Pallas kernels, attention_forward(): pl.pallas_call(forward_kernel, out_shape=[jax.ShapeDtypeStruct((batch, 3,...  38.3 us
    dot_general x10, matrix products, times(): return jnp.dot(left, right, preferred_element_type=F32)  27.3 us
    pallas_call x1, Pallas kernels, widened(): pl.pallas_call(widen_kernel, out_shape=[jax.ShapeDtypeStruct(a.shape, F32...  13.6 us
  transfers between devices with their start and end apart: 2, of which 1 were waited for; matrix products, arithmetic and copies ran while one was open for 0% of the time, Pallas kernels for 0%

profile of v5, /device:TPU:0, one launch (start us, length us, event | category | flops | bytes accessed | tf_op | source)
XLA Modules:
  0.0 646.6 jit_solution(12835656618050664012)
XLA Ops:
  0.7 1.4 copy.90.refs_30_
  2.1 177.9 %gather_weights.1 = (bf16[2,2,2,2,2,2,16,4096]{7,6,5,4,3,2,1,0:T(8,128)(2,1)}, bf16[2,2,2,2,2,2,64,1024]{7,6,5,4,3,2,1,0:T(8,128)(2,1)}, bf16[2,2,2,2,2,2,16,102...) custom-call(bf16[2,2,2,2,16,4096]{5,4,3,2,1,0:T(8,128)(2,1)} %bitcas, ...), custom_call_target="tpu_custom_call" | custom-call | tf_op jit(solution)/shard_map/gather_weights/pallas_call | solution.py:201
  180.1 0.8 convert_bitcast_fusion.1
  180.9 1.2 slice_convert_fusion.2
  182.1 0.9 slice_bitcast_fusion
  183.2 0.3 multiply_reduce_fusion.12
  183.7 1.9 gather_fusion
  186.0 0.3 add_convert_fusion.5
  186.3 8.2 %multiply_convert_fusion.1 = (bf16[256,4096]{1,0:T(8,128)(2,1)S(1)}, f32[256,4096]{1,0:T(8,128)}) fusion(f32[4096]{0:T(1024)S(1)} %bitcast.299, bf16[256,1024]{1,0:T(8,128)(2,1)S(1)} %bitcast.265, bf16[1024,4096]{1,0:T(8,128)(2,1)} %bitcast.305), kind=kOutput, calls=%fused_computation.11 | convolution fusion | flops 2153775104 | bytes 15220736 | tf_op jit(solution)/shard_map/dot_general | solution.py:1017
  194.5 2.5 fusion.31
  197.0 0.2 multiply_reduce_fusion.11
  197.3 0.3 add_convert_fusion.4.refs_3_
  197.6 0.7 fusion.9
  198.4 0.7 copy-done.18
  199.2 0.7 fusion.10
  200.1 0.7 fusion.11
  201.0 0.2 copy_bitcast_fusion.1
  201.4 38.3 %attention_forward.1 = (bf16[2,3,8,128,128]{4,3,2,1,0:T(8,128)(2,1)S(1)}, f32[2,8,128,128]{3,2,1,0:T(8,128)S(1)}, f32[2,8,128,128]{3,2,1,0:T(8,128)S(1)}, bf16[1,2,128,1024]{3,2,1,0:T(8,128)(2,1)S(1)}) custom-call(bf16[8,3,2,128,128]{4,3,2,1,0:T(8,128)(2,1)S(1)} %pad_maximum_fusion.x_ref, bf16[512,128]{1,0:T(8,128)(2,1)S(1)} %copy.97.table_ref.refs_2_), custom_call_target="tpu_custom_call" | custom-call | tf_op jit(solution)/shard_map/attention_forward/pallas_call | solution.py:777
  239.7 0.8 fusion.32
  240.6 0.3 multiply_reduce_fusion.10
  240.8 0.3 add_convert_fusion.3.refs_1_
  241.1 1.3 fusion.35.doubled_ref
  242.5 2.0 collective-permute-start
  244.5 0.9 convert_bitcast_fusion
  245.7 0.7 convert_reduce_fusion.2
  246.4 7.7 %conv_forward.1 = (f32[2,128,1024]{2,1,0:T(8,128)S(1)}, bf16[2,128,1024]{2,1,0:T(8,128)(2,1)S(1)}) custom-call(f32[2,128,2048]{2,1,0:T(8,128)S(1)} %fusion.35.doubled_ref, bf16[2,30,1024]{2,1,0:T(8,128)(2,1)S(1)} %collective-permute-done.rim_ref, f32[31,1024]{1,0:T(8,128)S(1)} %bitcast.211, f32[1,1024]{1,0:T(1,128)S(1)} %convert.27.gain_ref, ...), custom_call_target="tpu_custom_call" | custom-call | tf_op jit(solution)/shard_map/conv_forward/pallas_call | solution.py:1204
  254.1 0.8 fusion.33
  254.9 0.3 multiply_reduce_fusion.9
  255.2 0.3 add_convert_fusion.2.refs_6_
  255.5 4.9 multiply_convert_fusion
  260.4 6.7 %fusion.34 = (f32[256]{0:T(256)S(1)}, f32[256,1024]{1,0:T(8,128)S(1)}) fusion(f32[256,1024]{1,0:T(8,128)S(1)} %get-tuple-element.329, f32[1024]{0:T(1024)S(1)} %bitcast.301, bf16[256,4096]{1,0:T(8,128)(2,1)S(1)} %get-tuple-element.330.refs_5_, bf16[4096,1024]{1,0:T(8,128)(2,1)} %bitcast.317), kind=kOutput, calls=%fused_computation.156 | convolution fusion | flops 2148531968 | bytes 12588032 | tf_op jit(solution)/shard_map/dot_general | solution.py:1017
  267.1 0.2 multiply_reduce_fusion.8
  267.3 1.0 fusion.19
  268.4 1.0 convert_reduce_fusion.3
  269.4 12.0 %convert_reduce_fusion = (f32[4096]{0:T(1024)}, bf16[256,4096]{1,0:T(8,128)(2,1)}) fusion(f32[256,4096]{1,0:T(8,128)} %get-tuple-element.331, bf16[256,1024]{1,0:T(8,128)(2,1)S(1)} %get-tuple-element.283.refs_7_, bf16[4096,1024]{1,0:T(8,128)(2,1)} %bitcast.318), kind=kOutput, calls=%fused_computation.7 | convolution fusion | flops 2159013888 | bytes 15220736 | tf_op jit(solution)/shard_map/dot_general | solution.py:1021
  281.4 7.3 %multiply_reduce_fusion = (f32[1024]{0:T(1024)}, f32[256]{0:T(256)S(1)}, f32[256]{0:T(256)S(1)}, f32[1024]{0:T(1024)}, f32[256,1024]{1,0:T(8,128)S(1)}) fusion(f32[256,1024]{1,0:T(8,128)S(1)} %get-tuple-element.329, f32[256]{0:T(256)S(1)} %add_rsqrt_fusion.1, f32[256]{0:T(256)S(1)} %broadcast_multiply_fusion.10, f32[1024]{0:T(1024)S(1)} %bitcast.282, ...), kind=kOutput, calls=%fused_computation.49 | convolution fusion | flops 2149840384 | bytes 12599296 | tf_op jit(solution)/shard_map/dot_general | solution.py:1021
  288.8 1.6 fusion.28
  290.4 0.7 fusion.36.grad_ref
  291.1 3.0 depth_backward.1
  294.1 1.3 collective-permute-start.1
  295.4 0.6 fusion.30
  296.0 2.2 collective-permute-done.1.after_ref
  298.2 10.6 %conv_backward.1 = (bf16[2,128,2048]{2,1,0:T(8,128)(2,1)S(1)}, f32[32,1024]{1,0:T(8,128)S(1)}) custom-call(f32[2,128,1024]{2,1,0:T(8,128)S(1)} %get-tuple-element.111.back_ref, bf16[2,30,1024]{2,1,0:T(8,128)(2,1)S(1)} %collective-permute-done.1.after_ref, f32[2,128,2048]{2,1,0:T(8,128)S(1)} %fusion.35.doubled_ref, ...), custom_call_target="tpu_custom_call" | custom-call | tf_op jit(solution)/shard_map/conv_backward/pallas_call | solution.py:1325
  308.9 2.1 multiply_reduce_fusion.1
  311.0 2.0 convert_reduce_fusion.4
  313.0 0.7 fusion.12
  313.9 123.7 %attention_backward.1 = (bf16[3,2,128,1024]{3,2,1,0:T(8,128)(2,1)S(1)}, f32[512,128]{1,0:T(8,128)S(1)}, bf16[4,2,2,2,2,16,1024]{6,5,4,3,2,1,0:T(8,128)(2,1)}, bf16[2,2,2,2,16,4096]{5,4,3,2,1,0:T(8,128)(2,1)}) custom-call(bf16[8,1,2,128,128]{4,3,2,1,0:T(8,128)(2,1)S(1)} %bitcast.208, bf16[2,3,8,128,128]{4,3,2,1,0:T(8,128)(2,1)} %copy-done.2, ...), custom_call_target="tpu_custom_call" | custom-call | tf_op jit(solution)/shard_map/attention_backward/pallas_call | solution.py:948
  438.3 0.8 convert_reduce_fusion.5
  439.4 0.7 fusion.37
  440.1 0.7 convolution_add_fusion.3
  440.9 0.3 copy-done.6
  441.2 0.7 copy-done.26
  441.9 2.6 multiply_reduce_fusion.2
  445.1 0.6 reshape.598
  445.7 2.7 convert_reduce_fusion.7
  448.5 7.6 %convert_reduce_fusion.1 = (f32[4096]{0:T(1024)}, bf16[256,4096]{1,0:T(8,128)(2,1)S(1)}) fusion(f32[256,4096]{1,0:T(8,128)S(1)} %copy-done.30, bf16[256,1024]{1,0:T(8,128)(2,1)S(1)} %get-tuple-element.288.refs_12_, bf16[4096,1024]{1,0:T(8,128)(2,1)} %bitcast.309), kind=kOutput, calls=%fused_computation.8 | convolution fusion | flops 2159013888 | bytes 15220736 | tf_op jit(solution)/shard_map/dot_general | solution.py:1021
  456.1 4.0 multiply_reduce_fusion.3
  460.2 167.1 %reduce_grads.1 = (bf16[2,2,2,2,16,1024]{5,4,3,2,1,0:T(8,128)(2,1)}, bf16[2,2,2,2,16,2048]{5,4,3,2,1,0:T(8,128)(2,1)}, bf16[2,2,2,2,16,1024]{5,4,3,2,1,0:T(8,128...) custom-call(bf16[256,1024]{1,0:T(8,128)(2,1)} %bitcast.207, ...), custom_call_target="tpu_custom_call" | custom-call | tf_op jit(solution)/shard_map/reduce_grads/pallas_call | solution.py:582
  627.3 0.7 slice.149
  628.0 1.5 split_sums.1
  629.6 0.4 multiply_add_fusion
  630.0 2.0 copy.106
  632.1 0.7 copy.107
  632.8 13.6 %widen_sums.1 = (f32[1024,1024]{1,0:T(8,128)}, f32[256,4096]{1,0:T(8,128)}, f32[256,1024]{1,0:T(8,128)}, f32[256,2048]{1,0:T(8,128)}, f32[256,1024]{1,0:T(8,128)...) custom-call(bf16[1024,1024]{1,0:T(8,128)(2,1)} %bitcast.247, ...), custom_call_target="tpu_custom_call" | custom-call | tf_op jit(solution)/shard_map/widen_sums/pallas_call | solution.py:612
  (137 shorter events, 3.7 us)
Async XLA Ops:
  2.1 180.9 %copy-start.8 = (bf16[2,128,1,1024]{3,1,2,0:T(8,128)(2,1)S(1)}, bf16[2,128,1,1024]{3,1,2,0:T(8,128)(2,1)}, u32[]{:S(2)}) copy-start(bf16[2,128,1,1024]{3,1,2,0:T(8,128)(2,1)} %param.33) | copy-start | bytes 1572868
  186.0 8.5 %slice-start.2 = ((s8[8388608]{0:T(1024)(128)(4,1)}), s8[4194304]{0:T(1024)(128)(4,1)S(1)}, s32[]{:S(2)}) async-start(s8[8388608]{0:T(1024)(128)(4,1)} %bitcast.310), calls=%async_computation.2 | async-start | bytes 8388608
  186.3 8.2 %slice-start.3 = ((s8[8388608]{0:T(1024)(128)(4,1)}), s8[4194304]{0:T(1024)(128)(4,1)S(1)}, s32[]{:S(2)}) async-start(s8[8388608]{0:T(1024)(128)(4,1)} %bitcast.310), calls=%async_computation.3 | async-start | bytes 8388608
  194.5 2.5 copy-start.16
  194.5 3.1 copy-start.25
  197.0 42.7 %copy-start.5 = (f32[256,1024]{1,0:T(8,128)}, f32[256,1024]{1,0:T(8,128)S(1)}, u32[]{:S(2)}) copy-start(f32[256,1024]{1,0:T(8,128)S(1)} %get-tuple-element.325) | copy-start | bytes 3145732
  197.0 2.2 copy-start.18
  197.6 2.5 copy-start.20
  198.3 1.8 copy-start.21
  200.9 38.9 %copy-start.23 = (bf16[2,2,2,2,2,2,16,1024]{7,6,5,4,3,2,1,0:T(8,128)(2,1)S(1)}, bf16[2,2,2,2,2,2,16,1024]{7,6,5,4,3,2,1,0:T(8,128)(2,1)}, u32[]{:S(2)}) copy-start(bf16[2,2,2,2,2,2,16,1024]{7,6,5,4,3,2,1,0:T(8,128)(2,1)} %get-tuple-element.104) | copy-start | bytes 6291460
  201.4 39.7 %copy-start.15 = (bf16[2,2,2,2,2,2,16,2048]{7,6,5,4,3,2,1,0:T(8,128)(2,1)S(1)}, bf16[2,2,2,2,2,2,16,2048]{7,6,5,4,3,2,1,0:T(8,128)(2,1)}, u32[]{:S(2)}) copy-start(bf16[2,2,2,2,2,2,16,2048]{7,6,5,4,3,2,1,0:T(8,128)(2,1)} %get-tuple-element.105) | copy-start | bytes 12582916
  239.7 2.7 copy-start.1
  239.7 2.7 copy-start.2
  241.1 4.6 copy-start.13
  241.1 4.5 copy-start.9
  241.1 13.0 %copy-start.7 = (bf16[2,2,2,2,2,2,16,1024]{7,6,5,4,3,2,1,0:T(8,128)(2,1)S(1)}, bf16[2,2,2,2,2,2,16,1024]{7,6,5,4,3,2,1,0:T(8,128)(2,1)}, u32[]{:S(2)}) copy-start(bf16[2,2,2,2,2,2,16,1024]{7,6,5,4,3,2,1,0:T(8,128)(2,1)} %get-tuple-element.107) | copy-start | bytes 6291460
  241.1 14.3 %slice-start.4 = ((s8[8388608]{0:T(1024)(128)(4,1)}), s8[4194304]{0:T(1024)(128)(4,1)S(1)}, s32[]{:S(2)}) async-start(s8[8388608]{0:T(1024)(128)(4,1)} %bitcast.314), calls=%async_computation.4 | async-start | bytes 8388608
  242.5 3.9 collective-permute-start
  246.4 9.1 %slice-start.5 = ((s8[8388608]{0:T(1024)(128)(4,1)}), s8[4194304]{0:T(1024)(128)(4,1)S(1)}, s32[]{:S(2)}) async-start(s8[8388608]{0:T(1024)(128)(4,1)} %bitcast.314), calls=%async_computation.5 | async-start | bytes 8388608
  254.1 6.3 copy-start
  260.4 6.7 %copy-start.27 = (bf16[256,4096]{1,0:T(8,128)(2,1)}, bf16[256,4096]{1,0:T(8,128)(2,1)S(1)}, u32[]{:S(2)}) copy-start(bf16[256,4096]{1,0:T(8,128)(2,1)S(1)} %get-tuple-element.330.refs_5_) | copy-start | bytes 6291460
  290.4 18.4 %copy-start.10 = (bf16[256,1024]{1,0:T(8,128)(2,1)}, bf16[256,1024]{1,0:T(8,128)(2,1)S(1)}, u32[]{:S(2)}) copy-start(bf16[256,1024]{1,0:T(8,128)(2,1)S(1)} %get-tuple-element.290.refs_6_) | copy-start | bytes 1572868
  294.1 4.1 collective-permute-start.1
  308.8 2.1 copy-start.3
  308.8 2.1 copy-start.4
  311.0 2.0 copy-start.24
  313.0 124.6 %copy-start.28 = (bf16[256,1024]{1,0:T(8,128)(2,1)}, bf16[256,1024]{1,0:T(8,128)(2,1)S(1)}, u32[]{:S(2)}) copy-start(bf16[256,1024]{1,0:T(8,128)(2,1)S(1)} %get-tuple-element.285.refs_8_) | copy-start | bytes 1572868
  437.8 1.6 copy-start.19
  437.8 2.3 copy-start.22
  439.2 1.7 copy-start.11
  439.2 1.7 copy-start.12
  439.3 1.7 copy-start.14
  439.4 1.8 copy-start.6
  439.4 2.5 copy-start.26
  445.7 2.8 copy-start.30
  445.7 10.4 %slice-start = ((s8[8388608]{0:T(1024)(128)(4,1)}), s8[4194304]{0:T(1024)(128)(4,1)S(1)}, s32[]{:S(2)}) async-start(s8[8388608]{0:T(1024)(128)(4,1)} %bitcast.306), calls=%async_computation | async-start | bytes 8388608
  448.4 7.7 %copy-start.29 = (bf16[256,1024]{1,0:T(8,128)(2,1)}, bf16[256,1024]{1,0:T(8,128)(2,1)S(1)}, u32[]{:S(2)}) copy-start(bf16[256,1024]{1,0:T(8,128)(2,1)S(1)} %get-tuple-element.288.refs_12_) | copy-start | bytes 1572868
  448.5 7.6 %slice-start.1 = ((s8[8388608]{0:T(1024)(128)(4,1)}), s8[4194304]{0:T(1024)(128)(4,1)S(1)}, s32[]{:S(2)}) async-start(s8[8388608]{0:T(1024)(128)(4,1)} %bitcast.306), calls=%async_computation.1 | async-start | bytes 8388608
  456.1 4.0 copy-start.17
